TPU v7x, 32 devices: a whole 2x2x4 slice. The times are simulated.
32 devices in a mesh: rep: 2 (over x), shard: 16 (over z, y, core).
Axes of the slice: x: 2, y: 2, z: 4, core: 2. Of those that a mesh axis runs over, the one named last changes fastest.
Arguments:
- inputs: bfloat16 [32, 1024, 768], P(('rep', 'shard')), may hold values from -6 to 6
- doc_ids: int32 [32, 1024], P(('rep', 'shard')), may hold values from 0 to 3, never falling along the last dimension, each value on 1 to 512 neighbouring positions
- attn_gain: bfloat16 [768], P('shard'), may hold values from 0.25 to 1.75
- w_query: bfloat16 [768, 768], P('shard'), may hold values from -0.21875 to 0.21875
- w_key: bfloat16 [768, 768], P('shard'), may hold values from -0.21875 to 0.21875
- w_value: bfloat16 [768, 768], P('shard'), may hold values from -0.21875 to 0.21875
- w_out: bfloat16 [768, 768], P('shard'), may hold values from -1.75 to 1.75
- ffn_gain: bfloat16 [768], P('shard'), may hold values from 0.25 to 1.75
- w_gate: bfloat16 [768, 2048], P('shard'), may hold values from -0.21875 to 0.21875
- w_up: bfloat16 [768, 2048], P('shard'), may hold values from -0.21875 to 0.21875
- w_down: bfloat16 [2048, 768], P('shard'), may hold values from -0.125 to 0.125
- cotangent: bfloat16 [32, 1024, 768], P(('rep', 'shard')), may hold values from -6 to 6
Outputs:
- output: bfloat16 [32, 1024, 768], P(('rep', 'shard'))
- grad_input: float32 [32, 1024, 768], P(('rep', 'shard'))
- grad_attn_gain: float32 [768], P('shard')
- grad_w_query: float32 [768, 768], P('shard')
- grad_w_key: float32 [768, 768], P('shard')
- grad_w_value: float32 [768, 768], P('shard')
- grad_w_out: float32 [768, 768], P('shard')
- grad_ffn_gain: float32 [768], P('shard')
- grad_w_gate: float32 [768, 2048], P('shard')
- grad_w_up: float32 [768, 2048], P('shard')
- grad_w_down: float32 [2048, 768], P('shard')
Inputs may be any that keep to these rules, and one draw needn't show every extreme that they name: `doc_ids`: within a sequence document numbers never fall; every document has 1 to 512 tokens, and one has exactly 512.
All inputs are finite; a program needn't handle non-finite values.
Results may differ from a plain program's by a relative error of at most 0.017.
Values may be sent and summed in bfloat16 or wider, within the bound.
No kernel may reach another device: no remote copies, remote signals or barrier semaphores. Data moves between devices by JAX's collectives and lax.ppermute only.
A program may use at most 320 MiB of HBM per device.

v0:
```python
import jax
import jax.numpy as jnp
from jax import lax
from jax.sharding import PartitionSpec as P

H = 12
HD = 64
BLOCK = 256


epsilon = 1e-06
rope_base = 10000.0
masked_score = -1e30


def rope_tables(length, head_size):
    position = jnp.arange(length, dtype=jnp.float32)
    exponent = jnp.arange(head_size // 2, dtype=jnp.float32) * (2.0 / head_size)
    angles = position[:, None] * jnp.power(rope_base, -exponent)[None, :]
    return (jnp.cos(angles)[:, None, :], jnp.sin(angles)[:, None, :])


def rotate(tensor, cosine_table, sine_table):
    midway = tensor.shape[-1] // 2
    front_half = tensor[..., :midway]
    back_half = tensor[..., midway:]
    return jnp.concatenate(
        [
            front_half * cosine_table - back_half * sine_table,
            back_half * cosine_table + front_half * sine_table,
        ],
        axis=-1,
    )


def rotate_back(tensor, cosine_table, sine_table):
    midway = tensor.shape[-1] // 2
    front_half = tensor[..., :midway]
    back_half = tensor[..., midway:]
    return jnp.concatenate(
        [
            front_half * cosine_table + back_half * sine_table,
            back_half * cosine_table - front_half * sine_table,
        ],
        axis=-1,
    )


def allowed_pairs(doc_ids, offset, row_step, block_size):
    length = doc_ids.shape[1]
    row_docs = lax.dynamic_slice_in_dim(doc_ids, offset, row_step, 1)
    row_block = (offset + jnp.arange(row_step, dtype=jnp.int32)) // block_size
    col_block = jnp.arange(length, dtype=jnp.int32) // block_size
    same_doc = row_docs[:, :, None] == doc_ids[:, None, :]
    ordered = col_block[None, None, :] <= row_block[None, :, None]
    return (same_doc & ordered)[:, None, :, :]


def rows_product(left, right):
    return lax.dot_general(
        left, right, (((0,), (0,)), ((), ())), preferred_element_type=jnp.float32
    )


def right_transposed(left, right):
    return lax.dot_general(
        left, right, (((1,), (1,)), ((), ())), preferred_element_type=jnp.float32
    )


def norm_back(grad_normed, normed, inverse):
    return inverse * (grad_normed - normed * jnp.mean(grad_normed * normed, -1, keepdims=True))


def block_scores(query_block, keys_rot, doc_ids, offset, row_step, factor):
    allowed = allowed_pairs(doc_ids, offset, row_step, BLOCK)
    scores = (
        jnp.einsum("bqhd,bkhd->bhqk", query_block, keys_rot, preferred_element_type=jnp.float32)
        * factor
    )
    return jnp.where(allowed, scores, masked_score)


def per_device(
    inputs,
    doc_ids,
    attn_gain,
    w_query,
    w_key,
    w_value,
    w_out,
    ffn_gain,
    w_gate,
    w_up,
    w_down,
    cotangent,
):
    batch_size, length, model_width = inputs.shape
    rows_total = batch_size * length
    head_count = H
    head_size = HD
    row_step = min(512, length)
    factor = head_size ** (-0.5)
    gain_one, query_mat, key_mat, value_mat, out_mat, gain_two, gate_mat, up_mat, down_mat = (
        lax.all_gather(attn_gain, "shard", axis=0, tiled=True),
        lax.all_gather(w_query, "shard", axis=0, tiled=True),
        lax.all_gather(w_key, "shard", axis=0, tiled=True),
        lax.all_gather(w_value, "shard", axis=0, tiled=True),
        lax.all_gather(w_out, "shard", axis=0, tiled=True),
        lax.all_gather(ffn_gain, "shard", axis=0, tiled=True),
        lax.all_gather(w_gate, "shard", axis=0, tiled=True),
        lax.all_gather(w_up, "shard", axis=0, tiled=True),
        lax.all_gather(w_down, "shard", axis=0, tiled=True),
    )
    resid = inputs.astype(jnp.float32).reshape(rows_total, model_width)
    inv_one = lax.rsqrt(jnp.mean(resid * resid, -1, keepdims=True) + epsilon)
    normed_one = resid * inv_one
    gain_first = gain_one.astype(jnp.float32)
    attn_in = (normed_one * gain_first).astype(jnp.bfloat16)
    cosine_table, sine_table = rope_tables(length, head_size)

    def project(matrix):
        return jnp.dot(attn_in, matrix, preferred_element_type=jnp.float32).reshape(
            batch_size, length, head_count, head_size
        )

    queries = rotate(project(query_mat), cosine_table, sine_table).astype(jnp.bfloat16)
    keys_rot = rotate(project(key_mat), cosine_table, sine_table).astype(jnp.bfloat16)
    value_vec = project(value_mat).astype(jnp.bfloat16)
    mixed_blocks = []
    log_sums = []
    for offset in range(0, length, row_step):
        query_block = queries[:, offset : offset + row_step]
        scores = block_scores(query_block, keys_rot, doc_ids, offset, row_step, factor)
        row_peak = jnp.max(scores, -1, keepdims=True)
        exp_scores = jnp.exp(scores - row_peak)
        row_total = jnp.sum(exp_scores, -1, keepdims=True)
        attn_probs = (exp_scores / row_total).astype(jnp.bfloat16)
        log_sums.append(row_peak + jnp.log(row_total))
        mixed_blocks.append(
            jnp.einsum("bhqk,bkhd->bqhd", attn_probs, value_vec, preferred_element_type=jnp.float32)
        )
    mixed_heads = (
        jnp.concatenate(mixed_blocks, 1).reshape(rows_total, model_width).astype(jnp.bfloat16)
    )
    middle = resid + jnp.dot(mixed_heads, out_mat, preferred_element_type=jnp.float32)
    inv_two = lax.rsqrt(jnp.mean(middle * middle, -1, keepdims=True) + epsilon)
    normed_two = middle * inv_two
    gain_second = gain_two.astype(jnp.float32)
    ffn_in = (normed_two * gain_second).astype(jnp.bfloat16)
    gate_pre = jnp.dot(ffn_in, gate_mat, preferred_element_type=jnp.float32)
    up_pre = jnp.dot(ffn_in, up_mat, preferred_element_type=jnp.float32)
    gate_sigmoid = jax.nn.sigmoid(gate_pre)
    hidden = (gate_pre * gate_sigmoid * up_pre).astype(jnp.bfloat16)
    result = middle + jnp.dot(hidden, down_mat, preferred_element_type=jnp.float32)
    output = result.astype(jnp.bfloat16).reshape(batch_size, length, model_width)
    gain_one, query_mat, key_mat, value_mat, out_mat, gain_two, gate_mat, up_mat, down_mat = (
        lax.all_gather(attn_gain, "shard", axis=0, tiled=True),
        lax.all_gather(w_query, "shard", axis=0, tiled=True),
        lax.all_gather(w_key, "shard", axis=0, tiled=True),
        lax.all_gather(w_value, "shard", axis=0, tiled=True),
        lax.all_gather(w_out, "shard", axis=0, tiled=True),
        lax.all_gather(ffn_gain, "shard", axis=0, tiled=True),
        lax.all_gather(w_gate, "shard", axis=0, tiled=True),
        lax.all_gather(w_up, "shard", axis=0, tiled=True),
        lax.all_gather(w_down, "shard", axis=0, tiled=True),
    )
    branch_grad = cotangent.reshape(rows_total, model_width)
    grad_out = branch_grad.astype(jnp.float32)
    grad_w_down = rows_product(hidden, branch_grad)
    grad_hidden = right_transposed(branch_grad, down_mat)
    grad_gate = (
        grad_hidden * up_pre * gate_sigmoid * (1.0 + gate_pre * (1.0 - gate_sigmoid))
    ).astype(jnp.bfloat16)
    grad_up = (grad_hidden * gate_pre * gate_sigmoid).astype(jnp.bfloat16)
    grad_w_gate = rows_product(ffn_in, grad_gate)
    grad_w_up = rows_product(ffn_in, grad_up)
    grad_ffn_in = right_transposed(grad_gate, gate_mat) + right_transposed(grad_up, up_mat)
    grad_gain_two = jnp.sum(grad_ffn_in * normed_two, 0)
    grad_middle = grad_out + norm_back(grad_ffn_in * gain_second, normed_two, inv_two)
    attn_grad = grad_middle.astype(jnp.bfloat16)
    grad_w_out = rows_product(mixed_heads, attn_grad)
    grad_mixed = (
        right_transposed(attn_grad, out_mat)
        .astype(jnp.bfloat16)
        .reshape(batch_size, length, head_count, head_size)
    )
    grad_key = jnp.zeros((batch_size, length, head_count, head_size), jnp.float32)
    grad_value = jnp.zeros((batch_size, length, head_count, head_size), jnp.float32)
    grad_query_blocks = []
    for block_index, offset in enumerate(range(0, length, row_step)):
        query_block = queries[:, offset : offset + row_step]
        scores = block_scores(query_block, keys_rot, doc_ids, offset, row_step, factor)
        probs_full = jnp.exp(scores - log_sums[block_index])
        attn_probs = probs_full.astype(jnp.bfloat16)
        grad_block = grad_mixed[:, offset : offset + row_step]
        grad_value = grad_value + jnp.einsum(
            "bhqk,bqhd->bkhd", attn_probs, grad_block, preferred_element_type=jnp.float32
        )
        grad_probs = jnp.einsum(
            "bqhd,bkhd->bhqk", grad_block, value_vec, preferred_element_type=jnp.float32
        )
        grad_scores = (
            probs_full * (grad_probs - jnp.sum(probs_full * grad_probs, -1, keepdims=True))
        ).astype(jnp.bfloat16)
        grad_query_blocks.append(
            jnp.einsum("bhqk,bkhd->bqhd", grad_scores, keys_rot, preferred_element_type=jnp.float32)
            * factor
        )
        grad_key = (
            grad_key
            + jnp.einsum(
                "bhqk,bqhd->bkhd", grad_scores, query_block, preferred_element_type=jnp.float32
            )
            * factor
        )
    grad_query_rot = jnp.concatenate(grad_query_blocks, 1)
    grad_query = (
        rotate_back(grad_query_rot, cosine_table, sine_table)
        .astype(jnp.bfloat16)
        .reshape(rows_total, model_width)
    )
    grad_key_low = (
        rotate_back(grad_key, cosine_table, sine_table)
        .astype(jnp.bfloat16)
        .reshape(rows_total, model_width)
    )
    grad_value_low = grad_value.astype(jnp.bfloat16).reshape(rows_total, model_width)
    grad_w_query = rows_product(attn_in, grad_query)
    grad_w_key = rows_product(attn_in, grad_key_low)
    grad_w_value = rows_product(attn_in, grad_value_low)
    grad_attn_in = (
        right_transposed(grad_query, query_mat)
        + right_transposed(grad_key_low, key_mat)
        + right_transposed(grad_value_low, value_mat)
    )
    grad_gain_one = jnp.sum(grad_attn_in * normed_one, 0)
    grad_input = (grad_middle + norm_back(grad_attn_in * gain_first, normed_one, inv_one)).reshape(
        batch_size, length, model_width
    )
    replicas = lax.axis_size("rep")
    members = lax.axis_size("shard")
    parts = (
        lax.psum_scatter(grad_gain_one, "shard", scatter_dimension=0, tiled=True),
        lax.psum_scatter(grad_w_query, "shard", scatter_dimension=0, tiled=True),
        lax.psum_scatter(grad_w_key, "shard", scatter_dimension=0, tiled=True),
        lax.psum_scatter(grad_w_value, "shard", scatter_dimension=0, tiled=True),
        lax.psum_scatter(grad_w_out, "shard", scatter_dimension=0, tiled=True),
        lax.psum_scatter(grad_gain_two, "shard", scatter_dimension=0, tiled=True),
        lax.psum_scatter(grad_w_gate, "shard", scatter_dimension=0, tiled=True),
        lax.psum_scatter(grad_w_up, "shard", scatter_dimension=0, tiled=True),
        lax.psum_scatter(grad_w_down, "shard", scatter_dimension=0, tiled=True),
    )
    summed = (
        lax.psum(parts[0].astype(jnp.bfloat16), "rep").astype(jnp.float32),
        lax.psum(parts[1].astype(jnp.bfloat16), "rep").astype(jnp.float32),
        lax.psum(parts[2].astype(jnp.bfloat16), "rep").astype(jnp.float32),
        lax.psum(parts[3].astype(jnp.bfloat16), "rep").astype(jnp.float32),
        lax.psum(parts[4].astype(jnp.bfloat16), "rep").astype(jnp.float32),
        lax.psum(parts[5].astype(jnp.bfloat16), "rep").astype(jnp.float32),
        lax.psum(parts[6].astype(jnp.bfloat16), "rep").astype(jnp.float32),
        lax.psum(parts[7].astype(jnp.bfloat16), "rep").astype(jnp.float32),
        lax.psum(parts[8].astype(jnp.bfloat16), "rep").astype(jnp.float32),
    )
    inverse_count = 1.0 / (batch_size * replicas * members)
    return (
        output,
        grad_input,
        summed[0] * inverse_count,
        summed[1] * inverse_count,
        summed[2] * inverse_count,
        summed[3] * inverse_count,
        summed[4] * inverse_count,
        summed[5] * inverse_count,
        summed[6] * inverse_count,
        summed[7] * inverse_count,
        summed[8] * inverse_count,
    )


def solution(mesh):
    return jax.shard_map(
        per_device,
        mesh=mesh,
        in_specs=(
            P(("rep", "shard"), None, None),
            P(("rep", "shard"), None),
            P("shard"),
            P("shard", None),
            P("shard", None),
            P("shard", None),
            P("shard", None),
            P("shard"),
            P("shard", None),
            P("shard", None),
            P("shard", None),
            P(("rep", "shard"), None, None),
        ),
        out_specs=(
            P(("rep", "shard"), None, None),
            P(("rep", "shard"), None, None),
            P("shard"),
            P("shard", None),
            P("shard", None),
            P("shard", None),
            P("shard", None),
            P("shard"),
            P("shard", None),
            P("shard", None),
            P("shard", None),
        ),
        check_vma=False,
    )
```

profile of v0, /device:TPU:0, one launch (start us, length us, event | category | flops | bytes accessed | tf_op | source)
XLA Modules:
  0.0 944.5 jit_solution(17049137769246098057)
XLA Ops:
  15.7 35.2 %all-reduce.5 = (bf16[768]{0:T(1024)(128)(2,1)S(1)}, bf16[768]{0:T(1024)(128)(2,1)S(1)}) all-reduce(bf16[768]{0:T(1024)(128)(2,1)S(1)} %dynamic-update-slice, bf16[768]{0:T(1024)(128)(2,1)S(1)} %dynamic-update-slice.1), channel_id=1, replica_groups=mesh['rep'=2,'shard'=16] {'shard'}, use_global_device_ids=true, to_apply=%add | all-reduce | flops 1536 | bytes 6144
  60.4 30.6 %all-gather.12.cloned.1.call-done = bf16[768,768]{1,0:T(8,128)(2,1)} async-done(((bf16[48,768]{1,0:T(8,128)(2,1)}), bf16[768,768]{1,0:T(8,128)(2,1)}) %all-gather.12.cloned.1.call-update) | async-done | bytes 1179664 | tf_op jit(solution)/shard_map/all_gather | solution.py:107
  93.4 37.2 %all-gather.10.cloned.1.call-done = bf16[768,768]{1,0:T(8,128)(2,1)} async-done(((bf16[48,768]{1,0:T(8,128)(2,1)}), bf16[768,768]{1,0:T(8,128)(2,1)}) %all-gather.10.cloned.1.call-update) | async-done | bytes 1179664 | tf_op jit(solution)/shard_map/all_gather | solution.py:106
  141.4 11.3 %fusion.13 = (f32[12,512]{1,0:T(8,128)}, f32[12,512,1024]{2,1,0:T(8,128)}) fusion(pred[512,1024]{1,0:T(8,128)(4,1)S(1)} %get-tuple-element.66, bf16[1024,12,32]{0,2,1:T(8,128)(2,1)S(1)} %get-tuple-element.58, bf16[1024,12,32]{0,2,1:T(8,128)(2,1)S(1)} %get-tuple-element.57, bf16[1,1024,12,32]{1,3,2,0:T(8,128)(2,1)S(1)} %get-tuple-element.63, ...), kind=kOutput, calls=%fused_computation.23 | convolution fusion | flops 828893184 | bytes 28860416 | tf_op jit(solution)/shard_map/bqhd,bkhd->bhqk/dot_general | solution.py:78
  152.7 14.6 %fusion.12 = (f32[12,512]{1,0:T(8,128)}, f32[12,512,1024]{2,1,0:T(8,128)}) fusion(pred[512,1024]{1,0:T(8,128)(4,1)S(1)} %get-tuple-element.65, bf16[1024,12,32]{0,2,1:T(8,128)(2,1)} %copy-done.10, bf16[1024,12,32]{0,2,1:T(8,128)(2,1)} %copy-done.8, bf16[1,1024,12,32]{1,3,2,0:T(8,128)(2,1)} %copy-done.3, bf16[1,1024,12,32]{1,3,2,0:T(8,128)(2,1)} %copy-done.1), kind=kOutput, calls=%fused_computation.22 | convolution fusion | flops 828893184 | bytes 28860416 | tf_op jit(solution)/shard_map/bqhd,bkhd->bhqk/dot_general | solution.py:78
  167.3 12.8 %fusion.1 = f32[12,512]{1,0:T(8,128)S(1)} fusion(f32[12,512]{1,0:T(8,128)} %get-tuple-element.73, f32[12,512,1024]{2,1,0:T(8,128)} %get-tuple-element.74, pred[512,1024]{1,0:T(8,128)(4,1)S(1)} %get-tuple-element.66), kind=kLoop, calls=%fused_computation.13 | loop fusion | flops 25159680 | bytes 25739264 | tf_op jit(solution)/shard_map/reduce_sum | solution.py:137
  180.3 8.7 fusion.49
  188.9 13.4 %fusion = f32[12,512]{1,0:T(8,128)S(1)} fusion(f32[12,512]{1,0:T(8,128)} %get-tuple-element.75, f32[12,512,1024]{2,1,0:T(8,128)} %get-tuple-element.76, pred[512,1024]{1,0:T(8,128)(4,1)S(1)} %get-tuple-element.65), kind=kLoop, calls=%fused_computation.12 | loop fusion | flops 25159680 | bytes 25739264 | tf_op jit(solution)/shard_map/reduce_sum | solution.py:137
  204.9 9.2 fusion.48
  222.1 9.1 fusion.97
  231.1 31.5 %all-gather.16.cloned.1.call-done = bf16[768,2048]{1,0:T(8,128)(2,1)} async-done(((bf16[48,2048]{1,0:T(8,128)(2,1)}), bf16[768,2048]{1,0:T(8,128)(2,1)}) %all-gather.16.cloned.1.call-update) | async-done | bytes 3145744 | tf_op jit(solution)/shard_map/all_gather | solution.py:111
  262.6 9.1 fusion.96
  271.7 37.2 %all-gather.20.cloned.1.call-done = bf16[2048,768]{1,0:T(8,128)(2,1)} async-done(((bf16[128,768]{1,0:T(8,128)(2,1)}), bf16[2048,768]{1,0:T(8,128)(2,1)}) %all-gather.20.cloned.1.call-update) | async-done | bytes 3145744 | tf_op jit(solution)/shard_map/all_gather | solution.py:113
  309.0 14.4 %multiply_convert_fusion.2 = (bf16[1024,2048]{1,0:T(8,128)(2,1)S(1)}, bf16[1024,2048]{1,0:T(8,128)(2,1)}, bf16[1024,2048]{1,0:T(8,128)(2,1)}) fusion(f32[1024,2048]{1,0:T(8,128)} %fusion.96, f32[1024,2048]{1,0:T(8,128)} %fusion.97, bf16[2048,768]{1,0:T(8,128)(2,1)} %all-gather.20.cloned.1.call-done, bf16[1,1024,768]{2,1,0:T(8,128)(2,1)} %param.23), kind=kOutput, calls=%fused_computation.24 | convolution fusion | flops 3254779904 | bytes 34078720 | tf_op jit(solution)/shard_map/dot_general | solution.py:66
  323.4 7.4 fusion.98
  344.5 12.4 %fusion.4 = f32[12,64,1024]{2,1,0:T(8,128)S(1)} fusion(f32[12,512]{1,0:T(8,128)S(1)} %log_add_fusion, f32[12,512,1024]{2,1,0:T(8,128)} %get-tuple-element.74, pred[512,1024]{1,0:T(8,128)(4,1)S(1)} %get-tuple-element.66, bf16[1,1024,12,64]{1,3,2,0:T(8,128)(2,1)S(1)} %bitcast.182), kind=kOutput, calls=%fused_computation.16 | convolution fusion | flops 830472192 | bytes 29655040 | tf_op jit(solution)/shard_map/bhqk,bqhd->bkhd/dot_general | solution.py:197
  357.0 11.8 %add_convert_fusion = bf16[12,64,1024]{2,1,0:T(8,128)(2,1)S(1)} fusion(f32[12,64,1024]{2,1,0:T(8,128)S(1)} %fusion.4, f32[12,512]{1,0:T(8,128)S(1)} %log_add_fusion.1, f32[12,512,1024]{2,1,0:T(8,128)} %get-tuple-element.76, pred[512,1024]{1,0:T(8,128)(4,1)S(1)} %get-tuple-element.65, bf16[1,1024,12,64]{1,3,2,0:T(8,128)(2,1)S(1)} %bitcast.183), kind=kOutput, calls=%fused_computation.50 | convolution fusion | flops 832045056 | bytes 31227904 | tf_op jit(solution)/shard_map/bhqk,bqhd->bkhd/dot_general | solution.py:197
  372.9 18.2 %multiply_reduce_fusion = (f32[12,512]{1,0:T(8,128)S(1)}, f32[12,512,1024]{2,1,0:T(8,128)}) fusion(f32[12,512]{1,0:T(8,128)S(1)} %log_add_fusion, f32[12,512,1024]{2,1,0:T(8,128)} %get-tuple-element.74, pred[512,1024]{1,0:T(8,128)(4,1)S(1)} %get-tuple-element.66, bf16[1024,12,64]{0,2,1:T(8,128)(2,1)} %convolution_convert_fusion, ...), kind=kOutput, calls=%fused_computation.1 | convolution fusion | flops 836757504 | bytes 53264384 | tf_op jit(solution)/shard_map/bqhd,bkhd->bhqk/dot_general | solution.py:200
  391.1 18.2 %multiply_reduce_fusion.1 = (f32[12,512]{1,0:T(8,128)S(1)}, f32[12,512,1024]{2,1,0:T(8,128)}) fusion(f32[12,512]{1,0:T(8,128)S(1)} %log_add_fusion.1, f32[12,512,1024]{2,1,0:T(8,128)} %get-tuple-element.76, pred[512,1024]{1,0:T(8,128)(4,1)S(1)} %get-tuple-element.65, bf16[1024,12,64]{0,2,1:T(8,128)(2,1)} %convolution_convert_fusion, ...), kind=kOutput, calls=%fused_computation.4 | convolution fusion | flops 836757504 | bytes 53264384 | tf_op jit(solution)/shard_map/bqhd,bkhd->bhqk/dot_general | solution.py:200
  409.4 43.6 %multiply_convert_fusion = (bf16[12,512,1024]{2,1,0:T(8,128)(2,1)}, bf16[12,512,1024]{2,1,0:T(8,128)(2,1)}) fusion(f32[12,512,1024]{2,1,0:T(8,128)} %get-tuple-element.83, f32[12,512]{1,0:T(8,128)S(1)} %get-tuple-element.82, f32[12,512]{1,0:T(8,128)S(1)} %log_add_fusion, f32[12,512,1024]{2,1,0:T(8,128)} %get-tuple-element.74, ...), kind=kLoop, calls=%fused_computation | loop fusion | flops 75497472 | bytes 126976000 | tf_op jit(solution)/shard_map/convert_element_type | solution.py:205
  460.1 9.7 %multiply_bitcast_fusion.2 = f32[1,512,12,64]{1,3,2,0:T(8,128)} fusion(bf16[12,512,1024]{2,1,0:T(8,128)(2,1)} %get-tuple-element.86, bf16[1024,12,32]{0,2,1:T(8,128)(2,1)S(1)} %copy-done.11, bf16[1024,12,32]{0,2,1:T(8,128)(2,1)S(1)} %copy-done.9), kind=kOutput, calls=%fused_computation.89 | convolution fusion | flops 808845312 | bytes 15728640 | tf_op jit(solution)/shard_map/bhqk,bkhd->bqhd/dot_general | solution.py:207
  469.8 9.7 %multiply_bitcast_fusion.1 = f32[1,512,12,64]{1,3,2,0:T(8,128)} fusion(bf16[12,512,1024]{2,1,0:T(8,128)(2,1)} %get-tuple-element.85, bf16[1024,12,32]{0,2,1:T(8,128)(2,1)S(1)} %copy-done.11, bf16[1024,12,32]{0,2,1:T(8,128)(2,1)S(1)} %copy-done.9), kind=kOutput, calls=%fused_computation.88 | convolution fusion | flops 808845312 | bytes 15728640 | tf_op jit(solution)/shard_map/bhqk,bkhd->bqhd/dot_general | solution.py:207
  496.6 8.9 fusion.100
  505.6 8.9 fusion.99
  514.6 8.8 fusion.32
  524.3 8.7 fusion.45
  544.3 31.8 %all-reduce.4 = (bf16[768]{0:T(1024)(128)(2,1)S(1)}, bf16[768]{0:T(1024)(128)(2,1)S(1)}) all-reduce(f32[768]{0:T(1024)S(1)} %get-tuple-element.35, f32[768]{0:T(1024)S(1)} %copy-done.42), channel_id=2, replica_groups=mesh['rep'=2,'shard'=16] {'shard'}, use_global_device_ids=true, to_apply=%region_11.12.clone | all-reduce | flops 1536 | bytes 9216
  581.0 39.4 %reduce-scatter.10.cloned.1.call-done = f32[48,768]{1,0:T(8,128)} async-done(((f32[768,768]{1,0:T(8,128)}), f32[48,768]{1,0:T(8,128)}) %reduce-scatter.10.cloned.1.call-update) | async-done | bytes 147472 | tf_op jit(solution)/shard_map/reduce_scatter | solution.py:246
  621.9 86.6 %reduce-scatter.18.cloned.1.call-done = f32[48,2048]{1,0:T(8,128)} async-done(((f32[768,2048]{1,0:T(8,128)}), f32[48,2048]{1,0:T(8,128)}) %reduce-scatter.18.cloned.1.call-update) | async-done | bytes 393232 | tf_op jit(solution)/shard_map/reduce_scatter | solution.py:251
  710.2 87.3 %reduce-scatter.16.cloned.1.call-done = f32[48,2048]{1,0:T(8,128)} async-done(((f32[768,2048]{1,0:T(8,128)}), f32[48,2048]{1,0:T(8,128)}) %reduce-scatter.16.cloned.1.call-update) | async-done | bytes 393232 | tf_op jit(solution)/shard_map/reduce_scatter | solution.py:250
  799.2 86.5 %reduce-scatter.20.cloned.1.call-done = f32[128,768]{1,0:T(8,128)} async-done(((f32[2048,768]{1,0:T(8,128)}), f32[128,768]{1,0:T(8,128)}) %reduce-scatter.20.cloned.1.call-update) | async-done | bytes 393232 | tf_op jit(solution)/shard_map/reduce_scatter | solution.py:252
  902.4 24.1 %all-reduce.10.cloned.1.call-done = (bf16[48,768]{1,0:T(8,128)(2,1)}, bf16[48,768]{1,0:T(8,128)(2,1)}, bf16[48,768]{1,0:T(8,128)(2,1)}, bf16[48,768]{1,0:T(8,128...) async-done(((bf16[48,768]{1,0:T(8,128)(2,1)}, bf16[48,768]{1,0:T(8,128)(2,1)}, bf16[48,768]{1,0:T(8,128)(2,1)}, ...) | async-done | bytes 884752 | tf_op jit(solution)/shard_map/psum | solution.py:256
  (211 shorter events, 131.7 us)
Async XLA Ops:
  7.2 50.8 %all-gather.8.cloned.1.call-start = ((), (), s32[]{:S(2)}) async-start(), calls=%async_computation.7 | async-start | bytes 1253376 | tf_op jit(solution)/shard_map/all_gather | solution.py:108
  7.9 83.1 %all-gather.12.cloned.1.call-start = ((), (), s32[]{:S(2)}) async-start(), calls=%async_computation.9 | async-start | bytes 1253376 | tf_op jit(solution)/shard_map/all_gather | solution.py:107
  8.7 122.0 %all-gather.10.cloned.1.call-start = ((), (), s32[]{:S(2)}) async-start(), calls=%async_computation.8 | async-start | bytes 1253376 | tf_op jit(solution)/shard_map/all_gather | solution.py:106
  9.4 206.1 %all-gather.14.cloned.1.call-start = ((), (), s32[]{:S(2)}) async-start(), calls=%async_computation.10 | async-start | bytes 1253376 | tf_op jit(solution)/shard_map/all_gather | solution.py:109
  10.0 212.1 %all-gather.18.cloned.1.call-start = ((), (), s32[]{:S(2)}) async-start(), calls=%async_computation.12 | async-start | bytes 3342336 | tf_op jit(solution)/shard_map/all_gather | solution.py:112
  10.6 252.1 %all-gather.16.cloned.1.call-start = ((), (), s32[]{:S(2)}) async-start(), calls=%async_computation.11 | async-start | bytes 3342336 | tf_op jit(solution)/shard_map/all_gather | solution.py:111
  11.1 297.8 %all-gather.20.cloned.1.call-start = ((), (), s32[]{:S(2)}) async-start(), calls=%async_computation.13 | async-start | bytes 3342336 | tf_op jit(solution)/shard_map/all_gather | solution.py:113
  11.9 564.4 %reduce-scatter.14.cloned.1.call-start = ((), (), s32[]{:S(2)}) async-start(), calls=%async_computation.17 | async-start | bytes 2506752 | tf_op jit(solution)/shard_map/reduce_scatter | solution.py:248
  50.9 87.7 %copy-start.37 = (f32[768]{0:T(1024)}, f32[768]{0:T(1024)S(1)}, u32[]{:S(2)}) copy-start(f32[768]{0:T(1024)S(1)} %convert_element_type.200) | copy-start | bytes 9220
  52.2 88.0 %copy-start.24 = (f32[1024,32]{0,1:T(8,128)}, f32[1024,32]{0,1:T(8,128)S(1)}, u32[]{:S(2)}) copy-start(f32[1024,32]{0,1:T(8,128)S(1)} %get-tuple-element.71) | copy-start | bytes 393220
  52.2 88.0 %copy-start.26 = (f32[1024,32]{0,1:T(8,128)}, f32[1024,32]{0,1:T(8,128)S(1)}, u32[]{:S(2)}) copy-start(f32[1024,32]{0,1:T(8,128)S(1)} %get-tuple-element.72) | copy-start | bytes 393220
  54.4 84.3 %copy-start.39 = (f32[1024]{0:T(1024)}, f32[1024]{0:T(1024)S(1)}, u32[]{:S(2)}) copy-start(f32[1024]{0:T(1024)S(1)} %add_rsqrt_fusion.1) | copy-start | bytes 12292
  152.7 27.5 %slice-start = ((s8[25165824]{0:T(1024)(128)(4,1)}), s8[4194304]{0:T(1024)(128)(4,1)S(1)}, s32[]{:S(2)}) async-start(s8[25165824]{0:T(1024)(128)(4,1)} %bitcast.171), calls=%async_computation.22 | async-start | bytes 8388608
  152.7 27.5 %slice-start.1 = ((s8[25165824]{0:T(1024)(128)(4,1)}), s8[4194304]{0:T(1024)(128)(4,1)S(1)}, s32[]{:S(2)}) async-start(s8[25165824]{0:T(1024)(128)(4,1)} %bitcast.171), calls=%async_computation.23 | async-start | bytes 8388608
  152.7 27.5 %slice-start.2 = ((s8[25165824]{0:T(1024)(128)(4,1)}), s8[4194304]{0:T(1024)(128)(4,1)S(1)}, s32[]{:S(2)}) async-start(s8[25165824]{0:T(1024)(128)(4,1)} %bitcast.171), calls=%async_computation.24 | async-start | bytes 8388608
  152.7 27.5 %slice-start.3 = ((s8[25165824]{0:T(1024)(128)(4,1)}), s8[4194304]{0:T(1024)(128)(4,1)S(1)}, s32[]{:S(2)}) async-start(s8[25165824]{0:T(1024)(128)(4,1)} %bitcast.171), calls=%async_computation.25 | async-start | bytes 8388608
  167.3 12.9 %copy-start.12 = (bf16[1024,12,64]{0,2,1:T(8,128)(2,1)S(1)}, bf16[1024,12,64]{0,2,1:T(8,128)(2,1)}, u32[]{:S(2)}) copy-start(bf16[1024,12,64]{0,2,1:T(8,128)(2,1)} %convolution_convert_fusion) | copy-start | bytes 4718596
  167.3 12.9 %copy-start.32 = (f32[12,512]{1,0:T(8,128)S(1)}, f32[12,512]{1,0:T(8,128)}, u32[]{:S(2)}) copy-start(f32[12,512]{1,0:T(8,128)} %get-tuple-element.73) | copy-start | bytes 73732
  188.9 15.9 %copy-start = (f32[12,512,1024]{2,1,0:T(8,128)S(1)}, f32[12,512,1024]{2,1,0:T(8,128)}, u32[]{:S(2)}) copy-start(f32[12,512,1024]{2,1,0:T(8,128)} %get-tuple-element.76) | copy-start | bytes 75497472
  188.9 15.9 %copy-start.34 = (f32[12,512]{1,0:T(8,128)S(1)}, f32[12,512]{1,0:T(8,128)}, u32[]{:S(2)}) copy-start(f32[12,512]{1,0:T(8,128)} %get-tuple-element.75) | copy-start | bytes 73732
  308.9 14.4 %copy-start.44 = (bf16[768,2048]{1,0:T(8,128)(2,1)S(1)}, bf16[768,2048]{1,0:T(8,128)(2,1)}, u32[]{:S(2)}) copy-start(bf16[768,2048]{1,0:T(8,128)(2,1)} %all-gather.16.cloned.1.call-done) | copy-start | bytes 9437188
  340.8 237.1 %reduce-scatter.12.cloned.1.call-start = ((), (), s32[]{:S(2)}) async-start(), calls=%async_computation.16 | async-start | bytes 2506752 | tf_op jit(solution)/shard_map/reduce_scatter | solution.py:247
  356.9 13.1 %copy-start.38 = (f32[768]{0:T(1024)S(1)}, f32[768]{0:T(1024)}, u32[]{:S(2)}) copy-start(f32[768]{0:T(1024)} %copy-done.37) | copy-start | bytes 9220
  356.9 13.1 %copy-start.40 = (f32[1024]{0:T(1024)S(1)}, f32[1024]{0:T(1024)}, u32[]{:S(2)}) copy-start(f32[1024]{0:T(1024)} %copy-done.39) | copy-start | bytes 12292
  409.3 170.1 %reduce-scatter.8.cloned.1.call-start = ((), (), s32[]{:S(2)}) async-start(), calls=%async_computation.14 | async-start | bytes 2506752 | tf_op jit(solution)/shard_map/reduce_scatter | solution.py:245
  409.4 43.6 %copy-start.2 = (bf16[1,1024,12,32]{1,3,2,0:T(8,128)(2,1)S(1)}, bf16[1,1024,12,32]{1,3,2,0:T(8,128)(2,1)}, u32[]{:S(2)}) copy-start(bf16[1,1024,12,32]{1,3,2,0:T(8,128)(2,1)} %copy-done.1) | copy-start | bytes 2359300
  409.4 43.6 %copy-start.4 = (bf16[1,1024,12,32]{1,3,2,0:T(8,128)(2,1)S(1)}, bf16[1,1024,12,32]{1,3,2,0:T(8,128)(2,1)}, u32[]{:S(2)}) copy-start(bf16[1,1024,12,32]{1,3,2,0:T(8,128)(2,1)} %copy-done.3) | copy-start | bytes 2359300
  492.3 128.1 %reduce-scatter.10.cloned.1.call-start = ((), (), s32[]{:S(2)}) async-start(), calls=%async_computation.15 | async-start | bytes 2506752 | tf_op jit(solution)/shard_map/reduce_scatter | solution.py:246
  496.6 211.9 %reduce-scatter.18.cloned.1.call-start = ((), (), s32[]{:S(2)}) async-start(), calls=%async_computation.19 | async-start | bytes 6684672 | tf_op jit(solution)/shard_map/reduce_scatter | solution.py:251
  505.6 291.9 %reduce-scatter.16.cloned.1.call-start = ((), (), s32[]{:S(2)}) async-start(), calls=%async_computation.18 | async-start | bytes 6684672 | tf_op jit(solution)/shard_map/reduce_scatter | solution.py:250
  514.6 371.1 %reduce-scatter.20.cloned.1.call-start = ((), (), s32[]{:S(2)}) async-start(), calls=%async_computation.20 | async-start | bytes 6684672 | tf_op jit(solution)/shard_map/reduce_scatter | solution.py:252
  523.4 403.0 %all-reduce.10.cloned.1.call-start = ((), (), s32[]{:S(2)}) async-start(), calls=%async_computation.21 | async-start | bytes 1769472 | tf_op jit(solution)/shard_map/psum | solution.py:256
  (35 other events, 209.2 us)
Sparse Core Ops, SparseCore 0:
  10.3 41.1 all-gather.7
  53.7 37.2 all-gather.11
  93.3 37.2 all-gather.9
  132.8 37.3 all-gather.13
  172.3 44.1 all-gather.17
  218.6 43.9 all-gather.15
  264.9 43.9 all-gather.19
  340.9 61.7 reduce-scatter.13
  409.4 61.8 reduce-scatter.11
  492.4 61.8 reduce-scatter.7
  558.5 61.8 reduce-scatter.9
  624.2 84.2 reduce-scatter.17
  713.0 84.4 reduce-scatter.15
  801.3 84.3 reduce-scatter.19
  889.6 36.7 all-reduce.9
where the time goes:
time: 954 us; the launch traced here: 945 us
  waiting for transfers between devices  465 us (49%)
  matrix products  252 us (26%)
  other arithmetic  107 us (11%)
  blocking collectives  72 us (8%)
  local copies, waits for them, and re-layouts  31.4 us (3%)
  between operations  16.3 us (2%)
    reduce_scatter x1, waiting for transfers between devices, per_device(): lax.psum_scatter(grad_w_gate, 'shard', scatter_dimension=0, tiled=True)  87.3 us
    reduce_scatter x1, waiting for transfers between devices, per_device(): lax.psum_scatter(grad_w_up, 'shard', scatter_dimension=0, tiled=True)  86.6 us
    reduce_scatter x1, waiting for transfers between devices, per_device(): lax.psum_scatter(grad_w_down, 'shard', scatter_dimension=0, tiled=True)  86.5 us
    unnamed x2, blocking collectives  67.1 us
    convert_element_type x1, other arithmetic, per_device(): grad_scores = (probs_full * (grad_probs - jnp.sum(probs_full * grad_probs...  43.6 us
    reduce_scatter x1, waiting for transfers between devices, per_device(): lax.psum_scatter(grad_w_key, 'shard', scatter_dimension=0, tiled=True)  39.4 us
    dot_general x7, matrix products, right_transposed(): lax.dot_general(left, right, (((1,), (1,)), ((), ())), preferred_element_...  38.3 us
    dot_general x7, matrix products, rows_product(): lax.dot_general(left, right, (((0,), (0,)), ((), ())), preferred_element_...  38.2 us
  transfers between devices with their start and end apart: 15, of which 9 were waited for; matrix products, arithmetic and copies ran while one was open for 36% of the time, Pallas kernels for 0%

commit v1 on v0

v1 whole, which is shorter than its diff:
```python
import functools

import jax
import jax.numpy as jnp
from jax import lax
from jax.experimental import pallas as pl
from jax.experimental.pallas import tpu as pltpu
from jax.sharding import PartitionSpec as P

H = 12
HD = 64
BLOCK = 256
MAX_DOC = 512

epsilon = 1e-06
rope_base = 10000.0
far = 1e30

bf16 = jnp.bfloat16
f32 = jnp.float32
MIB = 1 << 20
NN = (((1,), (0,)), ((), ()))
NT = (((1,), (1,)), ((), ()))
TN = (((0,), (0,)), ((), ()))


def dot(left, right, dims=NN):
    return lax.dot_general(left, right, dims, preferred_element_type=f32)


def params(mib):
    return pltpu.CompilerParams(vmem_limit_bytes=mib * MIB)


def cost(flops, nbytes, trans=0):
    return pl.CostEstimate(flops=int(flops), bytes_accessed=int(nbytes), transcendentals=int(trans))


ANY = pl.BlockSpec(memory_space=pl.ANY)


def load_weight(pieces, tab_ref, dest, sem):
    copies = []
    index = 0
    for piece in pieces:
        count, rows = piece.shape[0], piece.shape[1]
        for b in range(count):
            row = pl.multiple_of(tab_ref[0, index] * rows, 16)
            copies.append(
                pltpu.make_async_copy(
                    piece.at[b], dest.at[tab_ref[1, index], pl.ds(row, rows)], sem.at[index]
                )
            )
            index += 1
    for copy in copies:
        copy.start()
    return copies


def wait_all(copies):
    for copy in copies:
        copy.wait()


def rope_tables(length):
    position = jnp.arange(length, dtype=f32)
    exponent = jnp.arange(HD // 2, dtype=f32) * (2.0 / HD)
    angles = position[:, None] * jnp.power(rope_base, -exponent)[None, :]
    cosine, sine = jnp.cos(angles), jnp.sin(angles)
    return jnp.concatenate([cosine] * 4, 1), jnp.concatenate([-sine, sine, -sine, sine], 1)


def swap_halves(tensor):
    lane = lax.broadcasted_iota(jnp.int32, tensor.shape, 1)
    return jnp.where(
        (lane & (HD // 2)) == 0, pltpu.roll(tensor, 128 - HD // 2, 1), pltpu.roll(tensor, HD // 2, 1)
    )


def project_kernel(tab_ref, *refs, n_pieces, halves):
    pieces, (x_ref, cos_ref, sin_ref) = refs[:n_pieces], refs[n_pieces : n_pieces + 3]
    n_ref, q_ref, k_ref, v_ref, weight, sem = refs[n_pieces + 3 :]

    @pl.when(pl.program_id(0) == 0)
    def _():
        wait_all(load_weight(pieces, tab_ref, weight, sem))

    x = x_ref[...].astype(f32)
    normed = (x * lax.rsqrt(jnp.mean(x * x, -1, keepdims=True) + epsilon)).astype(bf16)
    n_ref[...] = normed
    width = x_ref.shape[1] // halves
    cosine, sine = cos_ref[...], sin_ref[...]
    for half in range(halves):
        result = dot(normed, weight[half])
        for part, out, scale in ((0, q_ref, HD**-0.5), (1, k_ref, 1.0)):
            for c in range(0, width, 128):
                piece = result[:, part * width + c : part * width + c + 128]
                turned = piece * cosine + swap_halves(piece) * sine
                out[:, half * width + c : half * width + c + 128] = (
                    turned.astype(bf16) * jnp.asarray(scale, bf16)
                )
        v_ref[:, half * width : (half + 1) * width] = result[:, 2 * width :].astype(bf16)


def project(tab, pieces, x, cosine, sine, halves):
    length, width = x.shape
    rows = BLOCK
    n = len(pieces)
    blocks = sum(p.shape[0] for p in pieces)
    block = pl.BlockSpec((rows, width), lambda i, t: (i, 0))
    table = pl.BlockSpec((rows, 128), lambda i, t: (i, 0))
    shape = jax.ShapeDtypeStruct((length, width), bf16)
    return pl.pallas_call(
        functools.partial(project_kernel, n_pieces=n, halves=halves),
        grid_spec=pltpu.PrefetchScalarGridSpec(
            num_scalar_prefetch=1,
            grid=(length // rows,),
            in_specs=[ANY] * n + [block, table, table],
            out_specs=[block] * 4,
            scratch_shapes=[
                pltpu.VMEM((halves, width, 3 * width // halves), bf16),
                pltpu.SemaphoreType.DMA((blocks,)),
            ],
        ),
        out_shape=[shape] * 4,
        compiler_params=params(40),
        cost_estimate=cost(6 * length * width * width, 16 * length * width),
        name="project",
    )(tab, *pieces, x, cosine, sine)


def key_range(block):
    low = max(0, (block * BLOCK - (MAX_DOC - 1)) // BLOCK) if block * BLOCK > MAX_DOC - 1 else 0
    return low * BLOCK, (block + 1) * BLOCK


def marks(docs):
    lane = jnp.arange(128, dtype=jnp.int32)[None, :] % HD
    used = lane < 4
    same = docs == lane
    return (
        jnp.where(used & ~same, -far, 0.0).astype(bf16),
        jnp.where(used & same, 1.0, 0.0).astype(bf16),
    )


def attend_kernel(q_ref, k_ref, v_ref, qm_ref, km_ref, mixed_ref, inv_ref, e_ref):
    length = q_ref.shape[0]
    lane = lax.broadcasted_iota(jnp.int32, (length, 128), 1)
    q, k, v = q_ref[...], k_ref[...], v_ref[...]
    operands = []
    for head in range(2):
        own = (lane < HD) if head == 0 else (lane >= HD)
        ones = jnp.ones((length, 128), bf16)
        operands.append(
            (
                jnp.where(own, q, qm_ref[...]),
                jnp.where(own, k, km_ref[...]),
                jnp.where(own, v, ones).T,
            )
        )
    for block in range(length // BLOCK):
        low, high = key_range(block)
        rows = slice(block * BLOCK, (block + 1) * BLOCK)
        outs, invs = [], []
        for head in range(2):
            qa, ka, vt = operands[head]
            scores = dot(ka[low:high], qa[rows], NT)
            exps = jnp.exp(scores - jnp.max(scores, 0, keepdims=True)).astype(bf16)
            e_ref[head, block, 0 : high - low, :] = exps
            out = dot(vt[:, low:high], exps)
            total = out[HD : HD + 1] if head == 0 else out[0:1]
            inverse = 1.0 / total
            outs.append(out[head * HD : (head + 1) * HD] * inverse)
            invs.append(jnp.broadcast_to(inverse, (HD, BLOCK)))
        mixed_ref[rows, :] = jnp.concatenate(outs, 0).T.astype(bf16)
        inv_ref[rows, :] = jnp.concatenate(invs, 0).T


def attend(q, k, v, q_marks, k_marks):
    length, width = q.shape
    pairs = width // 128
    blocks = length // BLOCK
    most = max(key_range(b)[1] - key_range(b)[0] for b in range(blocks))
    column = pl.BlockSpec((length, 128), lambda i: (0, i))
    fixed = pl.BlockSpec((length, 128), lambda i: (0, 0))
    return pl.pallas_call(
        attend_kernel,
        grid=(pairs,),
        in_specs=[column, column, column, fixed, fixed],
        out_specs=[
            column,
            column,
            pl.BlockSpec((2, blocks, most, BLOCK), lambda i: (i, 0, 0, 0)),
        ],
        out_shape=[
            jax.ShapeDtypeStruct((length, width), bf16),
            jax.ShapeDtypeStruct((length, width), f32),
            jax.ShapeDtypeStruct((2 * pairs, blocks, most, BLOCK), bf16),
        ],
        compiler_params=params(48),
        cost_estimate=cost(10 * length * length * width, 30 * length * width, H * length * length),
        name="attend",
    )(q, k, v, q_marks, k_marks)


def attend_back_kernel(
    q_ref, k_ref, v_ref, mixed_ref, inv_ref, e_ref, grad_ref, cos_ref, sin_ref,
    dq_ref, dk_ref, dv_ref, dk_sum, dv_sum,
):
    length = q_ref.shape[0]
    lane = lax.broadcasted_iota(jnp.int32, (length, 128), 1)
    part = lax.broadcasted_iota(jnp.int32, (BLOCK, 128), 1)
    q, k, v = q_ref[...], k_ref[...], v_ref[...]
    zero = jnp.zeros((length, 128), bf16)
    dk_sum[...] = jnp.zeros_like(dk_sum)
    dv_sum[...] = jnp.zeros_like(dv_sum)
    operands = []
    for head in range(2):
        own = (lane < HD) if head == 0 else (lane >= HD)
        spare = (lane == HD) | (lane == HD + 1) if head == 0 else lane < 2
        minus = jnp.where(spare, -1.0, 0.0).astype(bf16)
        operands.append(
            (jnp.where(own, q, zero), jnp.where(own, k, zero).T, jnp.where(own, v, minus))
        )
    for block in range(length // BLOCK):
        low, high = key_range(block)
        rows = slice(block * BLOCK, (block + 1) * BLOCK)
        scaled = grad_ref[rows, :].astype(f32) * inv_ref[rows, :]
        inner = scaled * mixed_ref[rows, :].astype(f32)
        dq = jnp.zeros((128, BLOCK), f32)
        for head in range(2):
            qo, kt, va = operands[head]
            own = (part < HD) if head == 0 else (part >= HD)
            first = HD if head == 0 else 0
            delta = jnp.sum(jnp.where(own, inner, 0.0), 1, keepdims=True)
            upper = delta.astype(bf16).astype(f32)
            masked = jnp.where(own, scaled, 0.0)
            joined = jnp.where(part == first, upper, masked)
            joined = jnp.where(part == first + 1, delta - upper, joined).astype(bf16)
            masked = masked.astype(bf16)
            exps = e_ref[head, block, 0 : high - low, :]
            slope = dot(va[low:high], joined, NT)
            ds = (exps.astype(f32) * slope).astype(bf16)
            dv_sum[low:high, :] += dot(exps, masked)
            dk_sum[low:high, :] += dot(ds, qo[rows])
            dq += dot(kt[:, low:high], ds)
        turned = dq.T * (HD**-0.5)
        dq_ref[rows, :] = (
            turned * cos_ref[rows, :] - swap_halves(turned) * sin_ref[rows, :]
        ).astype(bf16)
    dk = dk_sum[...]
    dk_ref[...] = (dk * cos_ref[...] - swap_halves(dk) * sin_ref[...]).astype(bf16)
    dv_ref[...] = dv_sum[...].astype(bf16)


def attend_back(q, k, v, mixed, inv, exps, grad, cosine, sine):
    length, width = q.shape
    pairs = width // 128
    column = pl.BlockSpec((length, 128), lambda i: (0, i))
    fixed = pl.BlockSpec((length, 128), lambda i: (0, 0))
    shape = jax.ShapeDtypeStruct((length, width), bf16)
    return pl.pallas_call(
        attend_back_kernel,
        grid=(pairs,),
        in_specs=[column] * 5
        + [pl.BlockSpec((2,) + exps.shape[1:], lambda i: (i, 0, 0, 0)), column, fixed, fixed],
        out_specs=[column] * 3,
        out_shape=[shape] * 3,
        scratch_shapes=[pltpu.VMEM((length, 128), f32)] * 2,
        compiler_params=params(48),
        cost_estimate=cost(20 * length * length * width, 36 * length * width),
        name="attend_back",
    )(q, k, v, mixed, inv, exps, grad, cosine, sine)


def ffn_kernel(tab_ref, *refs, n_pieces, halves):
    pieces, (x_ref, mixed_ref) = refs[:n_pieces], refs[n_pieces : n_pieces + 2]
    middle_ref, normed_ref, hidden_ref, slope_g_ref, slope_u_ref, weight, sem = refs[n_pieces + 2 :]

    @pl.when(pl.program_id(0) == 0)
    def _():
        wait_all(load_weight(pieces, tab_ref, weight, sem))

    width = x_ref.shape[1] // halves
    inner = hidden_ref.shape[1] // halves
    mixed = mixed_ref[...]
    middle = x_ref[...].astype(f32) + jnp.concatenate(
        [dot(mixed, weight[h, :, 0:width]) for h in range(halves)], 1
    )
    middle_ref[...] = middle
    normed = (middle * lax.rsqrt(jnp.mean(middle * middle, -1, keepdims=True) + epsilon)).astype(bf16)
    normed_ref[...] = normed
    step = min(512, inner)
    for h in range(halves):
        for c in range(0, inner, step):
            gate = dot(normed, weight[h, :, width + c : width + c + step])
            up = dot(normed, weight[h, :, width + inner + c : width + inner + c + step])
            sigmoid = jax.nn.sigmoid(gate)
            silu = gate * sigmoid
            cols = slice(h * inner + c, h * inner + c + step)
            hidden_ref[:, cols] = (silu * up).astype(bf16)
            slope_u_ref[:, cols] = silu.astype(bf16)
            slope_g_ref[:, cols] = (up * sigmoid * (1.0 + gate * (1.0 - sigmoid))).astype(bf16)


def ffn(tab, pieces, x, mixed, inner, halves):
    length, width = x.shape
    rows = BLOCK
    n = len(pieces)
    blocks = sum(p.shape[0] for p in pieces)
    narrow = pl.BlockSpec((rows, width), lambda i, t: (i, 0))
    wide = pl.BlockSpec((rows, inner), lambda i, t: (i, 0))
    wide_shape = jax.ShapeDtypeStruct((length, inner), bf16)
    return pl.pallas_call(
        functools.partial(ffn_kernel, n_pieces=n, halves=halves),
        grid_spec=pltpu.PrefetchScalarGridSpec(
            num_scalar_prefetch=1,
            grid=(length // rows,),
            in_specs=[ANY] * n + [narrow, narrow],
            out_specs=[narrow, narrow, wide, wide, wide],
            scratch_shapes=[
                pltpu.VMEM((halves, width, (width + 2 * inner) // halves), bf16),
                pltpu.SemaphoreType.DMA((blocks,)),
            ],
        ),
        out_shape=[
            jax.ShapeDtypeStruct((length, width), f32),
            jax.ShapeDtypeStruct((length, width), bf16),
            wide_shape,
            wide_shape,
            wide_shape,
        ],
        compiler_params=params(48),
        cost_estimate=cost(2 * length * width * (width + 2 * inner), 8 * width * inner + 8 * length * inner),
        name="ffn",
    )(tab, *pieces, x, mixed)


def ffn_back_kernel(tab2_ref, tab3_ref, *refs, n2, n3, halves):
    pieces2, pieces3 = refs[:n2], refs[n2 : n2 + n3]
    middle_ref, hidden_ref, slope_g_ref, slope_u_ref, cot_ref = refs[n2 + n3 : n2 + n3 + 5]
    (
        output_ref, gg_ref, gu_ref, grad_middle_ref, attn_grad_ref, grad_mixed_ref,
        weight2, weight3, sem2, sem3,
    ) = refs[n2 + n3 + 5 :]

    @pl.when(pl.program_id(0) == 0)
    def _():
        copies = load_weight(pieces3, tab3_ref, weight3, sem3)
        copies += load_weight(pieces2, tab2_ref, weight2, sem2)
        wait_all(copies)

    width = cot_ref.shape[1] // halves
    inner = hidden_ref.shape[1] // halves
    middle = middle_ref[...]
    hidden = hidden_ref[...]
    cot = cot_ref[...]
    for h in range(halves):
        cols = slice(h * width, (h + 1) * width)
        output_ref[:, cols] = (middle[:, cols] + dot(hidden, weight3[h])).astype(bf16)
    grad = jnp.zeros(middle.shape, f32)
    step = min(512, inner)
    for h in range(halves):
        for c in range(0, inner, step):
            cols = slice(h * inner + c, h * inner + c + step)
            grad_hidden = jnp.zeros((middle.shape[0], step), f32)
            for j in range(halves):
                grad_hidden += dot(cot[:, j * width : (j + 1) * width], weight3[j, cols, :], NT)
            gg = (grad_hidden * slope_g_ref[:, cols].astype(f32)).astype(bf16)
            gu = (grad_hidden * slope_u_ref[:, cols].astype(f32)).astype(bf16)
            gg_ref[:, cols] = gg
            gu_ref[:, cols] = gu
            grad += dot(gg, weight2[h, :, width + c : width + c + step], NT)
            grad += dot(gu, weight2[h, :, width + inner + c : width + inner + c + step], NT)
    inverse = lax.rsqrt(jnp.mean(middle * middle, -1, keepdims=True) + epsilon)
    normed = middle * inverse
    grad_middle = cot.astype(f32) + inverse * (
        grad - normed * jnp.mean(grad * normed, -1, keepdims=True)
    )
    grad_middle_ref[...] = grad_middle
    low = grad_middle.astype(bf16)
    attn_grad_ref[...] = low
    total = jnp.zeros(middle.shape, f32)
    for h in range(halves):
        total += dot(low[:, h * width : (h + 1) * width], weight2[h, :, 0:width], NT)
    grad_mixed_ref[...] = total.astype(bf16)


def ffn_back(tab2, pieces2, tab3, pieces3, middle, hidden, slope_g, slope_u, cot, halves):
    length, width = middle.shape
    inner = hidden.shape[1]
    rows = BLOCK
    n2, n3 = len(pieces2), len(pieces3)
    narrow = pl.BlockSpec((rows, width), lambda i, t, u: (i, 0))
    wide = pl.BlockSpec((rows, inner), lambda i, t, u: (i, 0))
    narrow_low = jax.ShapeDtypeStruct((length, width), bf16)
    wide_low = jax.ShapeDtypeStruct((length, inner), bf16)
    return pl.pallas_call(
        functools.partial(ffn_back_kernel, n2=n2, n3=n3, halves=halves),
        grid_spec=pltpu.PrefetchScalarGridSpec(
            num_scalar_prefetch=2,
            grid=(length // rows,),
            in_specs=[ANY] * (n2 + n3) + [narrow, wide, wide, wide, narrow],
            out_specs=[narrow, wide, wide, narrow, narrow, narrow],
            scratch_shapes=[
                pltpu.VMEM((halves, width, (width + 2 * inner) // halves), bf16),
                pltpu.VMEM((halves, inner, width // halves), bf16),
                pltpu.SemaphoreType.DMA((sum(p.shape[0] for p in pieces2),)),
                pltpu.SemaphoreType.DMA((sum(p.shape[0] for p in pieces3),)),
            ],
        ),
        out_shape=[
            narrow_low,
            wide_low,
            wide_low,
            jax.ShapeDtypeStruct((length, width), f32),
            narrow_low,
            narrow_low,
        ],
        compiler_params=params(56),
        cost_estimate=cost(
            2 * length * width * (width + 4 * inner), 12 * width * inner + 12 * length * inner
        ),
        name="ffn_back",
    )(tab2, tab3, *pieces2, *pieces3, middle, hidden, slope_g, slope_u, cot)


def input_kernel(tab_ref, *refs, n_pieces, halves):
    pieces = refs[:n_pieces]
    x_ref, grad_middle_ref, dq_ref, dk_ref, dv_ref, out_ref, weight, sem = refs[n_pieces:]

    @pl.when(pl.program_id(0) == 0)
    def _():
        wait_all(load_weight(pieces, tab_ref, weight, sem))

    width = x_ref.shape[1] // halves
    grad = jnp.zeros(x_ref.shape, f32)
    for h in range(halves):
        for part, ref in ((0, dq_ref), (1, dk_ref), (2, dv_ref)):
            grad += dot(
                ref[:, h * width : (h + 1) * width],
                weight[h, :, part * width : (part + 1) * width],
                NT,
            )
    x = x_ref[...].astype(f32)
    inverse = lax.rsqrt(jnp.mean(x * x, -1, keepdims=True) + epsilon)
    normed = x * inverse
    out_ref[...] = grad_middle_ref[...] + inverse * (
        grad - normed * jnp.mean(grad * normed, -1, keepdims=True)
    )


def input_grad(tab, pieces, x, grad_middle, dq, dk, dv, halves):
    length, width = x.shape
    rows = BLOCK
    n = len(pieces)
    blocks = sum(p.shape[0] for p in pieces)
    block = pl.BlockSpec((rows, width), lambda i, t: (i, 0))
    return pl.pallas_call(
        functools.partial(input_kernel, n_pieces=n, halves=halves),
        grid_spec=pltpu.PrefetchScalarGridSpec(
            num_scalar_prefetch=1,
            grid=(length // rows,),
            in_specs=[ANY] * n + [block] * 5,
            out_specs=block,
            scratch_shapes=[
                pltpu.VMEM((halves, width, 3 * width // halves), bf16),
                pltpu.SemaphoreType.DMA((blocks,)),
            ],
        ),
        out_shape=jax.ShapeDtypeStruct((length, width), f32),
        compiler_params=params(40),
        cost_estimate=cost(6 * length * width * width, 20 * length * width),
        name="input_grad",
    )(tab, *pieces, x, grad_middle, dq, dk, dv)


def weight_kernel(tab_ref, *refs, n_right, block_rows, halves):
    left_ref, rights = refs[0], refs[1 : 1 + n_right]
    keep_ref, send_ref, held, sem = refs[1 + n_right :]
    step, steps = pl.program_id(0), pl.num_programs(0)
    slot = lax.rem(step, 2)
    rows = left_ref.shape[1]
    count = rows // block_rows
    kept = keep_ref.shape[0]

    def wait(which):
        for i in range(count * halves):
            pltpu.make_async_copy(held.at[which, 0, pl.ds(0, block_rows)], keep_ref.at[0], sem.at[which, i]).wait()

    @pl.when(step >= 2)
    def _():
        wait(slot)

    left = left_ref[...]
    for h in range(halves):
        offset = 0
        for right in rights:
            width = right.shape[1] // halves
            held[slot, h, :, offset : offset + width] = dot(
                left, right[:, h * width : (h + 1) * width], TN
            ).astype(bf16)
            offset += width
    for b in range(count):
        for h in range(halves):
            place = tab_ref[(step * count + b) * halves + h]
            source = held.at[slot, h, pl.ds(b * block_rows, block_rows)]
            signal = sem.at[slot, b * halves + h]

            @pl.when(place < kept)
            def _():
                pltpu.make_async_copy(source, keep_ref.at[place], signal).start()

            @pl.when(place >= kept)
            def _():
                pltpu.make_async_copy(source, send_ref.at[place - kept], signal).start()

    @pl.when(step == steps - 1)
    def _():
        wait(slot)

        @pl.when(steps > 1)
        def _():
            wait(1 - slot)


def weight_grad(tab, left, rights, block_rows, halves, steps, two, name):
    length, rows = left.shape
    columns = sum(r.shape[1] for r in rights) // halves
    blocks = rows // block_rows * halves
    kept = blocks // 2 if two else blocks
    sent = blocks - kept if two else 1
    step_rows = rows // steps
    return pl.pallas_call(
        functools.partial(weight_kernel, n_right=len(rights), block_rows=block_rows, halves=halves),
        grid_spec=pltpu.PrefetchScalarGridSpec(
            num_scalar_prefetch=1,
            grid=(steps,),
            in_specs=[pl.BlockSpec((length, step_rows), lambda i, t: (0, i))]
            + [pl.BlockSpec(r.shape, lambda i, t: (0, 0)) for r in rights],
            out_specs=[ANY, ANY],
            scratch_shapes=[
                pltpu.VMEM((2, halves, step_rows, columns), bf16),
                pltpu.SemaphoreType.DMA((2, step_rows // block_rows * halves)),
            ],
        ),
        out_shape=[
            jax.ShapeDtypeStruct((kept, block_rows, columns), bf16),
            jax.ShapeDtypeStruct((sent, block_rows, columns), bf16),
        ],
        compiler_params=params(48),
        cost_estimate=cost(
            2 * length * rows * columns * halves,
            2 * (length * rows + length * columns * halves + rows * columns * halves),
        ),
        name=name,
    )(tab, left, *rights)


def place_of(xr, yr, zr, cr):
    low = xr * 4 + yr * 2 + zr
    high = 8 + yr * 4 + xr * 2 + (zr - 2)
    return cr * 16 + jnp.where(zr < 2, low, high)


def swapped(bits, axis="shard"):
    count = lax.axis_size(axis)
    pairs = [(i, i ^ bits) for i in range(count)]
    return lambda array: lax.ppermute(array, axis, pairs)


class Direct:
    halves = 2
    two = True

    def __init__(self):
        self.me = lax.axis_index("shard")
        self.x = lax.axis_index("rep")
        self.core, self.y, self.x_move = swapped(1), swapped(2), swapped(1, "rep")
        self.z = [swapped(4), swapped(8), swapped(12)]
        shard = jnp.arange(16, dtype=jnp.int32)[:, None]
        half = jnp.arange(2, dtype=jnp.int32)[None, :]
        rel = shard ^ self.me
        place = place_of(half ^ self.x, (rel >> 1) & 1, rel >> 2, rel & 1)
        self.place = place.reshape(32)
        order = []
        for cr in range(2):
            for zs in ((0, 1), (2, 3)):
                for outer in range(2):
                    for inner in range(2):
                        for zr in zs:
                            xr, yr = (outer, inner) if zs[0] == 0 else (inner, outer)
                            order.append((zr * 4 + yr * 2 + cr, xr))
        rel_shard = jnp.array([o[0] for o in order], jnp.int32)
        rel_half = jnp.array([o[1] for o in order], jnp.int32)
        self.tab = jnp.stack([rel_shard ^ self.me, rel_half ^ self.x])

    def own_half(self, array):
        width = array.shape[1] // 2
        return lax.dynamic_slice(array, (0, self.x * width), (array.shape[0], width))

    def pack(self, arrays):
        return jnp.concatenate([self.own_half(a) for a in arrays], 1)

    def gather(self, block):
        own = block[None]
        z1, z2, z3 = (move(own) for move in self.z)
        a1 = jnp.concatenate([own, z1], 0)
        b1 = jnp.concatenate([z2, z3], 0)
        a2 = jnp.concatenate([a1, self.y(a1)], 0)
        b2 = jnp.concatenate([b1, self.x_move(b1)], 0)
        a2x, b2y = self.x_move(a2), self.y(b2)
        own_core = [a2, a2x, b2, b2y]
        return own_core + [self.core(p) for p in own_core]

    def scatter(self, grads):
        keep, send = grads
        got = self.core(send)

        def add(*terms):
            total = terms[0].astype(f32)
            for term in terms[1:]:
                total = total + term.astype(f32)
            return total

        ax = self.x_move(add(keep[4:8], got[4:8]).astype(bf16))
        by = self.y(add(keep[12:16], got[12:16]).astype(bf16))
        ay = self.y(add(keep[2:4], got[2:4], ax[2:4]).astype(bf16))
        bx = self.x_move(add(keep[10:12], got[10:12], by[2:4]).astype(bf16))
        z1 = self.z[0](add(keep[1], got[1], ax[1], ay[1]).astype(bf16))
        z2 = self.z[1](add(keep[8], got[8], by[0], bx[0]).astype(bf16))
        z3 = self.z[2](add(keep[9], got[9], by[1], bx[1]).astype(bf16))
        own = add(keep[0], got[0], ax[0], ay[0], z1, z2, z3).astype(bf16)
        other = self.x_move(own)
        return [jnp.where(self.x == 0, own, other), jnp.where(self.x == 0, other, own)]


class Plain:
    halves = 1
    two = False

    def __init__(self):
        self.place = jnp.zeros((1,), jnp.int32)
        self.tab = jnp.zeros((2, 1), jnp.int32)

    def pack(self, arrays):
        return jnp.concatenate(arrays, 1)

    def gather(self, block):
        return [lax.all_gather(block, "shard", axis=0, tiled=True)[None]]

    def scatter(self, grads):
        part = lax.psum_scatter(grads[0][0].astype(f32), "shard", scatter_dimension=0, tiled=True)
        return [lax.psum(part.astype(bf16), "rep")]


def columns_of(halves, *widths):
    arrays = []
    offset = 0
    for width in widths:
        step = width // len(halves)
        arrays.append(
            jnp.concatenate([h[:, offset : offset + step] for h in halves], 1).astype(f32)
        )
        offset += step
    return arrays


def one_sequence(moves, x, docs, tabs, w1, w2, w3, cot, inner):
    cosine, sine = rope_tables(x.shape[0])
    q_marks, k_marks = marks(docs.reshape(-1, 1))
    halves = moves.halves
    normed1, q, k, v = project(tabs, w1, x, cosine, sine, halves)
    mixed, inv, exps = attend(q, k, v, q_marks, k_marks)
    middle, normed2, hidden, slope_g, slope_u = ffn(tabs, w2, x, mixed, inner, halves)
    output, gg, gu, grad_middle, attn_grad, grad_mixed = ffn_back(
        tabs, w2, tabs, w3, middle, hidden, slope_g, slope_u, cot, halves
    )
    dq, dk, dv = attend_back(q, k, v, mixed, inv, exps, grad_mixed, cosine, sine)
    grad_input = input_grad(tabs, w1, x, grad_middle, dq, dk, dv, halves)
    width = x.shape[1]
    place = moves.place

    def cut(rows):
        return rows // 16 if moves.two else rows

    def weights(left, rights, steps, name):
        rows = left.shape[1]
        steps = steps if moves.two else 1
        return weight_grad(place, left, rights, cut(rows), halves, steps, moves.two, name)

    g3 = weights(hidden, [cot], 8, "grad_down")
    g2 = weights(normed2, [gg, gu], 2, "grad_gate_up")
    go = weights(mixed, [attn_grad], 2, "grad_out")
    g1 = weights(normed1, [dq, dk, dv], 2, "grad_qkv")
    return output, grad_input, g1, go, g2, g3


def per_device(
    inputs,
    doc_ids,
    attn_gain,
    w_query,
    w_key,
    w_value,
    w_out,
    ffn_gain,
    w_gate,
    w_up,
    w_down,
    cotangent,
):
    batch_size, length, width = inputs.shape
    inner = w_gate.shape[1]
    replicas, members = lax.axis_size("rep"), lax.axis_size("shard")
    moves = Direct() if (replicas, members, batch_size) == (2, 16, 1) else Plain()
    gain1 = attn_gain.astype(f32)[:, None]
    gain2 = ffn_gain.astype(f32)[:, None]

    def fold(weight, gain):
        return (weight.astype(f32) * gain).astype(bf16)

    w1 = moves.gather(moves.pack([fold(w, gain1) for w in (w_query, w_key, w_value)]))
    w2 = moves.gather(moves.pack([w_out, fold(w_gate, gain2), fold(w_up, gain2)]))
    w3 = moves.gather(moves.pack([w_down]))
    outputs, grad_inputs, totals = [], [], None
    for b in range(batch_size):
        output, grad_input, *grads = one_sequence(
            moves, inputs[b], doc_ids[b], moves.tab, w1, w2, w3, cotangent[b], inner
        )
        outputs.append(output)
        grad_inputs.append(grad_input)
        totals = grads if totals is None else jax.tree.map(jnp.add, totals, grads)
    g1, go, g2, g3 = totals
    scale = 1.0 / (batch_size * replicas * members)
    (down,) = columns_of(moves.scatter(g3), width)
    gate, up = columns_of(moves.scatter(g2), inner, inner)
    (out,) = columns_of(moves.scatter(go), width)
    query, key, value = columns_of(moves.scatter(g1), width, width, width)

    def gain_grad(pairs):
        total = sum(jnp.sum(w.astype(f32) * g, 1) for w, g in pairs)
        return total * scale

    return (
        jnp.stack(outputs),
        jnp.stack(grad_inputs),
        gain_grad([(w_query, query), (w_key, key), (w_value, value)]),
        query * gain1 * scale,
        key * gain1 * scale,
        value * gain1 * scale,
        out * scale,
        gain_grad([(w_gate, gate), (w_up, up)]),
        gate * gain2 * scale,
        up * gain2 * scale,
        down * scale,
    )


def solution(mesh):
    row = P("shard", None)
    tokens = P(("rep", "shard"), None, None)
    return jax.shard_map(
        per_device,
        mesh=mesh,
        in_specs=(
            tokens, P(("rep", "shard"), None), P("shard"), row, row, row, row, P("shard"), row, row, row, tokens,
        ),
        out_specs=(tokens, tokens, P("shard"), row, row, row, row, P("shard"), row, row, row),
        check_vma=False,
    )
```

time: 954 us -> 395 us (0.41)
  waiting for transfers between devices: 465 us -> 102 us
  matrix products: 252 us -> 0 us
  Pallas kernels: 0 us -> 169 us
  other arithmetic: 107 us -> 28.3 us
  blocking collectives: 72 us -> 0 us
  starting transfers between devices: 0.81 us -> 67.4 us
  between operations: 16.3 us -> 2.3 us
  local copies, waits for them, and re-layouts: 31.4 us -> 19.1 us
    reduce_scatter x7 -> x0, waiting for transfers between devices: 300 us -> none  [the longest x1 87.3 us: per_device(): lax.psum_scatter(grad_w_gate, 'shard', scatter_dimension=0, tiled=True)]
    dot_general x33 -> x0, matrix products: 252 us -> none  [the longest x7 38.3 us: right_transposed(): lax.dot_general(left, right, (((1,), (1,)), ((), ())), preferred_element_...]
    pallas_call x0 -> x10, Pallas kernels: none -> 169 us  [the longest x4 42.3 us: weight_grad(): pl.pallas_call(functools.partial(weight_kernel, n_right=len(rights), bloc...]
    all_gather x7 -> x0, waiting for transfers between devices: 137 us -> none  [the longest x1 37.2 us: per_device(): lax.all_gather(w_query, 'shard', axis=0, tiled=True)]
    ppermute x0 -> x69, waiting for transfers between devices: none -> 102 us  [swapped(): return lambda array: lax.ppermute(array, axis, pairs)]
    ppermute x0 -> x69, starting transfers between devices: none -> 67.4 us  [swapped(): return lambda array: lax.ppermute(array, axis, pairs)]
    unnamed x2 -> x0, blocking collectives: 67.1 us -> none
    convert_element_type x13 -> x22, other arithmetic: 56.7 us -> 15.5 us  [the longest x7 3.86 us: fold(): return (weight.astype(f32) * gain).astype(bf16)]
  transfers between devices with their start and end apart: 15 -> 69, of which waited for: 9 -> 23; matrix products, arithmetic and copies ran while one was open for 36% -> 7% of each run, Pallas kernels for 0% -> 34%
where the time goes in v1:
time: 395 us; the launch traced here: 389 us
  Pallas kernels  169 us (43%)
  waiting for transfers between devices  102 us (26%)
  starting transfers between devices  67.4 us (17%)
  other arithmetic  28.3 us (7%)
  local copies, waits for them, and re-layouts  19.1 us (5%)
    ppermute x69, waiting for transfers between devices, swapped(): return lambda array: lax.ppermute(array, axis, pairs)  102 us
    ppermute x69, starting transfers between devices, swapped(): return lambda array: lax.ppermute(array, axis, pairs)  67.4 us
    pallas_call x4, Pallas kernels, weight_grad(): pl.pallas_call(functools.partial(weight_kernel, n_right=len(rights), bloc...  42.3 us
    pallas_call x1, Pallas kernels, ffn_back(): pl.pallas_call(functools.partial(ffn_back_kernel, n2=n2, n3=n3, halves=ha...  31.3 us
    pallas_call x1, Pallas kernels, attend(): pl.pallas_call(attend_kernel, grid=(pairs,), in_specs=[column, column, co...  26.1 us
    pallas_call x1, Pallas kernels, ffn(): pl.pallas_call(functools.partial(ffn_kernel, n_pieces=n, halves=halves),...  23.4 us
    pallas_call x1, Pallas kernels, attend_back(): pl.pallas_call(attend_back_kernel, grid=(pairs,), in_specs=[column] * 5 +...  20.4 us
    unnamed x134, local copies, waits for them, and re-layouts  18.1 us
  transfers between devices with their start and end apart: 69, of which 23 were waited for; matrix products, arithmetic and copies ran while one was open for 7% of the time, Pallas kernels for 34%

profile of v1, /device:TPU:0, one launch (start us, length us, event | category | flops | bytes accessed | tf_op | source)
XLA Modules:
  0.0 388.7 jit_solution(221894439917706863)
XLA Ops:
  1.6 5.1 %collective-permute-start.15 = (bf16[1,128,384]{2,1,0:T(8,128)(2,1)S(1)}, bf16[1,128,384]{2,1,0:T(8,128)(2,1)S(1)}, u32[]{:S(2)}, u32[]{:S(2)}) collective-permute-start(bf16[1,128,384]{2,1,0:T(8,128)(2,1)S(1)} %dynamic-slice_bitcast_fusion), channel_id=1, source_target_pairs={{0,12},{1,13},{2,14},{3,15},{4,8},{5,9},{6,10},{7,11},{8,4},{9,5},... | collective-permute-start | bytes 294920 | tf_op jit(solution)/shard_map/ppermute | solution.py:570
  10.8 3.8 collective-permute-start.26
  21.1 3.8 collective-permute-start.4
  31.8 2.1 collective-permute-done.4
  35.3 9.2 %collective-permute-done.3 = bf16[1,48,2432]{2,1,0:T(8,128)(2,1)S(1)} collective-permute-done((bf16[1,48,2432]{2,1,0:T(8,128)(2,1)S(1)}, bf16[1,48,2432]{2,1,0:T(8,128)(2,1)S(1)}, u32[]{:S(2)}, u32[]{:S(2)}) %collective-permute-start.3) | collective-permute-done | bytes 233504 | tf_op jit(solution)/shard_map/ppermute | solution.py:570
  48.3 9.3 %collective-permute-done.5 = bf16[2,48,2432]{2,1,0:T(8,128)(2,1)S(1)} collective-permute-done((bf16[2,48,2432]{2,1,0:T(8,128)(2,1)S(1)}, bf16[2,48,2432]{2,1,0:T(8,128)(2,1)S(1)}, u32[]{:S(2)}, u32[]{:S(2)}) %collective-permute-start.5) | collective-permute-done | bytes 466976 | tf_op jit(solution)/shard_map/ppermute | solution.py:570
  57.7 3.3 collective-permute-done.1
  65.8 25.5 %collective-permute-done.28.refs_3_ = bf16[4,48,1152]{2,1,0:T(8,128)(2,1)S(1)} collective-permute-done((bf16[4,48,1152]{2,1,0:T(8,128)(2,1)S(1)}, bf16[4,48,1152]{2,1,0:T(8,128)(2,1)S(1)}, u32[]{:S(2)}, u32[]{:S(2)}) %collective-permute-start.28) | collective-permute-done | bytes 442400 | tf_op jit(solution)/shard_map/ppermute | solution.py:570
  95.7 12.0 %project.1 = (bf16[1024,768]{1,0:T(8,128)(2,1)S(1)}, bf16[1024,768]{1,0:T(8,128)(2,1)S(1)}, bf16[1024,768]{1,0:T(8,128)(2,1)S(1)}, bf16[1024,768]{1,0:T(8,128)(2,1)S(1)}) custom-call(s32[2,32]{1,0:T(2,128)S(1)} %pad_add_fusion.tab_ref.tab2_ref.tab3_ref, bf16[4,48,1152]{2,1,0:T(8,128)(2,1)S(1)} %pad_maximum_fusion.5.refs_0_, ...), custom_call_target="tpu_custom_call" | custom-call | flops 3623878656 | bytes 12582912 | tf_op jit(solution)/shard_map/project/pallas_call | solution.py:113
  116.7 26.1 %attend.1 = (bf16[1024,768]{1,0:T(8,128)(2,1)S(1)}, f32[1024,768]{1,0:T(8,128)}, bf16[12,4,768,256]{3,2,1,0:T(8,128)(2,1)}) custom-call(bf16[1024,768]{1,0:T(8,128)(2,1)S(1)} %copy-done.33, bf16[1024,768]{1,0:T(8,128)(2,1)S(1)} %copy-done.35, bf16[1024,768]{1,0:T(8,128)(2,1)} %copy-done.36, bf16[1024,128]{1,0:T(8,128)(2,1)S(1)} %get-tuple-element.126.qm_ref, ...), custom_call_target="tpu_custom_call" | custom-call | flops 8053063680 | bytes 23592960 | tf_op jit(solution)/shard_map/attend/pallas_call | solution.py:187
  145.7 23.4 %ffn.1 = (f32[1024,768]{1,0:T(8,128)}, bf16[1024,768]{1,0:T(8,128)(2,1)}, bf16[1024,2048]{1,0:T(8,128)(2,1)}, bf16[1024,2048]{1,0:T(8,128)(2,1)}, bf16[1024,2048]{1,0:T(8,128)(2,1)}) custom-call(s32[2,32]{1,0:T(2,128)S(1)} %pad_add_fusion.tab_ref.tab2_ref.tab3_ref, bf16[4,48,2432]{2,1,0:T(8,128)(2,1)S(1)} %pad_maximum_fusion.refs_0_, ...), custom_call_target="tpu_custom_call" | custom-call | flops 7650410496 | bytes 29360128 | tf_op jit(solution)/shard_map/ffn/pallas_call | solution.py:315
  169.2 10.9 %grad_down.1 = (bf16[16,128,384]{2,1,0:T(8,128)(2,1)S(1)}, bf16[16,128,384]{2,1,0:T(8,128)(2,1)}) custom-call(s32[32]{0:T(128)S(1)} %add.462.tab_ref, bf16[1024,2048]{1,0:T(8,128)(2,1)} %get-tuple-element.45.refs_17_.refs_0_, bf16[1024,768]{1,0:T(8,128)(2,1)S(1)} %bitcast.75), custom_call_target="tpu_custom_call" | custom-call | flops 3221225472 | bytes 8912896 | tf_op jit(solution)/shard_map/grad_down/pallas_call | solution.py:535
  181.3 31.3 %ffn_back.1 = (bf16[1024,768]{1,0:T(8,128)(2,1)}, bf16[1024,2048]{1,0:T(8,128)(2,1)}, bf16[1024,2048]{1,0:T(8,128)(2,1)}, f32[1024,768]{1,0:T(8,128)}, bf16[1024...) custom-call(s32[2,32]{1,0:T(2,128)} %copy-done.21, s32[2,32]{1,0:T(2,128)} %copy-done.21, bf16[4,48,2432]{2,1,0:T(8,128)(2,1)} %copy-done.7, ...), custom_call_target="tpu_custom_call" | custom-call | flops 14092861440 | bytes 44040192 | tf_op jit(solution)/shard_map/ffn_back/pallas_call | solution.py:399
  214.0 5.1 %grad_out.1 = (bf16[16,48,384]{2,1,0:T(8,128)(2,1)S(1)}, bf16[16,48,384]{2,1,0:T(8,128)(2,1)S(1)}) custom-call(s32[32]{0:T(128)S(1)} %add.462.tab_ref, bf16[1024,768]{1,0:T(8,128)(2,1)S(1)} %copy-done.28, bf16[1024,768]{1,0:T(8,128)(2,1)S(1)} %copy-done.29), custom_call_target="tpu_custom_call" | custom-call | flops 1207959552 | bytes 4325376 | tf_op jit(solution)/shard_map/grad_out/pallas_call | solution.py:535
  219.7 20.4 %attend_back.1 = (bf16[1024,768]{1,0:T(8,128)(2,1)S(1)}, bf16[1024,768]{1,0:T(8,128)(2,1)S(1)}, bf16[1024,768]{1,0:T(8,128)(2,1)S(1)}) custom-call(bf16[1024,768]{1,0:T(8,128)(2,1)} %copy-done.32, bf16[1024,768]{1,0:T(8,128)(2,1)} %copy-done.34, bf16[1024,768]{1,0:T(8,128)(2,1)} %copy-done.36, bf16[1024,768]{1,0:T(8,128)(2,1)} %copy-done.27, ...), custom_call_target="tpu_custom_call" | custom-call | flops 16106127360 | bytes 28311552 | tf_op jit(solution)/shard_map/attend_back/pallas_call | solution.py:263
  243.4 9.0 %grad_qkv.1 = (bf16[16,48,1152]{2,1,0:T(8,128)(2,1)}, bf16[16,48,1152]{2,1,0:T(8,128)(2,1)}) custom-call(s32[32]{0:T(128)S(1)} %add.462.tab_ref, bf16[1024,768]{1,0:T(8,128)(2,1)S(1)} %copy-done.31, bf16[1024,768]{1,0:T(8,128)(2,1)S(1)} %get-tuple-element.53.refs_10_.refs_1_, bf16[1024,768]{1,0:T(8,128)(2,1)S(1)} %get-tuple-element.54.refs_11_.refs_2_, ...), custom_call_target="tpu_custom_call" | custom-call | flops 3623878656 | bytes 9830400 | tf_op jit(solution)/shard_map/grad_qkv/pallas_call | solution.py:535
  255.3 17.2 %grad_gate_up.1 = (bf16[16,48,2048]{2,1,0:T(8,128)(2,1)S(1)}, bf16[16,48,2048]{2,1,0:T(8,128)(2,1)}) custom-call(s32[32]{0:T(128)S(1)} %add.462.tab_ref, bf16[1024,768]{1,0:T(8,128)(2,1)S(1)} %copy-done.37, bf16[1024,2048]{1,0:T(8,128)(2,1)} %get-tuple-element.63.refs_1_, bf16[1024,2048]{1,0:T(8,128)(2,1)} %get-tuple-element.64.refs_2_), custom_call_target="tpu_custom_call" | custom-call | flops 6442450944 | bytes 16252928 | tf_op jit(solution)/shard_map/grad_gate_up/pallas_call | solution.py:535
  273.8 2.3 collective-permute-start.49
  284.9 13.6 %input_grad.1 = f32[1024,768]{1,0:T(8,128)} custom-call(s32[2,32]{1,0:T(2,128)S(1)} %copy-done.22, bf16[4,48,1152]{2,1,0:T(8,128)(2,1)S(1)} %pad_maximum_fusion.5.refs_0_, bf16[4,48,1152]{2,1,0:T(8,128)(2,1)S(1)} %copy-done.13, bf16[4,48,1152]{2,1,0:T(8,128)(2,1)S(1)} %constant_dynamic-update-slice_fusion.6.refs_2_, bf16[4,48,1152]{2,1,0:T(8,128)(2,1)S(1)} %copy-done.11, ...), custom_call_target="tpu_custom_call" | custom-call | flops 3623878656 | bytes 15728640 | tf_op jit(solution)/shard_map/input_grad/pallas_call | solution.py:460
  306.3 2.0 collective-permute-done.62
  312.1 2.0 collective-permute-start.67
  314.0 5.0 %collective-permute-done.66 = bf16[128,384]{1,0:T(8,128)(2,1)S(1)} collective-permute-done((bf16[128,384]{1,0:T(8,128)(2,1)S(1)}, bf16[128,384]{1,0:T(8,128)(2,1)S(1)}, u32[]{:S(2)}, u32[]{:S(2)}) %collective-permute-start.66) | collective-permute-done | bytes 98336 | tf_op jit(solution)/shard_map/ppermute | solution.py:570
  319.7 3.9 %collective-permute-done.63 = bf16[128,384]{1,0:T(8,128)(2,1)S(1)} collective-permute-done((bf16[128,384]{1,0:T(8,128)(2,1)S(1)}, bf16[128,384]{1,0:T(8,128)(2,1)S(1)}, u32[]{:S(2)}, u32[]{:S(2)}) %collective-permute-start.63) | collective-permute-done | bytes 98336 | tf_op jit(solution)/shard_map/ppermute | solution.py:570
  329.4 2.6 collective-permute-done.35
  332.0 2.0 collective-permute-done.38
  335.2 2.0 collective-permute-start.39
  337.2 2.9 collective-permute-start.40
  348.8 9.9 %collective-permute-done.41 = bf16[48,1152]{1,0:T(8,128)(2,1)S(1)} collective-permute-done((bf16[48,1152]{1,0:T(8,128)(2,1)S(1)}, bf16[48,1152]{1,0:T(8,128)(2,1)S(1)}, u32[]{:S(2)}, u32[]{:S(2)}) %collective-permute-start.41) | collective-permute-done | bytes 110624 | tf_op jit(solution)/shard_map/ppermute | solution.py:570
  360.9 6.1 %collective-permute-done.53 = bf16[2,48,2048]{2,1,0:T(8,128)(2,1)S(1)} collective-permute-done((bf16[2,48,2048]{2,1,0:T(8,128)(2,1)S(1)}, bf16[2,48,2048]{2,1,0:T(8,128)(2,1)S(1)}, u32[]{:S(2)}, u32[]{:S(2)}) %collective-permute-start.53) | collective-permute-done | bytes 393248 | tf_op jit(solution)/shard_map/ppermute | solution.py:570
  369.1 2.5 collective-permute-start.58
  372.7 6.0 %collective-permute-done.57 = bf16[48,2048]{1,0:T(8,128)(2,1)S(1)} collective-permute-done((bf16[48,2048]{1,0:T(8,128)(2,1)S(1)}, bf16[48,2048]{1,0:T(8,128)(2,1)S(1)}, u32[]{:S(2)}, u32[]{:S(2)}) %collective-permute-start.57) | collective-permute-done | bytes 196640 | tf_op jit(solution)/shard_map/ppermute | solution.py:570
  382.5 3.9 %collective-permute-done.59 = bf16[48,2048]{1,0:T(8,128)(2,1)S(1)} collective-permute-done((bf16[48,2048]{1,0:T(8,128)(2,1)S(1)}, bf16[48,2048]{1,0:T(8,128)(2,1)S(1)}, u32[]{:S(2)}, u32[]{:S(2)}) %collective-permute-start.59) | collective-permute-done | bytes 196640 | tf_op jit(solution)/shard_map/ppermute | solution.py:570
  (320 shorter events, 102.1 us)
Async XLA Ops:
  1.6 19.5 %collective-permute-start.15 = (bf16[1,128,384]{2,1,0:T(8,128)(2,1)S(1)}, bf16[1,128,384]{2,1,0:T(8,128)(2,1)S(1)}, u32[]{:S(2)}, u32[]{:S(2)}) collective-permute-start(bf16[1,128,384]{2,1,0:T(8,128)(2,1)S(1)} %dynamic-slice_bitcast_fusion), channel_id=1, source_target_pairs={{0,12},{1,13},{2,14},{3,15},{4,8},{5,9},{6,10},{7,11},{8,4},{9,5},... | collective-permute-start | bytes 294920 | tf_op jit(solution)/shard_map/ppermute | solution.py:570
  6.7 18.2 %collective-permute-start.14 = (bf16[1,128,384]{2,1,0:T(8,128)(2,1)S(1)}, bf16[1,128,384]{2,1,0:T(8,128)(2,1)}, u32[]{:S(2)}, u32[]{:S(2)}) collective-permute-start(bf16[1,128,384]{2,1,0:T(8,128)(2,1)S(1)} %dynamic-slice_bitcast_fusion), channel_id=1, source_target_pairs={{0,8},{1,9},{2,10},{3,11},{4,12},{5,13},{6,14},{7,15},{8,0},{9,1},... | collective-permute-start | bytes 294920 | tf_op jit(solution)/shard_map/ppermute | solution.py:570
  25.0 19.5 %collective-permute-start.3 = (bf16[1,48,2432]{2,1,0:T(8,128)(2,1)S(1)}, bf16[1,48,2432]{2,1,0:T(8,128)(2,1)S(1)}, u32[]{:S(2)}, u32[]{:S(2)}) collective-permute-start(bf16[1,48,2432]{2,1,0:T(8,128)(2,1)S(1)} %maximum_bitcast_fusion), channel_id=1, source_target_pairs={{0,8},{1,9},{2,10},{3,11},{4,12},{5,13},{6,14},{7,15},{8,0},{9,1},... | collective-permute-start | bytes 700424 | tf_op jit(solution)/shard_map/ppermute | solution.py:570
  27.1 18.9 %collective-permute-start = (bf16[1,48,2432]{2,1,0:T(8,128)(2,1)S(1)}, bf16[1,48,2432]{2,1,0:T(8,128)(2,1)S(1)}, u32[]{:S(2)}, u32[]{:S(2)}) collective-permute-start(bf16[1,48,2432]{2,1,0:T(8,128)(2,1)S(1)} %maximum_bitcast_fusion), channel_id=1, source_target_pairs={{0,4},{1,5},{2,6},{3,7},{4,0},{5,1},{6,2},{7,3},{8,12},{9,13},{10,... | collective-permute-start | bytes 700424 | tf_op jit(solution)/shard_map/ppermute | solution.py:570
  27.2 37.1 %collective-permute-start.16 = (bf16[2,128,384]{2,1,0:T(8,128)(2,1)S(1)}, bf16[2,128,384]{2,1,0:T(8,128)(2,1)S(1)}, u32[]{:S(2)}, u32[]{:S(2)}) collective-permute-start(bf16[2,128,384]{2,1,0:T(8,128)(2,1)S(1)} %pad_maximum_fusion.10), channel_id=1, source_target_pairs={{0,16},{16,0},{1,17},{17,1},{2,18},{18,2},{3,19},{19,3},{4,20},{20... | collective-permute-start | bytes 589832 | tf_op jit(solution)/shard_map/ppermute | solution.py:570
  30.2 34.6 %collective-permute-start.12 = (bf16[2,128,384]{2,1,0:T(8,128)(2,1)S(1)}, bf16[2,128,384]{2,1,0:T(8,128)(2,1)S(1)}, u32[]{:S(2)}, u32[]{:S(2)}) collective-permute-start(bf16[2,128,384]{2,1,0:T(8,128)(2,1)S(1)} %pad_maximum_fusion.9), channel_id=1, source_target_pairs={{0,2},{1,3},{2,0},{3,1},{4,6},{5,7},{6,4},{7,5},{8,10},{9,11},{10,... | collective-permute-start | bytes 589832 | tf_op jit(solution)/shard_map/ppermute | solution.py:570
  44.5 18.2 %collective-permute-start.23 = (bf16[2,48,1152]{2,1,0:T(8,128)(2,1)S(1)}, bf16[2,48,1152]{2,1,0:T(8,128)(2,1)S(1)}, u32[]{:S(2)}, u32[]{:S(2)}) collective-permute-start(bf16[2,48,1152]{2,1,0:T(8,128)(2,1)S(1)} %pad_maximum_fusion.7), channel_id=1, source_target_pairs={{0,2},{1,3},{2,0},{3,1},{4,6},{5,7},{6,4},{7,5},{8,10},{9,11},{10,... | collective-permute-start | bytes 663560 | tf_op jit(solution)/shard_map/ppermute | solution.py:570
  61.0 34.2 %collective-permute-start.6 = (bf16[4,48,2432]{2,1,0:T(8,128)(2,1)S(1)}, bf16[4,48,2432]{2,1,0:T(8,128)(2,1)S(1)}, u32[]{:S(2)}, u32[]{:S(2)}) collective-permute-start(bf16[4,48,2432]{2,1,0:T(8,128)(2,1)S(1)} %constant_dynamic-update-slice_fusion.refs_2_), channel_id=1, source_target_pairs={{0,2},{1,3},{2,0},{3,1},{4,6},{5,7},{6,4},{7,5},{8,10},{9,11},{10,... | collective-permute-start | bytes 2801672 | tf_op jit(solution)/shard_map/ppermute | solution.py:570
  62.6 32.6 %collective-permute-start.2 = (bf16[4,48,2432]{2,1,0:T(8,128)(2,1)S(1)}, bf16[4,48,2432]{2,1,0:T(8,128)(2,1)S(1)}, u32[]{:S(2)}, u32[]{:S(2)}) collective-permute-start(bf16[4,48,2432]{2,1,0:T(8,128)(2,1)S(1)} %pad_maximum_fusion.refs_0_), channel_id=1, source_target_pairs={{0,16},{16,0},{1,17},{17,1},{2,18},{18,2},{3,19},{19,3},{4,20},{20... | collective-permute-start | bytes 2801672 | tf_op jit(solution)/shard_map/ppermute | solution.py:570
  64.3 27.0 %collective-permute-start.28 = (bf16[4,48,1152]{2,1,0:T(8,128)(2,1)S(1)}, bf16[4,48,1152]{2,1,0:T(8,128)(2,1)S(1)}, u32[]{:S(2)}, u32[]{:S(2)}) collective-permute-start(bf16[4,48,1152]{2,1,0:T(8,128)(2,1)S(1)} %constant_dynamic-update-slice_fusion.6.refs_2_), channel_id=1, source_target_pairs={{0,2},{1,3},{2,0},{3,1},{4,6},{5,7},{6,4},{7,5},{8,10},{9,11},{10,... | collective-permute-start | bytes 1327112 | tf_op jit(solution)/shard_map/ppermute | solution.py:570
  64.8 27.9 %collective-permute-start.24 = (bf16[4,48,1152]{2,1,0:T(8,128)(2,1)S(1)}, bf16[4,48,1152]{2,1,0:T(8,128)(2,1)S(1)}, u32[]{:S(2)}, u32[]{:S(2)}) collective-permute-start(bf16[4,48,1152]{2,1,0:T(8,128)(2,1)S(1)} %pad_maximum_fusion.5.refs_0_), channel_id=1, source_target_pairs={{0,16},{16,0},{1,17},{17,1},{2,18},{18,2},{3,19},{19,3},{4,20},{20... | collective-permute-start | bytes 1327112 | tf_op jit(solution)/shard_map/ppermute | solution.py:570
  65.7 28.2 %collective-permute-start.29 = (bf16[4,48,1152]{2,1,0:T(8,128)(2,1)S(1)}, bf16[4,48,1152]{2,1,0:T(8,128)(2,1)S(1)}, u32[]{:S(2)}, u32[]{:S(2)}) collective-permute-start(bf16[4,48,1152]{2,1,0:T(8,128)(2,1)S(1)} %pad_maximum_fusion.5.refs_0_), channel_id=1, source_target_pairs={{0,1},{1,0},{2,3},{3,2},{4,5},{5,4},{6,7},{7,6},{8,9},{9,8},{10,11... | collective-permute-start | bytes 1327112 | tf_op jit(solution)/shard_map/ppermute | solution.py:570
  93.8 18.5 %collective-permute-start.17 = (bf16[4,128,384]{2,1,0:T(8,128)(2,1)S(1)}, bf16[4,128,384]{2,1,0:T(8,128)(2,1)}, u32[]{:S(2)}, u32[]{:S(2)}) collective-permute-start(bf16[4,128,384]{2,1,0:T(8,128)(2,1)S(1)} %constant_dynamic-update-slice_fusion.3.refs_10_), channel_id=1, source_target_pairs={{0,2},{1,3},{2,0},{3,1},{4,6},{5,7},{6,4},{7,5},{8,10},{9,11},{10,... | collective-permute-start | bytes 1179656 | tf_op jit(solution)/shard_map/ppermute | solution.py:570
  94.6 49.4 %collective-permute-start.9 = (bf16[4,48,2432]{2,1,0:T(8,128)(2,1)S(1)}, bf16[4,48,2432]{2,1,0:T(8,128)(2,1)S(1)}, u32[]{:S(2)}, u32[]{:S(2)}) collective-permute-start(bf16[4,48,2432]{2,1,0:T(8,128)(2,1)S(1)} %constant_dynamic-update-slice_fusion.refs_2_), channel_id=1, source_target_pairs={{0,1},{1,0},{2,3},{3,2},{4,5},{5,4},{6,7},{7,6},{8,9},{9,8},{10,11... | collective-permute-start | bytes 2801672 | tf_op jit(solution)/shard_map/ppermute | solution.py:570
  94.7 49.9 %collective-permute-start.7 = (bf16[4,48,2432]{2,1,0:T(8,128)(2,1)S(1)}, bf16[4,48,2432]{2,1,0:T(8,128)(2,1)S(1)}, u32[]{:S(2)}, u32[]{:S(2)}) collective-permute-start(bf16[4,48,2432]{2,1,0:T(8,128)(2,1)S(1)} %pad_maximum_fusion.refs_0_), channel_id=1, source_target_pairs={{0,1},{1,0},{2,3},{3,2},{4,5},{5,4},{6,7},{7,6},{8,9},{9,8},{10,11... | collective-permute-start | bytes 2801672 | tf_op jit(solution)/shard_map/ppermute | solution.py:570
  95.2 49.5 %collective-permute-start.10 = (bf16[4,48,2432]{2,1,0:T(8,128)(2,1)S(1)}, bf16[4,48,2432]{2,1,0:T(8,128)(2,1)S(1)}, u32[]{:S(2)}, u32[]{:S(2)}) collective-permute-start(bf16[4,48,2432]{2,1,0:T(8,128)(2,1)S(1)} %collective-permute-done.6.refs_3_), channel_id=1, source_target_pairs={{0,1},{1,0},{2,3},{3,2},{4,5},{5,4},{6,7},{7,6},{8,9},{9,8},{10,11... | collective-permute-start | bytes 2801672 | tf_op jit(solution)/shard_map/ppermute | solution.py:570
  95.3 49.8 %collective-permute-start.8 = (bf16[4,48,2432]{2,1,0:T(8,128)(2,1)S(1)}, bf16[4,48,2432]{2,1,0:T(8,128)(2,1)}, u32[]{:S(2)}, u32[]{:S(2)}) collective-permute-start(bf16[4,48,2432]{2,1,0:T(8,128)(2,1)S(1)} %collective-permute-done.2.refs_1_), channel_id=1, source_target_pairs={{0,1},{1,0},{2,3},{3,2},{4,5},{5,4},{6,7},{7,6},{8,9},{9,8},{10,11... | collective-permute-start | bytes 2801672 | tf_op jit(solution)/shard_map/ppermute | solution.py:570
  112.4 31.6 %collective-permute-start.13 = (bf16[4,128,384]{2,1,0:T(8,128)(2,1)S(1)}, bf16[4,128,384]{2,1,0:T(8,128)(2,1)S(1)}, u32[]{:S(2)}, u32[]{:S(2)}) collective-permute-start(bf16[4,128,384]{2,1,0:T(8,128)(2,1)S(1)} %pad_maximum_fusion.6.refs_8_), channel_id=1, source_target_pairs={{0,16},{16,0},{1,17},{17,1},{2,18},{18,2},{3,19},{19,3},{4,20},{20... | collective-permute-start | bytes 1179656 | tf_op jit(solution)/shard_map/ppermute | solution.py:570
  143.9 36.2 %collective-permute-start.20 = (bf16[4,128,384]{2,1,0:T(8,128)(2,1)S(1)}, bf16[4,128,384]{2,1,0:T(8,128)(2,1)S(1)}, u32[]{:S(2)}, u32[]{:S(2)}) collective-permute-start(bf16[4,128,384]{2,1,0:T(8,128)(2,1)S(1)} %constant_dynamic-update-slice_fusion.3.refs_10_), channel_id=1, source_target_pairs={{0,1},{1,0},{2,3},{3,2},{4,5},{5,4},{6,7},{7,6},{8,9},{9,8},{10,11... | collective-permute-start | bytes 1179656 | tf_op jit(solution)/shard_map/ppermute | solution.py:570
  144.0 36.1 %collective-permute-start.18 = (bf16[4,128,384]{2,1,0:T(8,128)(2,1)S(1)}, bf16[4,128,384]{2,1,0:T(8,128)(2,1)S(1)}, u32[]{:S(2)}, u32[]{:S(2)}) collective-permute-start(bf16[4,128,384]{2,1,0:T(8,128)(2,1)S(1)} %pad_maximum_fusion.6.refs_8_), channel_id=1, source_target_pairs={{0,1},{1,0},{2,3},{3,2},{4,5},{5,4},{6,7},{7,6},{8,9},{9,8},{10,11... | collective-permute-start | bytes 1179656 | tf_op jit(solution)/shard_map/ppermute | solution.py:570
  144.6 35.6 %collective-permute-start.21 = (bf16[4,128,384]{2,1,0:T(8,128)(2,1)}, bf16[4,128,384]{2,1,0:T(8,128)(2,1)S(1)}, u32[]{:S(2)}, u32[]{:S(2)}) collective-permute-start(bf16[4,128,384]{2,1,0:T(8,128)(2,1)} %collective-permute-done.17.refs_11_), channel_id=1, source_target_pairs={{0,1},{1,0},{2,3},{3,2},{4,5},{5,4},{6,7},{7,6},{8,9},{9,8},{10,11... | collective-permute-start | bytes 1179656 | tf_op jit(solution)/shard_map/ppermute | solution.py:570
  144.7 35.5 %collective-permute-start.19 = (bf16[4,128,384]{2,1,0:T(8,128)(2,1)S(1)}, bf16[4,128,384]{2,1,0:T(8,128)(2,1)S(1)}, u32[]{:S(2)}, u32[]{:S(2)}) collective-permute-start(bf16[4,128,384]{2,1,0:T(8,128)(2,1)S(1)} %collective-permute-done.13.refs_9_), channel_id=1, source_target_pairs={{0,1},{1,0},{2,3},{3,2},{4,5},{5,4},{6,7},{7,6},{8,9},{9,8},{10,11... | collective-permute-start | bytes 1179656 | tf_op jit(solution)/shard_map/ppermute | solution.py:570
  219.2 22.1 %collective-permute-start.42 = (bf16[16,48,384]{2,1,0:T(8,128)(2,1)S(1)}, bf16[16,48,384]{2,1,0:T(8,128)(2,1)S(1)}, u32[]{:S(2)}, u32[]{:S(2)}) collective-permute-start(bf16[16,48,384]{2,1,0:T(8,128)(2,1)S(1)} %get-tuple-element.61), channel_id=1, source_target_pairs={{0,1},{1,0},{2,3},{3,2},{4,5},{5,4},{6,7},{7,6},{8,9},{9,8},{10,11... | collective-permute-start | bytes 1769480 | tf_op jit(solution)/shard_map/ppermute | solution.py:570
  219.2 56.9 %collective-permute-start.60 = (bf16[16,128,384]{2,1,0:T(8,128)(2,1)}, bf16[16,128,384]{2,1,0:T(8,128)(2,1)}, u32[]{:S(2)}, u32[]{:S(2)}) collective-permute-start(bf16[16,128,384]{2,1,0:T(8,128)(2,1)} %get-tuple-element.68), channel_id=1, source_target_pairs={{0,1},{1,0},{2,3},{3,2},{4,5},{5,4},{6,7},{7,6},{8,9},{9,8},{10,11... | collective-permute-start | bytes 4718600 | tf_op jit(solution)/shard_map/ppermute | solution.py:570
  252.5 50.9 %collective-permute-start.33 = (bf16[16,48,1152]{2,1,0:T(8,128)(2,1)}, bf16[16,48,1152]{2,1,0:T(8,128)(2,1)}, u32[]{:S(2)}, u32[]{:S(2)}) collective-permute-start(bf16[16,48,1152]{2,1,0:T(8,128)(2,1)} %get-tuple-element.58), channel_id=1, source_target_pairs={{0,1},{1,0},{2,3},{3,2},{4,5},{5,4},{6,7},{7,6},{8,9},{9,8},{10,11... | collective-permute-start | bytes 5308424 | tf_op jit(solution)/shard_map/ppermute | solution.py:570
  253.3 19.4 %collective-permute-start.44 = (bf16[2,48,384]{2,1,0:T(8,128)(2,1)}, bf16[2,48,384]{2,1,0:T(8,128)(2,1)S(1)}, u32[]{:S(2)}, u32[]{:S(2)}) collective-permute-start(bf16[2,48,384]{2,1,0:T(8,128)(2,1)} %get-tuple-element.93), channel_id=1, source_target_pairs={{0,2},{1,3},{2,0},{3,1},{4,6},{5,7},{6,4},{7,5},{8,10},{9,11},{10,... | collective-permute-start | bytes 221192 | tf_op jit(solution)/shard_map/ppermute | solution.py:570
  253.8 18.9 %collective-permute-start.47 = (bf16[2,48,384]{2,1,0:T(8,128)(2,1)S(1)}, bf16[2,48,384]{2,1,0:T(8,128)(2,1)S(1)}, u32[]{:S(2)}, u32[]{:S(2)}) collective-permute-start(bf16[2,48,384]{2,1,0:T(8,128)(2,1)S(1)} %get-tuple-element.94), channel_id=1, source_target_pairs={{0,16},{16,0},{1,17},{17,1},{2,18},{18,2},{3,19},{19,3},{4,20},{20... | collective-permute-start | bytes 221192 | tf_op jit(solution)/shard_map/ppermute | solution.py:570
  272.6 68.0 %collective-permute-start.51 = (bf16[16,48,2048]{2,1,0:T(8,128)(2,1)}, bf16[16,48,2048]{2,1,0:T(8,128)(2,1)S(1)}, u32[]{:S(2)}, u32[]{:S(2)}) collective-permute-start(bf16[16,48,2048]{2,1,0:T(8,128)(2,1)} %get-tuple-element.66), channel_id=1, source_target_pairs={{0,1},{1,0},{2,3},{3,2},{4,5},{5,4},{6,7},{7,6},{8,9},{9,8},{10,11... | collective-permute-start | bytes 9437192 | tf_op jit(solution)/shard_map/ppermute | solution.py:570
  276.1 22.4 %collective-permute-start.45 = (bf16[48,384]{1,0:T(8,128)(2,1)S(1)}, bf16[48,384]{1,0:T(8,128)(2,1)}, u32[]{:S(2)}, u32[]{:S(2)}) collective-permute-start(bf16[48,384]{1,0:T(8,128)(2,1)S(1)} %get-tuple-element.92), channel_id=1, source_target_pairs={{0,4},{1,5},{2,6},{3,7},{4,0},{5,1},{6,2},{7,3},{8,12},{9,13},{10,... | collective-permute-start | bytes 110600 | tf_op jit(solution)/shard_map/ppermute | solution.py:570
  279.7 21.3 %collective-permute-start.61 = (bf16[4,128,384]{2,1,0:T(8,128)(2,1)S(1)}, bf16[4,128,384]{2,1,0:T(8,128)(2,1)S(1)}, u32[]{:S(2)}, u32[]{:S(2)}) collective-permute-start(bf16[4,128,384]{2,1,0:T(8,128)(2,1)S(1)} %get-tuple-element.88), channel_id=1, source_target_pairs={{0,16},{16,0},{1,17},{17,1},{2,18},{18,2},{3,19},{19,3},{4,20},{20... | collective-permute-start | bytes 1179656 | tf_op jit(solution)/shard_map/ppermute | solution.py:570
  280.3 20.7 %collective-permute-start.64 = (bf16[4,128,384]{2,1,0:T(8,128)(2,1)S(1)}, bf16[4,128,384]{2,1,0:T(8,128)(2,1)S(1)}, u32[]{:S(2)}, u32[]{:S(2)}) collective-permute-start(bf16[4,128,384]{2,1,0:T(8,128)(2,1)S(1)} %get-tuple-element.89), channel_id=1, source_target_pairs={{0,2},{1,3},{2,0},{3,1},{4,6},{5,7},{6,4},{7,5},{8,10},{9,11},{10,... | collective-permute-start | bytes 1179656 | tf_op jit(solution)/shard_map/ppermute | solution.py:570
  304.8 19.9 %collective-permute-start.34 = (bf16[4,48,1152]{2,1,0:T(8,128)(2,1)S(1)}, bf16[4,48,1152]{2,1,0:T(8,128)(2,1)S(1)}, u32[]{:S(2)}, u32[]{:S(2)}) collective-permute-start(bf16[4,48,1152]{2,1,0:T(8,128)(2,1)S(1)} %get-tuple-element.83), channel_id=1, source_target_pairs={{0,16},{16,0},{1,17},{17,1},{2,18},{18,2},{3,19},{19,3},{4,20},{20... | collective-permute-start | bytes 1327112 | tf_op jit(solution)/shard_map/ppermute | solution.py:570
  (101 other events, 1450.8 us)

commit v2 on v1

v2 whole, which is shorter than its diff:
```python
import functools

import jax
import jax.numpy as jnp
from jax import lax
from jax.experimental import pallas as pl
from jax.experimental.pallas import tpu as pltpu
from jax.sharding import PartitionSpec as P

H = 12
HD = 64
BLOCK = 256
MAX_DOC = 512

epsilon = 1e-06
rope_base = 10000.0
far = 1e30

bf16 = jnp.bfloat16
f32 = jnp.float32
MIB = 1 << 20
NN = (((1,), (0,)), ((), ()))
NT = (((1,), (1,)), ((), ()))
TN = (((0,), (0,)), ((), ()))


def dot(left, right, dims=NN):
    return lax.dot_general(left, right, dims, preferred_element_type=f32)


def params():
    return pltpu.CompilerParams(vmem_limit_bytes=60 * MIB)


HINT = 1.0


def cost(flops, nbytes, trans=0):
    return pl.CostEstimate(
        flops=int(HINT * flops), bytes_accessed=int(HINT * nbytes), transcendentals=int(HINT * trans)
    )


ANY = pl.BlockSpec(memory_space=pl.ANY)


def weight_copies(pieces, tab_ref, dest, sem, start, width):
    copies = []
    index = 0
    for piece in pieces:
        count, rows = piece.shape[0], piece.shape[1]
        for b in range(count):
            row = pl.multiple_of(tab_ref[0, index] * rows, 16)
            col = pl.multiple_of(tab_ref[1, index] * width, 128)
            copies.append(
                pltpu.make_async_copy(
                    piece.at[b, :, pl.ds(start, width)],
                    dest.at[pl.ds(row, rows), pl.ds(col, width)],
                    sem.at[index],
                )
            )
            index += 1
    return copies


def start_all(copies):
    for copy in copies:
        copy.start()


def wait_all(copies):
    for copy in copies:
        copy.wait()


def load_weight(pieces, tab_ref, dest, sem):
    copies = weight_copies(pieces, tab_ref, dest, sem, 0, pieces[0].shape[2])
    start_all(copies)
    wait_all(copies)


GROUPS = 3


def in_order(refs, half=0, halves=1):
    return jnp.concatenate(
        [
            ref[:, j * 128 : (j + 1) * 128]
            for j in range(2)
            if j * halves // 2 == half
            for ref in refs
        ],
        1,
    )


def pack_kernel(half_ref, *refs, folded):
    *sources, gain_ref, out_ref = refs
    offset = 0
    for source, scaled in zip(sources, folded):
        width = source.shape[1]
        value = source[...]
        if scaled:
            value = (value.astype(f32) * gain_ref[...]).astype(bf16)
        out_ref[:, offset : offset + width] = value
        offset += width


def pack(half, arrays, gain, halves):
    folded = [scaled for _, scaled in arrays]
    arrays = [array for array, _ in arrays]
    rows = arrays[0].shape[0]
    columns = sum(array.shape[1] for array in arrays) // halves
    return pl.pallas_call(
        functools.partial(pack_kernel, folded=folded),
        grid_spec=pltpu.PrefetchScalarGridSpec(
            num_scalar_prefetch=1,
            grid=(1,),
            in_specs=[
                pl.BlockSpec((rows, array.shape[1] // halves), lambda i, h: (0, h[0])) for array in arrays
            ]
            + [pl.BlockSpec((rows, 1), lambda i, h: (0, 0))],
            out_specs=pl.BlockSpec((rows, columns), lambda i, h: (0, 0)),
        ),
        out_shape=jax.ShapeDtypeStruct((rows, columns), bf16),
        compiler_params=params(),
        cost_estimate=cost(rows * columns, 4 * rows * columns),
        name="pack",
    )(half.reshape(1), *arrays, gain)


def rope_tables(length):
    position = jnp.arange(length, dtype=f32)
    exponent = jnp.arange(HD // 2, dtype=f32) * (2.0 / HD)
    angles = position[:, None] * jnp.power(rope_base, -exponent)[None, :]
    cosine, sine = jnp.cos(angles), jnp.sin(angles)
    return jnp.concatenate([cosine] * 4, 1), jnp.concatenate([-sine, sine, -sine, sine], 1)


def swap_halves(tensor):
    lane = lax.broadcasted_iota(jnp.int32, tensor.shape, 1)
    return jnp.where(
        (lane & (HD // 2)) == 0, pltpu.roll(tensor, 128 - HD // 2, 1), pltpu.roll(tensor, HD // 2, 1)
    )


def project_kernel(tab_ref, *refs, n_pieces, halves):
    pieces, (x_ref, cos_ref, sin_ref) = refs[:n_pieces], refs[n_pieces : n_pieces + 3]
    n_ref, q_ref, k_ref, v_ref, weight, sem = refs[n_pieces + 3 :]

    @pl.when(pl.program_id(0) == 0)
    def _():
        load_weight(pieces, tab_ref, weight, sem)

    x = x_ref[...].astype(f32)
    normed = (x * lax.rsqrt(jnp.mean(x * x, -1, keepdims=True) + epsilon)).astype(bf16)
    n_ref[...] = normed
    width = x_ref.shape[1] // halves
    cosine, sine = cos_ref[...], sin_ref[...]
    for half in range(halves):
        result = dot(normed, weight[:, 3 * half * width : 3 * (half + 1) * width])
        for part, out, scale in ((0, q_ref, HD**-0.5), (1, k_ref, 1.0)):
            for c in range(0, width, 128):
                piece = result[:, part * width + c : part * width + c + 128]
                turned = piece * cosine + swap_halves(piece) * sine
                out[:, half * width + c : half * width + c + 128] = (
                    turned.astype(bf16) * jnp.asarray(scale, bf16)
                )
        v_ref[:, half * width : (half + 1) * width] = result[:, 2 * width :].astype(bf16)


def project(tab, pieces, x, cosine, sine, halves):
    length, width = x.shape
    rows = BLOCK
    n = len(pieces)
    blocks = sum(p.shape[0] for p in pieces)
    block = pl.BlockSpec((rows, width), lambda i, t: (i, 0))
    table = pl.BlockSpec((rows, 128), lambda i, t: (i, 0))
    shape = jax.ShapeDtypeStruct((length, width), bf16)
    return pl.pallas_call(
        functools.partial(project_kernel, n_pieces=n, halves=halves),
        grid_spec=pltpu.PrefetchScalarGridSpec(
            num_scalar_prefetch=1,
            grid=(length // rows,),
            in_specs=[ANY] * n + [block, table, table],
            out_specs=[block] * 4,
            scratch_shapes=[
                pltpu.VMEM((width, 3 * width), bf16),
                pltpu.SemaphoreType.DMA((blocks,)),
            ],
        ),
        out_shape=[shape] * 4,
        compiler_params=params(),
        cost_estimate=cost(6 * length * width * width, 16 * length * width),
        name="project",
    )(tab, *pieces, x, cosine, sine)


def key_range(block):
    low = max(0, (block * BLOCK - (MAX_DOC - 1)) // BLOCK) if block * BLOCK > MAX_DOC - 1 else 0
    return low * BLOCK, (block + 1) * BLOCK


def marks(docs):
    lane = jnp.arange(128, dtype=jnp.int32)[None, :] % HD
    used = lane < 4
    same = docs == lane
    return (
        jnp.where(used & ~same, -far, 0.0).astype(bf16),
        jnp.where(used & same, 1.0, 0.0).astype(bf16),
    )


def pipeline(items, first, second, third):
    ahead = 2
    made = [first(item) for item in items[:ahead]]
    pending = None
    for i, item in enumerate(items):
        if i + ahead < len(items):
            made.append(first(items[i + ahead]))
        middle = second(item, made[i])
        made[i] = None
        if pending is not None:
            third(*pending)
        pending = (item, middle)
    third(*pending)


def attend_kernel(q_ref, k_ref, v_ref, qm_ref, km_ref, mixed_ref, inv_ref, e_ref):
    length = q_ref.shape[0]
    lane = lax.broadcasted_iota(jnp.int32, (length, 128), 1)
    front = lax.broadcasted_iota(jnp.int32, (BLOCK, 128), 1) < HD
    q, k, v = q_ref[...], k_ref[...], v_ref[...]
    ones = jnp.ones((length, 128), bf16)
    operands = []
    for head in range(2):
        own = (lane < HD) if head == 0 else (lane >= HD)
        operands.append(
            (jnp.where(own, q, qm_ref[...]), jnp.where(own, k, km_ref[...]), jnp.where(own, v, ones))
        )
    outs = {}

    def scores(item):
        block, head = item
        low, high = key_range(block)
        qa, ka, _ = operands[head]
        return dot(ka[low:high], qa[block * BLOCK : (block + 1) * BLOCK], NT)

    def softmax(item, values):
        block, head = item
        low, high = key_range(block)
        exps = jnp.exp(values - jnp.max(values, 0, keepdims=True)).astype(bf16)
        for kb in range(low // BLOCK, high // BLOCK):
            e_ref[head, kb, :, (block - kb) * BLOCK : (block - kb + 1) * BLOCK] = exps[
                kb * BLOCK - low : (kb + 1) * BLOCK - low
            ]
        return exps

    def mix(item, exps):
        block, head = item
        low, high = key_range(block)
        outs[head] = dot(exps, operands[head][2][low:high], TN)
        if head == 1:
            rows = slice(block * BLOCK, (block + 1) * BLOCK)
            value = jnp.where(front, outs[0], outs[1])
            total = jnp.where(front, outs[1], outs[0])
            inverse = pltpu.roll(1.0 / total, HD, 1)
            mixed_ref[rows, :] = (value * inverse).astype(bf16)
            inv_ref[rows, :] = inverse

    items = [(block, head) for block in range(length // BLOCK) for head in range(2)]
    pipeline(items, scores, softmax, mix)


def span(length):
    return min(length, MAX_DOC + BLOCK)


def attend(q, k, v, q_marks, k_marks, first, jump):
    length = q.shape[0]
    blocks = length // BLOCK
    column = pl.BlockSpec((length, 128), lambda i: (0, first + jump * i))
    fixed = pl.BlockSpec((length, 128), lambda i: (0, 0))
    part = pl.BlockSpec((length, 128), lambda i: (0, i))
    return pl.pallas_call(
        attend_kernel,
        grid=(2,),
        in_specs=[column, column, column, fixed, fixed],
        out_specs=[part, part, pl.BlockSpec((2, blocks, BLOCK, span(length)), lambda i: (i, 0, 0, 0))],
        out_shape=[
            jax.ShapeDtypeStruct((length, 256), bf16),
            jax.ShapeDtypeStruct((length, 256), f32),
            jax.ShapeDtypeStruct((4, blocks, BLOCK, span(length)), bf16),
        ],
        compiler_params=params(),
        cost_estimate=cost(10 * length * length * 256, 30 * length * 256, 4 * length * length),
        name="attend",
    )(q, k, v, q_marks, k_marks)


def attend_back_kernel(
    q_ref, k_ref, v_ref, mixed_ref, inv_ref, e_ref, grad_ref, cos_ref, sin_ref,
    dq_ref, dk_ref, dv_ref, ds_ref,
):
    length = q_ref.shape[0]
    count = length // BLOCK
    lane = lax.broadcasted_iota(jnp.int32, (length, 128), 1)
    q, k, v = q_ref[...], k_ref[...], v_ref[...]
    zero = jnp.zeros((length, 128), bf16)
    scaled = grad_ref[...].astype(f32) * inv_ref[...]
    inner = scaled * mixed_ref[...].astype(f32)
    operands = []
    for head in range(2):
        own = (lane < HD) if head == 0 else (lane >= HD)
        first = HD if head == 0 else 0
        spare = (lane == first) | (lane == first + 1)
        minus = jnp.where(spare, -1.0, 0.0).astype(bf16)
        delta = jnp.sum(jnp.where(own, inner, 0.0), 1, keepdims=True)
        upper = delta.astype(bf16).astype(f32)
        masked = jnp.where(own, scaled, 0.0)
        joined = jnp.where(lane == first, upper, masked)
        joined = jnp.where(lane == first + 1, delta - upper, joined).astype(bf16)
        operands.append(
            (
                jnp.where(own, q, zero),
                jnp.where(own, k, zero),
                jnp.where(own, v, minus),
                masked.astype(bf16),
                joined,
            )
        )
    sums = {}

    def turn_back(value, rows):
        return (value * cos_ref[rows, :] - swap_halves(value) * sin_ref[rows, :]).astype(bf16)

    def slopes(item):
        block, head = item
        low, high = key_range(block)
        return dot(
            operands[head][2][low:high], operands[head][4][block * BLOCK : (block + 1) * BLOCK], NT
        )

    def products(item, slope):
        block, head = item
        low, high = key_range(block)
        parts = []
        for kb in range(low // BLOCK, high // BLOCK):
            cols = slice((block - kb) * BLOCK, (block - kb + 1) * BLOCK)
            part = e_ref[head, kb, :, cols].astype(f32) * slope[kb * BLOCK - low : (kb + 1) * BLOCK - low]
            part = part.astype(bf16)
            ds_ref[head, kb, :, cols] = part
            parts.append(part)
        return jnp.concatenate(parts, 0)

    def finish(item, ds):
        block, head = item
        low, high = key_range(block)
        rows = slice(block * BLOCK, (block + 1) * BLOCK)
        part = dot(ds, operands[head][1][low:high], TN)
        if head == 0:
            sums["q"] = part
        else:
            dq_ref[rows, :] = turn_back((sums["q"] + part) * (HD**-0.5), rows)
        for kb in range(count):
            if max(b for b in range(count) if key_range(b)[0] <= kb * BLOCK) != block:
                continue
            width = (block - kb + 1) * BLOCK
            seen = slice(kb * BLOCK, kb * BLOCK + width)
            keys = slice(kb * BLOCK, (kb + 1) * BLOCK)
            dv = dot(e_ref[head, kb, :, 0:width], operands[head][3][seen])
            dk = dot(ds_ref[head, kb, :, 0:width], operands[head][0][seen])
            if head == 0:
                sums[kb] = (dv, dk)
            else:
                dv_ref[keys, :] = (sums[kb][0] + dv).astype(bf16)
                dk_ref[keys, :] = turn_back(sums[kb][1] + dk, keys)

    items = [(block, head) for block in range(count) for head in range(2)]
    pipeline(items, slopes, products, finish)


def attend_back(q, k, v, mixed, inv, exps, grad, cosine, sine, first, jump):
    length = q.shape[0]
    column = pl.BlockSpec((length, 128), lambda i: (0, first + jump * i))
    part = pl.BlockSpec((length, 128), lambda i: (0, i))
    fixed = pl.BlockSpec((length, 128), lambda i: (0, 0))
    shape = jax.ShapeDtypeStruct((length, 256), bf16)
    return pl.pallas_call(
        attend_back_kernel,
        grid=(2,),
        in_specs=[column] * 3
        + [part, part, pl.BlockSpec((2,) + exps.shape[1:], lambda i: (i, 0, 0, 0)), column, fixed, fixed],
        out_specs=[part] * 3,
        out_shape=[shape] * 3,
        scratch_shapes=[pltpu.VMEM((2,) + exps.shape[1:], bf16)],
        compiler_params=params(),
        cost_estimate=cost(20 * length * length * 256, 36 * length * 256),
        name="attend_back",
    )(q, k, v, mixed, inv, exps, grad, cosine, sine)


def ffn_kernel(tab_ref, *refs, n_pieces, halves):
    pieces, x_ref, mixed_refs = refs[:n_pieces], refs[n_pieces], refs[n_pieces + 1 : n_pieces + 4]
    middle_ref, normed_ref, hidden_ref, slope_g_ref, slope_u_ref, w_out, w_in, sem = refs[n_pieces + 4 :]
    width = x_ref.shape[1] // halves
    inner = hidden_ref.shape[1] // halves
    early = weight_copies(pieces, tab_ref, w_out, sem.at[0], 0, width)
    late = weight_copies(pieces, tab_ref, w_in, sem.at[1], width, 2 * inner)

    @pl.when(pl.program_id(0) == 0)
    def _():
        start_all(early)
        start_all(late)
        wait_all(early)

    middle = x_ref[...].astype(f32) + dot(in_order(mixed_refs), w_out[...])
    middle_ref[...] = middle
    normed = (middle * lax.rsqrt(jnp.mean(middle * middle, -1, keepdims=True) + epsilon)).astype(bf16)
    normed_ref[...] = normed

    @pl.when(pl.program_id(0) == 0)
    def _():
        wait_all(late)

    step = min(512, inner)
    for h in range(halves):
        for c in range(0, inner, step):
            first = 2 * h * inner + c
            gate = dot(normed, w_in[:, first : first + step])
            up = dot(normed, w_in[:, first + inner : first + inner + step])
            sigmoid = jax.nn.sigmoid(gate)
            silu = gate * sigmoid
            cols = slice(h * inner + c, h * inner + c + step)
            hidden_ref[:, cols] = (silu * up).astype(bf16)
            slope_u_ref[:, cols] = silu.astype(bf16)
            slope_g_ref[:, cols] = (up * sigmoid * (1.0 + gate * (1.0 - sigmoid))).astype(bf16)


def ffn(tab, pieces, x, mixed, inner, halves):
    length, width = x.shape
    rows = BLOCK
    n = len(pieces)
    blocks = sum(p.shape[0] for p in pieces)
    narrow = pl.BlockSpec((rows, width), lambda i, t: (i, 0))
    third = pl.BlockSpec((rows, width // 3), lambda i, t: (i, 0))
    wide = pl.BlockSpec((rows, inner), lambda i, t: (i, 0))
    wide_shape = jax.ShapeDtypeStruct((length, inner), bf16)
    return pl.pallas_call(
        functools.partial(ffn_kernel, n_pieces=n, halves=halves),
        grid_spec=pltpu.PrefetchScalarGridSpec(
            num_scalar_prefetch=1,
            grid=(length // rows,),
            in_specs=[ANY] * n + [narrow] + [third] * 3,
            out_specs=[narrow, narrow, wide, wide, wide],
            scratch_shapes=[
                pltpu.VMEM((width, width), bf16),
                pltpu.VMEM((width, 2 * inner), bf16),
                pltpu.SemaphoreType.DMA((2, blocks)),
            ],
        ),
        out_shape=[
            jax.ShapeDtypeStruct((length, width), f32),
            jax.ShapeDtypeStruct((length, width), bf16),
            wide_shape,
            wide_shape,
            wide_shape,
        ],
        compiler_params=params(),
        cost_estimate=cost(2 * length * width * (width + 2 * inner), 8 * width * inner + 8 * length * inner),
        name="ffn",
    )(tab, *pieces, x, *mixed)


def hidden_back_kernel(tab_ref, *refs, n_pieces, halves):
    pieces = refs[:n_pieces]
    middle_ref, hidden_ref, slope_g_ref, slope_u_ref, cot_ref = refs[n_pieces : n_pieces + 5]
    output_ref, gg_ref, gu_ref, weight, sem = refs[n_pieces + 5 :]

    @pl.when(pl.program_id(0) == 0)
    def _():
        load_weight(pieces, tab_ref, weight, sem)

    inner = hidden_ref.shape[1]
    step = min(512, inner)
    cot = cot_ref[...]
    for c in range(0, inner, step):
        cols = slice(c, c + step)
        grad_hidden = dot(cot, weight[cols, :], NT)
        gg_ref[:, cols] = (grad_hidden * slope_g_ref[:, cols].astype(f32)).astype(bf16)
        gu_ref[:, cols] = (grad_hidden * slope_u_ref[:, cols].astype(f32)).astype(bf16)
    output_ref[...] = (middle_ref[...] + dot(hidden_ref[...], weight[...])).astype(bf16)


def hidden_back(tab, pieces, middle, hidden, slope_g, slope_u, cot, halves):
    length, width = middle.shape
    inner = hidden.shape[1]
    rows = BLOCK
    n = len(pieces)
    narrow = pl.BlockSpec((rows, width), lambda i, t: (i, 0))
    wide = pl.BlockSpec((rows, inner), lambda i, t: (i, 0))
    wide_low = jax.ShapeDtypeStruct((length, inner), bf16)
    return pl.pallas_call(
        functools.partial(hidden_back_kernel, n_pieces=n, halves=halves),
        grid_spec=pltpu.PrefetchScalarGridSpec(
            num_scalar_prefetch=1,
            grid=(length // rows,),
            in_specs=[ANY] * n + [narrow, wide, wide, wide, narrow],
            out_specs=[narrow, wide, wide],
            scratch_shapes=[
                pltpu.VMEM((inner, width), bf16),
                pltpu.SemaphoreType.DMA((sum(p.shape[0] for p in pieces),)),
            ],
        ),
        out_shape=[jax.ShapeDtypeStruct((length, width), bf16), wide_low, wide_low],
        compiler_params=params(),
        cost_estimate=cost(4 * length * width * inner, 2 * width * inner + 12 * length * inner),
        name="hidden_back",
    )(tab, *pieces, middle, hidden, slope_g, slope_u, cot)


def middle_back_kernel(tab_ref, *refs, n_pieces, halves):
    pieces = refs[:n_pieces]
    middle_ref, gg_ref, gu_ref, cot_ref = refs[n_pieces : n_pieces + 4]
    grad_middle_ref, attn_grad_ref, grad_mixed_ref, w_out, w_in, sem = refs[n_pieces + 4 :]
    width = cot_ref.shape[1] // halves
    inner = gg_ref.shape[1] // halves
    early = weight_copies(pieces, tab_ref, w_in, sem.at[0], width, 2 * inner)
    late = weight_copies(pieces, tab_ref, w_out, sem.at[1], 0, width)

    @pl.when(pl.program_id(0) == 0)
    def _():
        start_all(early)
        start_all(late)
        wait_all(early)
        wait_all(late)

    middle = middle_ref[...]
    both = [
        ref[:, h * inner : (h + 1) * inner] for h in range(halves) for ref in (gg_ref, gu_ref)
    ]
    grad = dot(jnp.concatenate(both, 1), w_in[...], NT)
    inverse = lax.rsqrt(jnp.mean(middle * middle, -1, keepdims=True) + epsilon)
    normed = middle * inverse
    grad_middle = cot_ref[...].astype(f32) + inverse * (
        grad - normed * jnp.mean(grad * normed, -1, keepdims=True)
    )
    grad_middle_ref[...] = grad_middle
    low = grad_middle.astype(bf16)
    attn_grad_ref[...] = low
    grad_mixed_ref[...] = dot(low, w_out[...], NT).astype(bf16)


def middle_back(tab, pieces, middle, gg, gu, cot, halves):
    length, width = middle.shape
    inner = gg.shape[1]
    rows = BLOCK
    n = len(pieces)
    narrow = pl.BlockSpec((rows, width), lambda i, t: (i, 0))
    wide = pl.BlockSpec((rows, inner), lambda i, t: (i, 0))
    low = jax.ShapeDtypeStruct((length, width), bf16)
    return pl.pallas_call(
        functools.partial(middle_back_kernel, n_pieces=n, halves=halves),
        grid_spec=pltpu.PrefetchScalarGridSpec(
            num_scalar_prefetch=1,
            grid=(length // rows,),
            in_specs=[ANY] * n + [narrow, wide, wide, narrow],
            out_specs=[narrow] * 3,
            scratch_shapes=[
                pltpu.VMEM((width, width), bf16),
                pltpu.VMEM((width, 2 * inner), bf16),
                pltpu.SemaphoreType.DMA((2, sum(p.shape[0] for p in pieces))),
            ],
        ),
        out_shape=[jax.ShapeDtypeStruct((length, width), f32), low, low],
        compiler_params=params(),
        cost_estimate=cost(
            2 * length * width * (width + 2 * inner), 4 * width * inner + 4 * length * inner
        ),
        name="middle_back",
    )(tab, *pieces, middle, gg, gu, cot)


def input_kernel(tab_ref, *refs, n_pieces, halves):
    pieces = refs[:n_pieces]
    x_ref, grad_middle_ref = refs[n_pieces : n_pieces + 2]
    parts = refs[n_pieces + 2 : n_pieces + 2 + 3 * GROUPS]
    out_ref, weight, sem = refs[n_pieces + 2 + 3 * GROUPS :]

    @pl.when(pl.program_id(0) == 0)
    def _():
        load_weight(pieces, tab_ref, weight, sem)

    left = [
        in_order(parts[part * GROUPS : (part + 1) * GROUPS], h, halves)
        for h in range(halves)
        for part in range(3)
    ]
    grad = dot(jnp.concatenate(left, 1), weight[...], NT)
    x = x_ref[...].astype(f32)
    inverse = lax.rsqrt(jnp.mean(x * x, -1, keepdims=True) + epsilon)
    normed = x * inverse
    out_ref[...] = grad_middle_ref[...] + inverse * (
        grad - normed * jnp.mean(grad * normed, -1, keepdims=True)
    )


def input_grad(tab, pieces, x, grad_middle, parts, halves):
    length, width = x.shape
    rows = BLOCK
    n = len(pieces)
    blocks = sum(p.shape[0] for p in pieces)
    block = pl.BlockSpec((rows, width), lambda i, t: (i, 0))
    third = pl.BlockSpec((rows, width // GROUPS), lambda i, t: (i, 0))
    return pl.pallas_call(
        functools.partial(input_kernel, n_pieces=n, halves=halves),
        grid_spec=pltpu.PrefetchScalarGridSpec(
            num_scalar_prefetch=1,
            grid=(length // rows,),
            in_specs=[ANY] * n + [block] * 2 + [third] * (3 * GROUPS),
            out_specs=block,
            scratch_shapes=[
                pltpu.VMEM((width, 3 * width), bf16),
                pltpu.SemaphoreType.DMA((blocks,)),
            ],
        ),
        out_shape=jax.ShapeDtypeStruct((length, width), f32),
        compiler_params=params(),
        cost_estimate=cost(6 * length * width * width, 20 * length * width),
        name="input_grad",
    )(tab, *pieces, x, grad_middle, *parts)


def weight_kernel(tab_ref, *refs, counts, block_rows, chunks):
    n_left, n_right = sum(n for n, _ in counts), sum(n for _, n in counts)
    lefts, rights = list(refs[:n_left]), list(refs[n_left : n_left + n_right])
    keep_ref, send_ref, held, sem = refs[n_left + n_right :]
    step, steps = pl.program_id(0), pl.num_programs(0)
    slot = lax.rem(step, 2)
    half, chunk = step // chunks, lax.rem(step, chunks)
    halves = tab_ref.shape[0] * block_rows // held.shape[1]
    kept = keep_ref.shape[0]
    widths = [r.shape[1] for r in rights]
    if chunks == 1:
        widths = [sum(widths)]

    def pieces():
        for b in range(held.shape[1] // block_rows):
            offset = 0
            for i, width in enumerate(widths):
                yield b, i, offset, width
                offset += width

    def wait(which):
        for b, i, offset, width in pieces():
            pltpu.make_async_copy(
                held.at[which, pl.ds(0, block_rows), pl.ds(offset, width)],
                keep_ref.at[0, :, pl.ds(offset, width)],
                sem.at[which, b * len(widths) + i],
            ).wait()

    @pl.when(step >= 2)
    def _():
        wait(slot)

    offset = 0
    queue = list(rights)
    for n_left, n_right in counts:
        left = lefts.pop(0)[...] if n_left == 1 else in_order([lefts.pop(0) for _ in range(n_left)])
        right = jnp.concatenate([queue.pop(0)[...] for _ in range(n_right)], 1)
        held[slot, :, offset : offset + right.shape[1]] = dot(left, right, TN).astype(bf16)
        offset += right.shape[1]
    for b, i, offset, width in pieces():
        place = tab_ref[b * halves + half]
        source = held.at[slot, pl.ds(b * block_rows, block_rows), pl.ds(offset, width)]
        cols = pl.ds(pl.multiple_of(offset * chunks + chunk * width, 128), width)
        signal = sem.at[slot, b * len(widths) + i]

        @pl.when(place < kept)
        def _():
            pltpu.make_async_copy(source, keep_ref.at[place, :, cols], signal).start()

        @pl.when(place >= kept)
        def _():
            pltpu.make_async_copy(source, send_ref.at[place - kept, :, cols], signal).start()

    @pl.when(step == steps - 1)
    def _():
        wait(slot)

        @pl.when(steps > 1)
        def _():
            wait(1 - slot)


def weight_grad(moves, products, chunks, name):
    lefts = [left for group, _ in products for left in group]
    rights = [right for _, group in products for right in group]
    counts = [(len(left), len(right)) for left, right in products]
    length, rows = lefts[0].shape
    halves, blocks = moves.halves, moves.place.shape[0]
    block_rows = rows * halves // blocks
    columns = sum(r.shape[1] for r in rights) // halves
    kept = moves.kept
    sent = max(1, blocks - kept)
    steps = halves * chunks
    n_pieces = rows // block_rows * (1 if chunks == 1 else len(rights))
    return pl.pallas_call(
        functools.partial(weight_kernel, counts=counts, block_rows=block_rows, chunks=chunks),
        grid_spec=pltpu.PrefetchScalarGridSpec(
            num_scalar_prefetch=1,
            grid=(steps,),
            in_specs=[pl.BlockSpec(left.shape, lambda i, t: (0, 0)) for left in lefts]
            + [pl.BlockSpec((length, r.shape[1] // steps), lambda i, t: (0, i)) for r in rights],
            out_specs=[ANY, ANY],
            scratch_shapes=[
                pltpu.VMEM((2, rows, columns // chunks), bf16),
                pltpu.SemaphoreType.DMA((2, n_pieces)),
            ],
        ),
        out_shape=[
            jax.ShapeDtypeStruct((kept, block_rows, columns), bf16),
            jax.ShapeDtypeStruct((sent, block_rows, columns), bf16),
        ],
        compiler_params=params(),
        cost_estimate=cost(
            2 * length * rows * columns * halves,
            2 * (length * rows + length * columns * halves + rows * columns * halves),
        ),
        name=name,
    )(moves.place, *lefts, *rights)


def after(value, *others):
    return lax.optimization_barrier((value, others))[0]


def place_of(xr, yr, zr, cr):
    low = xr * 4 + yr * 2 + zr
    high = 8 + yr * 4 + xr * 2 + (zr - 2)
    return cr * 16 + jnp.where(zr < 2, low, high)


def swapped(bits, axis="shard"):
    count = lax.axis_size(axis)
    pairs = [(i, i ^ bits) for i in range(count)]
    return lambda array: lax.ppermute(array, axis, pairs)


class Direct:
    halves = 2
    kept = 16

    def __init__(self):
        self.me = lax.axis_index("shard")
        self.x = lax.axis_index("rep")
        self.core, self.y, self.x_move = swapped(1), swapped(2), swapped(1, "rep")
        self.z = [swapped(4), swapped(8), swapped(12)]
        shard = jnp.arange(16, dtype=jnp.int32)[:, None]
        half = jnp.arange(2, dtype=jnp.int32)[None, :]
        rel = shard ^ self.me
        place = place_of(half ^ self.x, (rel >> 1) & 1, rel >> 2, rel & 1)
        self.place = place.reshape(32)
        order = []
        for cr in range(2):
            for zs in ((0, 1), (2, 3)):
                for outer in range(2):
                    for inner in range(2):
                        for zr in zs:
                            xr, yr = (outer, inner) if zs[0] == 0 else (inner, outer)
                            order.append((zr * 4 + yr * 2 + cr, xr))
        rel_shard = jnp.array([o[0] for o in order], jnp.int32)
        rel_half = jnp.array([o[1] for o in order], jnp.int32)
        self.tab = jnp.stack([rel_shard ^ self.me, rel_half ^ self.x])

    def pack(self, arrays, gain):
        return pack(self.x, arrays, gain, 2)

    def along_z(self, own):
        z1, z2, z3 = (move(own) for move in self.z)
        return jnp.concatenate([own, z1], 0), jnp.concatenate([z2, z3], 0), (z1, z2, z3)

    def one_axis(self, a, b):
        ay, bx = self.y(a), self.x_move(b)
        return (a, ay), (b, bx)

    def rest(self, a, b):
        ax, by = self.x_move(a), self.y(b)
        return [a, ax, b, by]

    def with_core(self, own, *deps):
        own = [after(p, *deps) for p in own] if deps else own
        return own + [self.core(p) for p in own]

    def gather(self, blocks):
        first, second, third = (block[None] for block in blocks)
        a1, b1, z_done1 = self.along_z(first)
        a2, b2, z_done2 = self.along_z(after(second, *z_done1))
        a1, b1 = self.one_axis(a1, b1)
        a1, b1 = jnp.concatenate(a1, 0), jnp.concatenate(b1, 0)
        own1 = self.rest(a1, b1)
        w1 = self.with_core(own1)
        self.a2, self.b2 = after(a2, *own1), after(b2, *own1)
        self.third = after(third, *z_done2, *own1)
        return w1

    def stage0(self):
        self.pair2 = self.one_axis(self.a2, self.b2)
        self.z3 = self.z[0](self.third)
        return self.a2, self.b2, self.third

    def stage1(self, *deps):
        (a, ay), (b, bx) = self.pair2
        deps = (*deps, self.z3, ay, bx)
        a = jnp.concatenate([after(a, *deps), ay], 0)
        b = jnp.concatenate([after(b, *deps), bx], 0)
        a3 = jnp.concatenate([after(self.third, *deps), self.z3], 0)
        self.a3, self.b3 = a3, self.z[1](a3)
        self.own2 = self.rest(a, b)
        self.core2 = [self.core(a), None, self.core(b), None]
        return a, b, a3

    def stage2(self, *deps):
        deps = (*deps, self.b3, self.core2[0], self.core2[2])
        self.a3, self.b3 = after(self.a3, *deps), after(self.b3, *deps)
        self.pair3 = self.one_axis(self.a3, self.b3)
        return self.a3, self.b3

    def stage3(self, *deps):
        (a, ay), (b, bx) = self.pair3
        deps = (*deps, *self.own2, ay, bx)
        a = jnp.concatenate([after(a, *deps), ay], 0)
        b = jnp.concatenate([after(b, *deps), bx], 0)
        self.own3 = self.rest(a, b)
        for i in (1, 3):
            self.core2[i] = self.core(after(self.own2[i], *deps, a, b))
        self.own2 += self.core2
        return a, b

    def scatter(self, grads, direct=False):
        return Direct.Sum(self, grads, direct)

    class Sum:
        def __init__(self, moves, grads, direct):
            self.moves = moves
            self.keep, self.send = grads
            over_z = [self.over_z] if direct else [self.over_z2, self.over_z1]
            self.steps = [self.over_core, self.over_two, self.over_other, *over_z, self.over_x]
            self.start = self.steps[0]
            self.got = ()

        def step(self, *deps):
            if deps:
                self.keep = after(self.keep, *deps)
                if self.steps[0] == self.start:
                    self.send = after(self.send, *deps)
            return self.steps.pop(0)()

        def finish(self):
            while self.steps:
                self.step()
            return self.result

        @staticmethod
        def add(*terms):
            total = terms[0].astype(f32)
            for term in terms[1:]:
                total = total + term.astype(f32)
            return total.astype(bf16)

        def over_core(self):
            self.core = self.moves.core(self.send)
            self.got = (self.core,)
            return (self.send,)

        def over_two(self):
            keep, core = self.keep, self.core
            to_x, to_y = self.add(keep[4:8], core[4:8]), self.add(keep[12:16], core[12:16])
            self.ax, self.by = self.got = self.moves.x_move(to_x), self.moves.y(to_y)
            return to_x, to_y

        def over_other(self):
            keep, core, ax, by = self.keep, self.core, self.ax, self.by
            to_y = self.add(keep[2:4], core[2:4], ax[2:4])
            to_x = self.add(keep[10:12], core[10:12], by[2:4])
            self.ay, self.bx = self.got = self.moves.y(to_y), self.moves.x_move(to_x)
            return to_y, to_x

        def over_z(self):
            keep, core, ax, by, ay, bx = self.keep, self.core, self.ax, self.by, self.ay, self.bx
            sends = (
                self.add(keep[1], core[1], ax[1], ay[1]),
                self.add(keep[8], core[8], by[0], bx[0]),
                self.add(keep[9], core[9], by[1], bx[1]),
            )
            self.got = self.zs = tuple(move(send) for move, send in zip(self.moves.z, sends))
            return sends

        def over_z2(self):
            keep, core = self.keep, self.core
            send = self.add(keep[8:10], core[8:10], self.by[0:2], self.bx[0:2])
            self.z2 = self.moves.z[1](send)
            self.got = (self.z2,)
            return (send,)

        def over_z1(self):
            send = self.add(self.keep[1], self.core[1], self.ax[1], self.ay[1], self.z2[1])
            z1 = self.moves.z[0](send)
            self.zs = (self.z2[0], z1)
            self.got = (z1,)
            return (send,)

        def over_x(self):
            own = self.add(self.keep[0], self.core[0], self.ax[0], self.ay[0], *self.zs)
            other = self.moves.x_move(own)
            first = self.moves.x == 0
            self.result = [jnp.where(first, own, other), jnp.where(first, other, own)]
            self.got = (other,)
            return (own,)


class Plain:
    halves = 1
    kept = 1

    def __init__(self):
        self.place = jnp.zeros((1,), jnp.int32)
        self.tab = jnp.zeros((2, 1), jnp.int32)

    def pack(self, arrays, gain):
        return pack(jnp.int32(0), arrays, gain, 1)

    def gather(self, blocks):
        first, *others = (
            [lax.all_gather(block, "shard", axis=0, tiled=True)[None]] for block in blocks
        )
        self.own2, self.own3 = others
        return first

    def with_core(self, own, *deps):
        return own

    def stage0(self):
        return ()

    def stage1(self, *deps):
        return ()

    stage2 = stage3 = stage1

    def scatter(self, grads, direct=False):
        return Plain.Sum(grads)

    class Sum:
        got = ()

        def __init__(self, grads):
            self.grads = grads

        def step(self, *deps):
            return ()

        def finish(self):
            total = self.grads[0][0].astype(f32)
            part = lax.psum_scatter(total, "shard", scatter_dimension=0, tiled=True)
            return [lax.psum(part.astype(bf16), "rep")]


def columns(halves, start, width):
    step = width // len(halves)
    first = start // len(halves)
    return jnp.concatenate([h[:, first : first + step] for h in halves], 1).astype(f32)


def one_sequence(moves, x, docs, w1, cot, inner):
    cosine, sine = rope_tables(x.shape[0])
    q_marks, k_marks = marks(docs.reshape(-1, 1))
    halves, tab = moves.halves, moves.tab
    sends = moves.stage0()
    normed1, q, k, v = project(tab, w1, after(x, *sends), cosine, sine, halves)
    sends = moves.stage1(normed1)
    seen = []
    for g in range(GROUPS):
        seen.append(attend(q, k, v, after(q_marks, *sends), k_marks, g, GROUPS))
        sends = (seen[-1][0],)
        if g == 1:
            sends = moves.stage2(*sends)
    mixed = [s[0] for s in seen]
    sends = moves.stage3(mixed[2])
    w2 = moves.own2
    middle, normed2, hidden, slope_g, slope_u = ffn(
        tab, w2, after(x, *sends), mixed, inner, halves
    )
    w3 = moves.with_core(moves.own3, hidden)
    g3 = weight_grad(moves, [([after(hidden, *moves.own3)], [cot])], 1, "grad_down")
    sum3 = moves.scatter(g3)
    sum3.step(*g3, *w3)
    output, gg, gu = hidden_back(
        tab, w3, middle, after(hidden, *g3), slope_g, slope_u, cot, halves
    )
    sends = sum3.step(gg, *sum3.got)
    g2 = weight_grad(moves, [([after(normed2, *sends)], [gg, gu])], 2, "grad_gate_up")
    sum2 = moves.scatter(g2)
    due = (*g2, *sum3.got)
    sends = sum3.step(*due)
    sends = (*sends, *sum2.step(*due))
    grad_middle, attn_grad, grad_mixed = middle_back(
        tab, w2, after(middle, *g2, *sends), gg, gu, cot, halves
    )
    due = (attn_grad, *sum3.got, *sum2.got)
    sends = sum3.step(*due)
    sends = (*sends, *sum2.step(*due))

    def back(g, sends):
        return attend_back(q, k, v, *seen[g], after(grad_mixed, *sends), cosine, sine, g, GROUPS)

    turned0 = back(0, sends)
    sends = sum3.step(*turned0[:1], *sum3.got)
    turned1 = back(1, (*turned0[:1], *sends))
    due = (*turned1[:1], *sum2.got, *sum3.got)
    sends = sum2.step(*due)
    sends = (*sends, *sum3.step(*due))
    g1 = weight_grad(
        moves,
        [([after(normed1, *sends)], [*turned0, *turned1]), (mixed, [attn_grad])],
        1,
        "grad_qk_out",
    )
    sum1 = moves.scatter(g1)
    due = (*g1, *sum2.got, *sum3.got)
    sum1.step(*due)
    sends = sum2.step(*due)
    sends = (*sends, *sum1.step(*sends, *sum1.got))
    turned2 = back(2, (*g1, *sends))
    due = (*turned2[:1], *sum1.got, *sum2.got)
    sends = sum1.step(*due)
    sends = (*sends, *sum2.step(*due))
    g0 = weight_grad(moves, [([after(normed1, *sends)], turned2)], 1, "grad_qkv_rest")
    sum0 = moves.scatter(g0, True)
    due = (*g0, *sum1.got, *sum2.got)
    sum0.step(*due)
    sends = (*sum1.step(*due), *sum2.step(*due))
    sends = (*sends, *sum0.step(*sends, *sum0.got))
    parts = [t[part] for part in range(3) for t in (turned0, turned1, turned2)]
    grad_input = input_grad(tab, w1, after(x, *g0, *sends), grad_middle, parts, halves)
    sums = (sum0, sum1, sum2, sum3)
    due = (grad_input, *sum2.got, *sum1.got, *sum0.got)
    for one in (sum0, sum1):
        one.step(*due)
    return output, grad_input, [s.finish() for s in sums]


def per_device(
    inputs,
    doc_ids,
    attn_gain,
    w_query,
    w_key,
    w_value,
    w_out,
    ffn_gain,
    w_gate,
    w_up,
    w_down,
    cotangent,
):
    batch_size, length, width = inputs.shape
    inner = w_gate.shape[1]
    replicas, members = lax.axis_size("rep"), lax.axis_size("shard")
    moves = Direct() if (replicas, members, batch_size) == (2, 16, 1) else Plain()
    gain1 = attn_gain.astype(f32)[:, None]
    gain2 = ffn_gain.astype(f32)[:, None]

    w1 = moves.gather(
        [
            moves.pack([(w, True) for w in (w_query, w_key, w_value)], gain1),
            moves.pack([(w_out, False), (w_gate, True), (w_up, True)], gain2),
            moves.pack([(w_down, False)], jnp.ones((w_down.shape[0], 1), f32)),
        ]
    )
    outputs, grad_inputs, sums = [], [], None
    for b in range(batch_size):
        output, grad_input, own = one_sequence(
            moves, inputs[b], doc_ids[b], w1, cotangent[b], inner
        )
        outputs.append(output)
        grad_inputs.append(grad_input)
        sums = own if sums is None else jax.tree.map(jnp.add, sums, own)
    s0, s1, s2, s3 = sums
    scale = 1.0 / (batch_size * replicas * members)
    down = columns(s3, 0, width)
    gate, up = columns(s2, 0, inner), columns(s2, inner, inner)
    third = width // GROUPS
    out = columns(s1, 6 * third, width)

    def head_columns(part):
        sources = [columns(s, start * third, third) for s, start in ((s1, part), (s1, part + 3), (s0, part))]
        return jnp.concatenate([c[:, j * 128 : (j + 1) * 128] for j in range(2) for c in sources], 1)

    query, key, value = (head_columns(part) for part in range(3))

    def gain_grad(pairs):
        total = sum(jnp.sum(w.astype(f32) * g, 1) for w, g in pairs)
        return total * scale

    return (
        jnp.stack(outputs),
        jnp.stack(grad_inputs),
        gain_grad([(w_query, query), (w_key, key), (w_value, value)]),
        query * gain1 * scale,
        key * gain1 * scale,
        value * gain1 * scale,
        out * scale,
        gain_grad([(w_gate, gate), (w_up, up)]),
        gate * gain2 * scale,
        up * gain2 * scale,
        down * scale,
    )


def solution(mesh):
    row = P("shard", None)
    tokens = P(("rep", "shard"), None, None)
    return jax.shard_map(
        per_device,
        mesh=mesh,
        in_specs=(
            tokens, P(("rep", "shard"), None), P("shard"), row, row, row, row, P("shard"), row, row, row, tokens,
        ),
        out_specs=(tokens, tokens, P("shard"), row, row, row, row, P("shard"), row, row, row),
        check_vma=False,
    )
```

time: 395 us -> 328 us (0.83)
  waiting for transfers between devices: 102 us -> 36.9 us
  other arithmetic: 28.3 us -> 37.3 us
  local copies, waits for them, and re-layouts: 19.1 us -> 10.5 us
  starting transfers between devices: 67.4 us -> 61.9 us
  Pallas kernels: 169 us -> 174 us
    ppermute x69 -> x65, waiting for transfers between devices: 102 us -> 36.9 us  [swapped(): return lambda array: lax.ppermute(array, axis, pairs)]
    pallas_call x7 -> x15, Pallas kernels: 120 us -> 134 us  [the longest x4 37.5 us: weight_grad(): pl.pallas_call(functools.partial(weight_kernel, counts=counts, block_rows...]
    unnamed x134 -> x116, local copies, waits for them, and re-layouts: 18.1 us -> 6.79 us
    convert_element_type x19 -> x27, other arithmetic: 13.9 us -> 24.2 us  [the longest x18 24.2 us: add(): return total.astype(bf16)]
    ppermute x69 -> x65, starting transfers between devices: 67.4 us -> 61.9 us  [swapped(): return lambda array: lax.ppermute(array, axis, pairs)]
    pallas_call x1, Pallas kernels: 23.4 us -> 18.1 us  [ffn(): pl.pallas_call(functools.partial(ffn_kernel, n_pieces=n, halves=halves),...]
  transfers between devices with their start and end apart: 69 -> 65, of which waited for: 23 -> 15; matrix products, arithmetic and copies ran while one was open for 7% -> 9% of each run, Pallas kernels for 34% -> 53%
where the time goes in v2:
time: 328 us; the launch traced here: 323 us
  Pallas kernels  174 us (53%)
  starting transfers between devices  61.9 us (19%)
  other arithmetic  37.3 us (11%)
  waiting for transfers between devices  36.9 us (11%)
  local copies, waits for them, and re-layouts  10.5 us (3%)
    ppermute x65, starting transfers between devices, swapped(): return lambda array: lax.ppermute(array, axis, pairs)  61.9 us
    pallas_call x4, Pallas kernels, weight_grad(): pl.pallas_call(functools.partial(weight_kernel, counts=counts, block_rows...  37.5 us
    ppermute x65, waiting for transfers between devices, swapped(): return lambda array: lax.ppermute(array, axis, pairs)  36.9 us
    pallas_call x3, Pallas kernels, attend_back(): pl.pallas_call(attend_back_kernel, grid=(2,), in_specs=[column] * 3 + [pa...  31.8 us
    pallas_call x3, Pallas kernels, attend(): pl.pallas_call(attend_kernel, grid=(2,), in_specs=[column, column, column...  24.4 us
    convert_element_type x18, other arithmetic, add(): return total.astype(bf16)  24.2 us
    pallas_call x1, Pallas kernels, middle_back(): pl.pallas_call(functools.partial(middle_back_kernel, n_pieces=n, halves=h...  19.9 us
    pallas_call x1, Pallas kernels, ffn(): pl.pallas_call(functools.partial(ffn_kernel, n_pieces=n, halves=halves),...  18.1 us
  transfers between devices with their start and end apart: 65, of which 15 were waited for; matrix products, arithmetic and copies ran while one was open for 9% of the time, Pallas kernels for 53%

profile of v2, /device:TPU:0, one launch (start us, length us, event | category | flops | bytes accessed | tf_op | source)
XLA Modules:
  0.0 322.9 jit_solution(3362203383087105893)
XLA Ops:
  3.6 5.0 %collective-permute-start.2 = (bf16[1,48,1152]{2,1,0:T(8,128)(2,1)}, bf16[1,48,1152]{2,1,0:T(8,128)(2,1)S(1)}, u32[]{:S(2)}, u32[]{:S(2)}) collective-permute-start(bf16[1,48,1152]{2,1,0:T(8,128)(2,1)} %bitcast.53), channel_id=1, source_target_pairs={{0,12},{1,13},{2,14},{3,15},{4,8},{5,9},{6,10},{7,11},{8,4},{9,5},... | collective-permute-start | bytes 331784 | tf_op jit(solution)/shard_map/ppermute | solution.py:747
  10.6 2.0 fusion.9
  21.8 2.9 collective-permute-done.8
  27.9 2.7 collective-permute-start.5
  30.7 6.8 %collective-permute-done.5 = bf16[1,48,2432]{2,1,0:T(8,128)(2,1)S(1)} collective-permute-done((bf16[1,48,2432]{2,1,0:T(8,128)(2,1)S(1)}, bf16[1,48,2432]{2,1,0:T(8,128)(2,1)S(1)}, u32[]{:S(2)}, u32[]{:S(2)}) %collective-permute-start.5) | collective-permute-done | bytes 233504 | tf_op jit(solution)/shard_map/ppermute | solution.py:747
  38.1 10.2 %collective-permute-done.4 = bf16[1,48,2432]{2,1,0:T(8,128)(2,1)S(1)} collective-permute-done((bf16[1,48,2432]{2,1,0:T(8,128)(2,1)S(1)}, bf16[1,48,2432]{2,1,0:T(8,128)(2,1)S(1)}, u32[]{:S(2)}, u32[]{:S(2)}) %collective-permute-start.4) | collective-permute-done | bytes 233504 | tf_op jit(solution)/shard_map/ppermute | solution.py:747
  54.5 10.8 %project.1 = (bf16[1024,768]{1,0:T(8,128)(2,1)}, bf16[1024,768]{1,0:T(8,128)(2,1)}, bf16[1024,768]{1,0:T(8,128)(2,1)}, bf16[1024,768]{1,0:T(8,128)(2,1)}) custom-call(s32[2,32]{1,0:T(2,128)} %pad_add_fusion.tab_ref, bf16[4,48,1152]{2,1,0:T(8,128)(2,1)} %copy-done.1, bf16[4,48,1152]{2,1,0:T(8,128)(2,1)} %copy-done.13, bf16[4,48,1152]{2,1,0:T(8,128)(2,1)} %copy-done.8, ...), custom_call_target="tpu_custom_call" | custom-call | flops 3623878656 | bytes 12582912 | tf_op jit(solution)/shard_map/project/pallas_call | solution.py:180
  71.1 2.5 collective-permute-start.17
  73.5 8.1 %attend.3 = (bf16[1024,256]{1,0:T(8,128)(2,1)}, f32[1024,256]{1,0:T(8,128)}, bf16[4,4,256,768]{3,2,1,0:T(8,128)(2,1)}) custom-call(bf16[1024,768]{1,0:T(8,128)(2,1)} %get-tuple-element.115.q_ref, bf16[1024,768]{1,0:T(8,128)(2,1)} %get-tuple-element.116.k_ref, bf16[1024,768]{1,0:T(8,128)(2,1)} %get-tuple-element.117.v_ref, ...), custom_call_target="tpu_custom_call" | custom-call | flops 2684354560 | bytes 7864320 | tf_op jit(solution)/shard_map/attend/pallas_call | solution.py:285
  81.6 8.3 %attend.4 = (bf16[1024,256]{1,0:T(8,128)(2,1)}, f32[1024,256]{1,0:T(8,128)}, bf16[4,4,256,768]{3,2,1,0:T(8,128)(2,1)}) custom-call(bf16[1024,768]{1,0:T(8,128)(2,1)} %get-tuple-element.115.q_ref, bf16[1024,768]{1,0:T(8,128)(2,1)} %get-tuple-element.116.k_ref, bf16[1024,768]{1,0:T(8,128)(2,1)} %get-tuple-element.117.v_ref, ...), custom_call_target="tpu_custom_call" | custom-call | flops 2684354560 | bytes 7864320 | tf_op jit(solution)/shard_map/attend/pallas_call | solution.py:285
  91.7 8.1 %attend.5 = (bf16[1024,256]{1,0:T(8,128)(2,1)}, f32[1024,256]{1,0:T(8,128)}, bf16[4,4,256,768]{3,2,1,0:T(8,128)(2,1)}) custom-call(bf16[1024,768]{1,0:T(8,128)(2,1)} %get-tuple-element.115.q_ref, bf16[1024,768]{1,0:T(8,128)(2,1)} %get-tuple-element.116.k_ref, bf16[1024,768]{1,0:T(8,128)(2,1)} %get-tuple-element.117.v_ref, ...), custom_call_target="tpu_custom_call" | custom-call | flops 2684354560 | bytes 7864320 | tf_op jit(solution)/shard_map/attend/pallas_call | solution.py:285
  105.1 18.1 %ffn.1 = (f32[1024,768]{1,0:T(8,128)}, bf16[1024,768]{1,0:T(8,128)(2,1)}, bf16[1024,2048]{1,0:T(8,128)(2,1)}, bf16[1024,2048]{1,0:T(8,128)(2,1)}, bf16[1024,2048]{1,0:T(8,128)(2,1)}) custom-call(s32[2,32]{1,0:T(2,128)} %pad_add_fusion.tab_ref, bf16[4,48,2432]{2,1,0:T(8,128)(2,1)} %copy-done.26, bf16[4,48,2432]{2,1,0:T(8,128)(2,1)} %collective-permute-done.20.refs_1_, ...), custom_call_target="tpu_custom_call" | custom-call | flops 7650410496 | bytes 29360128 | tf_op jit(solution)/shard_map/ffn/pallas_call | solution.py:449
  125.0 9.5 %grad_down.1 = (bf16[16,128,384]{2,1,0:T(8,128)(2,1)}, bf16[16,128,384]{2,1,0:T(8,128)(2,1)}) custom-call(s32[32]{0:T(128)} %add.392.tab_ref, bf16[1024,2048]{1,0:T(8,128)(2,1)} %get-tuple-element.142.refs_0_.refs_9_, bf16[1024,768]{1,0:T(8,128)(2,1)} %bitcast.65), custom_call_target="tpu_custom_call" | custom-call | flops 3221225472 | bytes 8912896 | tf_op jit(solution)/shard_map/grad_down/pallas_call | solution.py:708
  135.8 15.3 %hidden_back.1 = (bf16[1024,768]{1,0:T(8,128)(2,1)}, bf16[1024,2048]{1,0:T(8,128)(2,1)}, bf16[1024,2048]{1,0:T(8,128)(2,1)}) custom-call(s32[2,32]{1,0:T(2,128)} %pad_add_fusion.tab_ref, bf16[4,128,384]{2,1,0:T(8,128)(2,1)} %copy-done.30, bf16[4,128,384]{2,1,0:T(8,128)(2,1)} %copy-done.42, bf16[4,128,384]{2,1,0:T(8,128)(2,1)} %copy-done.29, ...), custom_call_target="tpu_custom_call" | custom-call | flops 6442450944 | bytes 28311552 | tf_op jit(solution)/shard_map/hidden_back/pallas_call | solution.py:503
  153.7 12.5 %grad_gate_up.1 = (bf16[16,48,2048]{2,1,0:T(8,128)(2,1)}, bf16[16,48,2048]{2,1,0:T(8,128)(2,1)}) custom-call(s32[32]{0:T(128)} %add.392.tab_ref, bf16[1024,768]{1,0:T(8,128)(2,1)} %get-tuple-element.151.refs_0_, bf16[1024,2048]{1,0:T(8,128)(2,1)} %get-tuple-element.148.refs_1_.refs_9_, bf16[1024,2048]{1,0:T(8,128)(2,1)} %get-tuple-element.152.refs_2_.refs_10_), custom_call_target="tpu_custom_call" | custom-call | flops 6442450944 | bytes 16252928 | tf_op jit(solution)/shard_map/grad_gate_up/pallas_call | solution.py:708
  170.4 19.9 %middle_back.1 = (f32[1024,768]{1,0:T(8,128)}, bf16[1024,768]{1,0:T(8,128)(2,1)}, bf16[1024,768]{1,0:T(8,128)(2,1)}) custom-call(s32[2,32]{1,0:T(2,128)} %pad_add_fusion.tab_ref, bf16[4,48,2432]{2,1,0:T(8,128)(2,1)} %copy-done.26, bf16[4,48,2432]{2,1,0:T(8,128)(2,1)} %collective-permute-done.20.refs_1_, ...), custom_call_target="tpu_custom_call" | custom-call | flops 7650410496 | bytes 14680064 | tf_op jit(solution)/shard_map/middle_back/pallas_call | solution.py:562
  192.2 3.1 add_convert_fusion
  197.6 10.6 %attend_back.3 = (bf16[1024,256]{1,0:T(8,128)(2,1)}, bf16[1024,256]{1,0:T(8,128)(2,1)}, bf16[1024,256]{1,0:T(8,128)(2,1)}) custom-call(bf16[1024,768]{1,0:T(8,128)(2,1)} %get-tuple-element.115.q_ref, bf16[1024,768]{1,0:T(8,128)(2,1)} %get-tuple-element.116.k_ref, bf16[1024,768]{1,0:T(8,128)(2,1)} %get-tuple-element.117.v_ref, ...), custom_call_target="tpu_custom_call" | custom-call | flops 5368709120 | bytes 9437184 | tf_op jit(solution)/shard_map/attend_back/pallas_call | solution.py:389
  211.0 10.6 %attend_back.4 = (bf16[1024,256]{1,0:T(8,128)(2,1)}, bf16[1024,256]{1,0:T(8,128)(2,1)}, bf16[1024,256]{1,0:T(8,128)(2,1)}) custom-call(bf16[1024,768]{1,0:T(8,128)(2,1)} %get-tuple-element.115.q_ref, bf16[1024,768]{1,0:T(8,128)(2,1)} %get-tuple-element.116.k_ref, bf16[1024,768]{1,0:T(8,128)(2,1)} %get-tuple-element.117.v_ref, ...), custom_call_target="tpu_custom_call" | custom-call | flops 5368709120 | bytes 9437184 | tf_op jit(solution)/shard_map/attend_back/pallas_call | solution.py:389
  227.8 9.8 %grad_qk_out.1 = (bf16[16,48,1152]{2,1,0:T(8,128)(2,1)}, bf16[16,48,1152]{2,1,0:T(8,128)(2,1)}) custom-call(s32[32]{0:T(128)} %add.392.tab_ref, bf16[1024,768]{1,0:T(8,128)(2,1)} %get-tuple-element.191.refs_0_, bf16[1024,256]{1,0:T(8,128)(2,1)} %get-tuple-element.121.refs_9_.mixed_ref.refs_1_, ...), custom_call_target="tpu_custom_call" | custom-call | flops 3623878656 | bytes 9830400 | tf_op jit(solution)/shard_map/grad_qk_out/pallas_call | solution.py:708
  238.8 2.2 add_convert_fusion.4
  242.5 2.3 add_convert_fusion.2
  246.8 10.6 %attend_back.5 = (bf16[1024,256]{1,0:T(8,128)(2,1)}, bf16[1024,256]{1,0:T(8,128)(2,1)}, bf16[1024,256]{1,0:T(8,128)(2,1)}) custom-call(bf16[1024,768]{1,0:T(8,128)(2,1)} %get-tuple-element.115.q_ref, bf16[1024,768]{1,0:T(8,128)(2,1)} %get-tuple-element.116.k_ref, bf16[1024,768]{1,0:T(8,128)(2,1)} %get-tuple-element.117.v_ref, ...), custom_call_target="tpu_custom_call" | custom-call | flops 5368709120 | bytes 9437184 | tf_op jit(solution)/shard_map/attend_back/pallas_call | solution.py:389
  257.4 4.7 %collective-permute-done.48 = bf16[2,48,2048]{2,1,0:T(8,128)(2,1)} collective-permute-done((bf16[2,48,2048]{2,1,0:T(8,128)(2,1)}, bf16[2,48,2048]{2,1,0:T(8,128)(2,1)}, u32[]{:S(2)}, u32[]{:S(2)}) %collective-permute-start.48) | collective-permute-done | bytes 393248 | tf_op jit(solution)/shard_map/ppermute | solution.py:747
  262.1 2.2 fusion.10
  264.3 2.2 add_convert_fusion.10
  269.4 5.7 %grad_qkv_rest.1 = (bf16[16,48,384]{2,1,0:T(8,128)(2,1)}, bf16[16,48,384]{2,1,0:T(8,128)(2,1)}) custom-call(s32[32]{0:T(128)} %add.392.tab_ref, bf16[1024,768]{1,0:T(8,128)(2,1)} %get-tuple-element.191.refs_0_, bf16[1024,256]{1,0:T(8,128)(2,1)} %get-tuple-element.188.refs_1_.refs_12_, bf16[1024,256]{1,0:T(8,128)(2,1)} %get-tuple-element.192.refs_2_.refs_15_, ...), custom_call_target="tpu_custom_call" | custom-call | flops 1207959552 | bytes 4325376 | tf_op jit(solution)/shard_map/grad_qkv_rest/pallas_call | solution.py:708
  279.6 2.9 collective-permute-start.54
  286.4 11.6 %input_grad.1 = f32[1024,768]{1,0:T(8,128)} custom-call(s32[2,32]{1,0:T(2,128)} %pad_add_fusion.tab_ref, bf16[4,48,1152]{2,1,0:T(8,128)(2,1)} %copy-done.1, bf16[4,48,1152]{2,1,0:T(8,128)(2,1)} %copy-done.13, bf16[4,48,1152]{2,1,0:T(8,128)(2,1)} %copy-done.8, bf16[4,48,1152]{2,1,0:T(8,128)(2,1)} %copy-done.12, bf16[4,48,1152]{2,1,0:T(8,128)(2,1)} %copy-done.15, ...), custom_call_target="tpu_custom_call" | custom-call | flops 3623878656 | bytes 15728640 | tf_op jit(solution)/shard_map/input_grad/pallas_call | solution.py:615
  304.1 2.7 collective-permute-start.62
  309.4 2.1 collective-permute-start.57
  316.9 3.3 %collective-permute-done.58 = bf16[48,1152]{1,0:T(8,128)(2,1)S(1)} collective-permute-done((bf16[48,1152]{1,0:T(8,128)(2,1)S(1)}, bf16[48,1152]{1,0:T(8,128)(2,1)S(1)}, u32[]{:S(2)}, u32[]{:S(2)}) %collective-permute-start.58) | collective-permute-done | bytes 110624 | tf_op jit(solution)/shard_map/ppermute | solution.py:747
  (312 shorter events, 91.7 us)
Async XLA Ops:
  3.6 13.5 %collective-permute-start.2 = (bf16[1,48,1152]{2,1,0:T(8,128)(2,1)}, bf16[1,48,1152]{2,1,0:T(8,128)(2,1)S(1)}, u32[]{:S(2)}, u32[]{:S(2)}) collective-permute-start(bf16[1,48,1152]{2,1,0:T(8,128)(2,1)} %bitcast.53), channel_id=1, source_target_pairs={{0,12},{1,13},{2,14},{3,15},{4,8},{5,9},{6,10},{7,11},{8,4},{9,5},... | collective-permute-start | bytes 331784 | tf_op jit(solution)/shard_map/ppermute | solution.py:747
  24.7 12.8 %collective-permute-start.9 = (bf16[4,48,1152]{2,1,0:T(8,128)(2,1)S(1)}, bf16[4,48,1152]{2,1,0:T(8,128)(2,1)S(1)}, u32[]{:S(2)}, u32[]{:S(2)}) collective-permute-start(bf16[4,48,1152]{2,1,0:T(8,128)(2,1)S(1)} %constant_dynamic-update-slice_fusion.refs_2_), channel_id=1, source_target_pairs={{0,2},{1,3},{2,0},{3,1},{4,6},{5,7},{6,4},{7,5},{8,10},{9,11},{10,... | collective-permute-start | bytes 1327112 | tf_op jit(solution)/shard_map/ppermute | solution.py:747
  30.6 17.8 %collective-permute-start.4 = (bf16[1,48,2432]{2,1,0:T(8,128)(2,1)S(1)}, bf16[1,48,2432]{2,1,0:T(8,128)(2,1)S(1)}, u32[]{:S(2)}, u32[]{:S(2)}) collective-permute-start(bf16[1,48,2432]{2,1,0:T(8,128)(2,1)S(1)} %bitcast.60), channel_id=1, source_target_pairs={{0,8},{1,9},{2,10},{3,11},{4,12},{5,13},{6,14},{7,15},{8,0},{9,1},... | collective-permute-start | bytes 700424 | tf_op jit(solution)/shard_map/ppermute | solution.py:747
  30.6 18.4 %collective-permute-start.12 = (bf16[4,48,1152]{2,1,0:T(8,128)(2,1)S(1)}, bf16[4,48,1152]{2,1,0:T(8,128)(2,1)S(1)}, u32[]{:S(2)}, u32[]{:S(2)}) collective-permute-start(bf16[4,48,1152]{2,1,0:T(8,128)(2,1)S(1)} %constant_dynamic-update-slice_fusion.refs_2_), channel_id=1, source_target_pairs={{0,1},{1,0},{2,3},{3,2},{4,5},{5,4},{6,7},{7,6},{8,9},{9,8},{10,11... | collective-permute-start | bytes 1327112 | tf_op jit(solution)/shard_map/ppermute | solution.py:747
  37.5 15.4 %collective-permute-start.10 = (bf16[4,48,1152]{2,1,0:T(8,128)(2,1)S(1)}, bf16[4,48,1152]{2,1,0:T(8,128)(2,1)S(1)}, u32[]{:S(2)}, u32[]{:S(2)}) collective-permute-start(bf16[4,48,1152]{2,1,0:T(8,128)(2,1)S(1)} %pad_maximum_fusion.4.refs_0_), channel_id=1, source_target_pairs={{0,1},{1,0},{2,3},{3,2},{4,5},{5,4},{6,7},{7,6},{8,9},{9,8},{10,11... | collective-permute-start | bytes 1327112 | tf_op jit(solution)/shard_map/ppermute | solution.py:747
  37.5 15.5 %collective-permute-start.13 = (bf16[4,48,1152]{2,1,0:T(8,128)(2,1)S(1)}, bf16[4,48,1152]{2,1,0:T(8,128)(2,1)S(1)}, u32[]{:S(2)}, u32[]{:S(2)}) collective-permute-start(bf16[4,48,1152]{2,1,0:T(8,128)(2,1)S(1)} %collective-permute-done.9.refs_3_), channel_id=1, source_target_pairs={{0,1},{1,0},{2,3},{3,2},{4,5},{5,4},{6,7},{7,6},{8,9},{9,8},{10,11... | collective-permute-start | bytes 1327112 | tf_op jit(solution)/shard_map/ppermute | solution.py:747
  38.0 15.0 %collective-permute-start.11 = (bf16[4,48,1152]{2,1,0:T(8,128)(2,1)S(1)}, bf16[4,48,1152]{2,1,0:T(8,128)(2,1)S(1)}, u32[]{:S(2)}, u32[]{:S(2)}) collective-permute-start(bf16[4,48,1152]{2,1,0:T(8,128)(2,1)S(1)} %collective-permute-done.7.refs_1_), channel_id=1, source_target_pairs={{0,1},{1,0},{2,3},{3,2},{4,5},{5,4},{6,7},{7,6},{8,9},{9,8},{10,11... | collective-permute-start | bytes 1327112 | tf_op jit(solution)/shard_map/ppermute | solution.py:747
  48.4 16.9 %collective-permute-start.16 = (bf16[2,48,2432]{2,1,0:T(8,128)(2,1)S(1)}, bf16[2,48,2432]{2,1,0:T(8,128)(2,1)S(1)}, u32[]{:S(2)}, u32[]{:S(2)}) collective-permute-start(bf16[2,48,2432]{2,1,0:T(8,128)(2,1)S(1)} %pad_maximum_fusion.3), channel_id=1, source_target_pairs={{0,16},{16,0},{1,17},{17,1},{2,18},{18,2},{3,19},{19,3},{4,20},{20... | collective-permute-start | bytes 1400840 | tf_op jit(solution)/shard_map/ppermute | solution.py:747
  49.8 15.5 %collective-permute-start.15 = (bf16[2,48,2432]{2,1,0:T(8,128)(2,1)S(1)}, bf16[2,48,2432]{2,1,0:T(8,128)(2,1)S(1)}, u32[]{:S(2)}, u32[]{:S(2)}) collective-permute-start(bf16[2,48,2432]{2,1,0:T(8,128)(2,1)S(1)} %pad_maximum_fusion.2), channel_id=1, source_target_pairs={{0,2},{1,3},{2,0},{3,1},{4,6},{5,7},{6,4},{7,5},{8,10},{9,11},{10,... | collective-permute-start | bytes 1400840 | tf_op jit(solution)/shard_map/ppermute | solution.py:747
  67.0 22.9 %collective-permute-start.19 = (bf16[4,48,2432]{2,1,0:T(8,128)(2,1)}, bf16[4,48,2432]{2,1,0:T(8,128)(2,1)S(1)}, u32[]{:S(2)}, u32[]{:S(2)}) collective-permute-start(bf16[4,48,2432]{2,1,0:T(8,128)(2,1)} %constant_dynamic-update-slice_fusion.7.refs_2_), channel_id=1, source_target_pairs={{0,1},{1,0},{2,3},{3,2},{4,5},{5,4},{6,7},{7,6},{8,9},{9,8},{10,11... | collective-permute-start | bytes 2801672 | tf_op jit(solution)/shard_map/ppermute | solution.py:747
  67.0 22.9 %collective-permute-start.18 = (bf16[4,48,2432]{2,1,0:T(8,128)(2,1)S(1)}, bf16[4,48,2432]{2,1,0:T(8,128)(2,1)S(1)}, u32[]{:S(2)}, u32[]{:S(2)}) collective-permute-start(bf16[4,48,2432]{2,1,0:T(8,128)(2,1)S(1)} %constant_dynamic-update-slice_fusion.5.refs_0_), channel_id=1, source_target_pairs={{0,1},{1,0},{2,3},{3,2},{4,5},{5,4},{6,7},{7,6},{8,9},{9,8},{10,11... | collective-permute-start | bytes 2801672 | tf_op jit(solution)/shard_map/ppermute | solution.py:747
  68.7 31.1 %collective-permute-start.21 = (bf16[4,48,2432]{2,1,0:T(8,128)(2,1)}, bf16[4,48,2432]{2,1,0:T(8,128)(2,1)}, u32[]{:S(2)}, u32[]{:S(2)}) collective-permute-start(bf16[4,48,2432]{2,1,0:T(8,128)(2,1)} %constant_dynamic-update-slice_fusion.7.refs_2_), channel_id=1, source_target_pairs={{0,2},{1,3},{2,0},{3,1},{4,6},{5,7},{6,4},{7,5},{8,10},{9,11},{10,... | collective-permute-start | bytes 2801672 | tf_op jit(solution)/shard_map/ppermute | solution.py:747
  69.5 30.3 %collective-permute-start.20 = (bf16[4,48,2432]{2,1,0:T(8,128)(2,1)S(1)}, bf16[4,48,2432]{2,1,0:T(8,128)(2,1)}, u32[]{:S(2)}, u32[]{:S(2)}) collective-permute-start(bf16[4,48,2432]{2,1,0:T(8,128)(2,1)S(1)} %constant_dynamic-update-slice_fusion.5.refs_0_), channel_id=1, source_target_pairs={{0,16},{16,0},{1,17},{17,1},{2,18},{18,2},{3,19},{19,3},{4,20},{20... | collective-permute-start | bytes 2801672 | tf_op jit(solution)/shard_map/ppermute | solution.py:747
  71.1 18.8 %collective-permute-start.17 = (bf16[2,128,384]{2,1,0:T(8,128)(2,1)S(1)}, bf16[2,128,384]{2,1,0:T(8,128)(2,1)S(1)}, u32[]{:S(2)}, u32[]{:S(2)}) collective-permute-start(bf16[2,128,384]{2,1,0:T(8,128)(2,1)S(1)} %constant_dynamic-update-slice_fusion.3), channel_id=1, source_target_pairs={{0,8},{1,9},{2,10},{3,11},{4,12},{5,13},{6,14},{7,15},{8,0},{9,1},... | collective-permute-start | bytes 589832 | tf_op jit(solution)/shard_map/ppermute | solution.py:747
  100.7 22.5 %collective-permute-start.27 = (bf16[4,128,384]{2,1,0:T(8,128)(2,1)S(1)}, bf16[4,128,384]{2,1,0:T(8,128)(2,1)S(1)}, u32[]{:S(2)}, u32[]{:S(2)}) collective-permute-start(bf16[4,128,384]{2,1,0:T(8,128)(2,1)S(1)} %constant_dynamic-update-slice_fusion.11.refs_2_), channel_id=1, source_target_pairs={{0,2},{1,3},{2,0},{3,1},{4,6},{5,7},{6,4},{7,5},{8,10},{9,11},{10,... | collective-permute-start | bytes 1179656 | tf_op jit(solution)/shard_map/ppermute | solution.py:747
  101.6 21.6 %collective-permute-start.26 = (bf16[4,128,384]{2,1,0:T(8,128)(2,1)S(1)}, bf16[4,128,384]{2,1,0:T(8,128)(2,1)S(1)}, u32[]{:S(2)}, u32[]{:S(2)}) collective-permute-start(bf16[4,128,384]{2,1,0:T(8,128)(2,1)S(1)} %constant_dynamic-update-slice_fusion.9.refs_0_), channel_id=1, source_target_pairs={{0,16},{16,0},{1,17},{17,1},{2,18},{18,2},{3,19},{19,3},{4,20},{20... | collective-permute-start | bytes 1179656 | tf_op jit(solution)/shard_map/ppermute | solution.py:747
  135.6 15.5 %collective-permute-start.32 = (bf16[16,128,384]{2,1,0:T(8,128)(2,1)}, bf16[16,128,384]{2,1,0:T(8,128)(2,1)S(1)}, u32[]{:S(2)}, u32[]{:S(2)}) collective-permute-start(bf16[16,128,384]{2,1,0:T(8,128)(2,1)} %get-tuple-element.149), channel_id=1, source_target_pairs={{0,1},{1,0},{2,3},{3,2},{4,5},{5,4},{6,7},{7,6},{8,9},{9,8},{10,11... | collective-permute-start | bytes 4718600 | tf_op jit(solution)/shard_map/ppermute | solution.py:747
  151.3 14.9 %collective-permute-start.34 = (bf16[4,128,384]{2,1,0:T(8,128)(2,1)S(1)}, bf16[4,128,384]{2,1,0:T(8,128)(2,1)S(1)}, u32[]{:S(2)}, u32[]{:S(2)}) collective-permute-start(bf16[4,128,384]{2,1,0:T(8,128)(2,1)S(1)} %get-tuple-element.215), channel_id=1, source_target_pairs={{0,2},{1,3},{2,0},{3,1},{4,6},{5,7},{6,4},{7,5},{8,10},{9,11},{10,... | collective-permute-start | bytes 1179656 | tf_op jit(solution)/shard_map/ppermute | solution.py:747
  152.2 14.1 %collective-permute-start.33 = (bf16[4,128,384]{2,1,0:T(8,128)(2,1)S(1)}, bf16[4,128,384]{2,1,0:T(8,128)(2,1)S(1)}, u32[]{:S(2)}, u32[]{:S(2)}) collective-permute-start(bf16[4,128,384]{2,1,0:T(8,128)(2,1)S(1)} %get-tuple-element.216), channel_id=1, source_target_pairs={{0,16},{16,0},{1,17},{17,1},{2,18},{18,2},{3,19},{19,3},{4,20},{20... | collective-permute-start | bytes 1179656 | tf_op jit(solution)/shard_map/ppermute | solution.py:747
  167.1 23.2 %collective-permute-start.37 = (bf16[16,48,2048]{2,1,0:T(8,128)(2,1)}, bf16[16,48,2048]{2,1,0:T(8,128)(2,1)S(1)}, u32[]{:S(2)}, u32[]{:S(2)}) collective-permute-start(bf16[16,48,2048]{2,1,0:T(8,128)(2,1)} %get-tuple-element.157), channel_id=1, source_target_pairs={{0,1},{1,0},{2,3},{3,2},{4,5},{5,4},{6,7},{7,6},{8,9},{9,8},{10,11... | collective-permute-start | bytes 9437192 | tf_op jit(solution)/shard_map/ppermute | solution.py:747
  168.6 21.7 %collective-permute-start.36 = (bf16[2,128,384]{2,1,0:T(8,128)(2,1)S(1)}, bf16[2,128,384]{2,1,0:T(8,128)(2,1)}, u32[]{:S(2)}, u32[]{:S(2)}) collective-permute-start(bf16[2,128,384]{2,1,0:T(8,128)(2,1)S(1)} %get-tuple-element.213), channel_id=1, source_target_pairs={{0,16},{16,0},{1,17},{17,1},{2,18},{18,2},{3,19},{19,3},{4,20},{20... | collective-permute-start | bytes 589832 | tf_op jit(solution)/shard_map/ppermute | solution.py:747
  169.2 21.2 %collective-permute-start.35 = (bf16[2,128,384]{2,1,0:T(8,128)(2,1)S(1)}, bf16[2,128,384]{2,1,0:T(8,128)(2,1)}, u32[]{:S(2)}, u32[]{:S(2)}) collective-permute-start(bf16[2,128,384]{2,1,0:T(8,128)(2,1)S(1)} %get-tuple-element.214), channel_id=1, source_target_pairs={{0,2},{1,3},{2,0},{3,1},{4,6},{5,7},{6,4},{7,5},{8,10},{9,11},{10,... | collective-permute-start | bytes 589832 | tf_op jit(solution)/shard_map/ppermute | solution.py:747
  191.6 16.6 %collective-permute-start.38 = (bf16[2,128,384]{2,1,0:T(8,128)(2,1)S(1)}, bf16[2,128,384]{2,1,0:T(8,128)(2,1)S(1)}, u32[]{:S(2)}, u32[]{:S(2)}) collective-permute-start(bf16[2,128,384]{2,1,0:T(8,128)(2,1)S(1)} %add_convert_fusion.13), channel_id=1, source_target_pairs={{0,8},{1,9},{2,10},{3,11},{4,12},{5,13},{6,14},{7,15},{8,0},{9,1},... | collective-permute-start | bytes 589832 | tf_op jit(solution)/shard_map/ppermute | solution.py:747
  195.3 26.3 %collective-permute-start.40 = (bf16[4,48,2048]{2,1,0:T(8,128)(2,1)}, bf16[4,48,2048]{2,1,0:T(8,128)(2,1)}, u32[]{:S(2)}, u32[]{:S(2)}) collective-permute-start(bf16[4,48,2048]{2,1,0:T(8,128)(2,1)} %get-tuple-element.207), channel_id=1, source_target_pairs={{0,2},{1,3},{2,0},{3,1},{4,6},{5,7},{6,4},{7,5},{8,10},{9,11},{10,... | collective-permute-start | bytes 2359304 | tf_op jit(solution)/shard_map/ppermute | solution.py:747
  196.2 25.5 %collective-permute-start.39 = (bf16[4,48,2048]{2,1,0:T(8,128)(2,1)}, bf16[4,48,2048]{2,1,0:T(8,128)(2,1)}, u32[]{:S(2)}, u32[]{:S(2)}) collective-permute-start(bf16[4,48,2048]{2,1,0:T(8,128)(2,1)} %get-tuple-element.208), channel_id=1, source_target_pairs={{0,16},{16,0},{1,17},{17,1},{2,18},{18,2},{3,19},{19,3},{4,20},{20... | collective-permute-start | bytes 2359304 | tf_op jit(solution)/shard_map/ppermute | solution.py:747
  224.0 13.6 %collective-permute-start.43 = (bf16[2,48,2048]{2,1,0:T(8,128)(2,1)S(1)}, bf16[2,48,2048]{2,1,0:T(8,128)(2,1)}, u32[]{:S(2)}, u32[]{:S(2)}) collective-permute-start(bf16[2,48,2048]{2,1,0:T(8,128)(2,1)S(1)} %get-tuple-element.205), channel_id=1, source_target_pairs={{0,16},{16,0},{1,17},{17,1},{2,18},{18,2},{3,19},{19,3},{4,20},{20... | collective-permute-start | bytes 1179656 | tf_op jit(solution)/shard_map/ppermute | solution.py:747
  224.6 13.0 %collective-permute-start.42 = (bf16[2,48,2048]{2,1,0:T(8,128)(2,1)S(1)}, bf16[2,48,2048]{2,1,0:T(8,128)(2,1)}, u32[]{:S(2)}, u32[]{:S(2)}) collective-permute-start(bf16[2,48,2048]{2,1,0:T(8,128)(2,1)S(1)} %get-tuple-element.206), channel_id=1, source_target_pairs={{0,2},{1,3},{2,0},{3,1},{4,6},{5,7},{6,4},{7,5},{8,10},{9,11},{10,... | collective-permute-start | bytes 1179656 | tf_op jit(solution)/shard_map/ppermute | solution.py:747
  241.0 21.1 %collective-permute-start.48 = (bf16[2,48,2048]{2,1,0:T(8,128)(2,1)}, bf16[2,48,2048]{2,1,0:T(8,128)(2,1)}, u32[]{:S(2)}, u32[]{:S(2)}) collective-permute-start(bf16[2,48,2048]{2,1,0:T(8,128)(2,1)} %add_convert_fusion.4), channel_id=1, source_target_pairs={{0,8},{1,9},{2,10},{3,11},{4,12},{5,13},{6,14},{7,15},{8,0},{9,1},... | collective-permute-start | bytes 1179656 | tf_op jit(solution)/shard_map/ppermute | solution.py:747
  244.7 17.4 %collective-permute-start.47 = (bf16[4,48,1152]{2,1,0:T(8,128)(2,1)}, bf16[4,48,1152]{2,1,0:T(8,128)(2,1)}, u32[]{:S(2)}, u32[]{:S(2)}) collective-permute-start(bf16[4,48,1152]{2,1,0:T(8,128)(2,1)} %get-tuple-element.211), channel_id=1, source_target_pairs={{0,2},{1,3},{2,0},{3,1},{4,6},{5,7},{6,4},{7,5},{8,10},{9,11},{10,... | collective-permute-start | bytes 1327112 | tf_op jit(solution)/shard_map/ppermute | solution.py:747
  246.2 15.9 %collective-permute-start.46 = (bf16[4,48,1152]{2,1,0:T(8,128)(2,1)}, bf16[4,48,1152]{2,1,0:T(8,128)(2,1)S(1)}, u32[]{:S(2)}, u32[]{:S(2)}) collective-permute-start(bf16[4,48,1152]{2,1,0:T(8,128)(2,1)} %get-tuple-element.212), channel_id=1, source_target_pairs={{0,16},{16,0},{1,17},{17,1},{2,18},{18,2},{3,19},{19,3},{4,20},{20... | collective-permute-start | bytes 1327112 | tf_op jit(solution)/shard_map/ppermute | solution.py:747
  279.6 18.5 %collective-permute-start.54 = (bf16[2,48,1152]{2,1,0:T(8,128)(2,1)S(1)}, bf16[2,48,1152]{2,1,0:T(8,128)(2,1)S(1)}, u32[]{:S(2)}, u32[]{:S(2)}) collective-permute-start(bf16[2,48,1152]{2,1,0:T(8,128)(2,1)S(1)} %add_convert_fusion.9), channel_id=1, source_target_pairs={{0,8},{1,9},{2,10},{3,11},{4,12},{5,13},{6,14},{7,15},{8,0},{9,1},... | collective-permute-start | bytes 663560 | tf_op jit(solution)/shard_map/ppermute | solution.py:747
  284.6 13.4 %collective-permute-start.56 = (bf16[4,48,384]{2,1,0:T(8,128)(2,1)S(1)}, bf16[4,48,384]{2,1,0:T(8,128)(2,1)S(1)}, u32[]{:S(2)}, u32[]{:S(2)}) collective-permute-start(bf16[4,48,384]{2,1,0:T(8,128)(2,1)S(1)} %get-tuple-element.222), channel_id=1, source_target_pairs={{0,2},{1,3},{2,0},{3,1},{4,6},{5,7},{6,4},{7,5},{8,10},{9,11},{10,... | collective-permute-start | bytes 442376 | tf_op jit(solution)/shard_map/ppermute | solution.py:747
  (80 other events, 707.1 us)

commit v3 on v2

--- a/solution.py
+++ b/solution.py
@@ -2,6 +2,7 @@
 
 import jax
 import jax.numpy as jnp
+import numpy as np
 from jax import lax
 from jax.experimental import pallas as pl
 from jax.experimental.pallas import tpu as pltpu
@@ -44,54 +45,61 @@
 ANY = pl.BlockSpec(memory_space=pl.ANY)
 
 
-def weight_copies(pieces, tab_ref, dest, sem, start, width):
-    copies = []
-    index = 0
-    for piece in pieces:
-        count, rows = piece.shape[0], piece.shape[1]
-        for b in range(count):
-            row = pl.multiple_of(tab_ref[0, index] * rows, 16)
-            col = pl.multiple_of(tab_ref[1, index] * width, 128)
-            copies.append(
-                pltpu.make_async_copy(
-                    piece.at[b, :, pl.ds(start, width)],
-                    dest.at[pl.ds(row, rows), pl.ds(col, width)],
-                    sem.at[index],
+class WeightCopies:
+    def __init__(self, pieces, tab_ref, dest, sem, start, width):
+        self.pieces, self.tab, self.dest, self.sem = pieces, tab_ref, dest, sem
+        self.start_col, self.width = start, width
+
+    def each(self, act):
+        for number, piece in enumerate(self.pieces):
+            count, rows = piece.shape[0], piece.shape[1]
+
+            def step(b, carry):
+                index = number * count + b
+                row = pl.multiple_of(self.tab[0, index] * rows, 16)
+                col = pl.multiple_of(self.tab[1, index] * self.width, 128)
+                act(
+                    pltpu.make_async_copy(
+                        piece.at[b, :, pl.ds(self.start_col, self.width)],
+                        self.dest.at[pl.ds(row, rows), pl.ds(col, self.width)],
+                        self.sem.at[index],
+                    )
                 )
-            )
-            index += 1
-    return copies
-
-
-def start_all(copies):
-    for copy in copies:
-        copy.start()
-
-
-def wait_all(copies):
-    for copy in copies:
-        copy.wait()
+                return carry
+
+            lax.fori_loop(0, count, step, 0)
+
+    def start(self):
+        self.each(lambda copy: copy.start())
+
+    def wait(self):
+        self.each(lambda copy: copy.wait())
 
 
 def load_weight(pieces, tab_ref, dest, sem):
-    copies = weight_copies(pieces, tab_ref, dest, sem, 0, pieces[0].shape[2])
-    start_all(copies)
-    wait_all(copies)
-
-
-GROUPS = 3
+    copies = WeightCopies(pieces, tab_ref, dest, sem, 0, pieces[0].shape[2])
+    copies.start()
+    copies.wait()
+
+
+SPLIT = (2, 1)
 
 
 def in_order(refs, half=0, halves=1):
     return jnp.concatenate(
         [
-            ref[:, j * 128 : (j + 1) * 128]
+            ref[:, j * (ref.shape[1] // 2) : (j + 1) * (ref.shape[1] // 2)]
             for j in range(2)
             if j * halves // 2 == half
             for ref in refs
         ],
         1,
     )
+
+
+def pair_of(call):
+    first, count = sum(SPLIT[:call]), SPLIT[call]
+    return lambda i: (0, first + i % count + sum(SPLIT) * (i // count))
 
 
 def pack_kernel(half_ref, *refs, folded):
@@ -130,11 +138,16 @@
 
 
 def rope_tables(length):
-    position = jnp.arange(length, dtype=f32)
-    exponent = jnp.arange(HD // 2, dtype=f32) * (2.0 / HD)
-    angles = position[:, None] * jnp.power(rope_base, -exponent)[None, :]
-    cosine, sine = jnp.cos(angles), jnp.sin(angles)
-    return jnp.concatenate([cosine] * 4, 1), jnp.concatenate([-sine, sine, -sine, sine], 1)
+    frequency = rope_base ** -(np.arange(HD // 2) * (2.0 / HD))
+    coarse = np.arange(length // 32)[:, None] * 32.0 * frequency[None, :]
+    fine = np.arange(32)[:, None] * frequency[None, :]
+    coarse, fine = np.tile(coarse, (1, 4))[:, None, :], np.tile(fine, (1, 4))[None, :, :]
+    sign = np.tile(np.repeat([-1.0, 1.0], HD // 2), 2)
+    cos_a, sin_a = jnp.asarray(np.cos(coarse), f32), jnp.asarray(np.sin(coarse), f32)
+    cos_b, sin_b = jnp.asarray(np.cos(fine), f32), jnp.asarray(np.sin(fine), f32)
+    cosine = cos_a * cos_b - sin_a * sin_b
+    sine = (sin_a * cos_b + cos_a * sin_b) * jnp.asarray(sign, f32)
+    return cosine.reshape(length, 128), sine.reshape(length, 128)
 
 
 def swap_halves(tensor):
@@ -157,8 +170,9 @@
     n_ref[...] = normed
     width = x_ref.shape[1] // halves
     cosine, sine = cos_ref[...], sin_ref[...]
+    everything = dot(normed, weight[...])
     for half in range(halves):
-        result = dot(normed, weight[:, 3 * half * width : 3 * (half + 1) * width])
+        result = everything[:, 3 * half * width : 3 * (half + 1) * width]
         for part, out, scale in ((0, q_ref, HD**-0.5), (1, k_ref, 1.0)):
             for c in range(0, width, 128):
                 piece = result[:, part * width + c : part * width + c + 128]
@@ -211,8 +225,7 @@
     )
 
 
-def pipeline(items, first, second, third):
-    ahead = 2
+def pipeline(items, first, second, third, ahead=2):
     made = [first(item) for item in items[:ahead]]
     pending = None
     for i, item in enumerate(items):
@@ -276,24 +289,24 @@
     return min(length, MAX_DOC + BLOCK)
 
 
-def attend(q, k, v, q_marks, k_marks, first, jump):
-    length = q.shape[0]
+def attend(q, k, v, q_marks, k_marks):
+    length, width = q.shape
     blocks = length // BLOCK
-    column = pl.BlockSpec((length, 128), lambda i: (0, first + jump * i))
+    pairs = width // 128
+    column = pl.BlockSpec((length, 128), lambda i: (0, i))
     fixed = pl.BlockSpec((length, 128), lambda i: (0, 0))
-    part = pl.BlockSpec((length, 128), lambda i: (0, i))
     return pl.pallas_call(
         attend_kernel,
-        grid=(2,),
+        grid=(pairs,),
         in_specs=[column, column, column, fixed, fixed],
-        out_specs=[part, part, pl.BlockSpec((2, blocks, BLOCK, span(length)), lambda i: (i, 0, 0, 0))],
+        out_specs=[column, column, pl.BlockSpec((2, blocks, BLOCK, span(length)), lambda i: (i, 0, 0, 0))],
         out_shape=[
-            jax.ShapeDtypeStruct((length, 256), bf16),
-            jax.ShapeDtypeStruct((length, 256), f32),
-            jax.ShapeDtypeStruct((4, blocks, BLOCK, span(length)), bf16),
+            jax.ShapeDtypeStruct((length, 128 * pairs), bf16),
+            jax.ShapeDtypeStruct((length, 128 * pairs), f32),
+            jax.ShapeDtypeStruct((2 * pairs, blocks, BLOCK, span(length)), bf16),
         ],
         compiler_params=params(),
-        cost_estimate=cost(10 * length * length * 256, 30 * length * 256, 4 * length * length),
+        cost_estimate=cost(1280 * pairs * length * length, 3840 * pairs * length, 2 * pairs * length * length),
         name="attend",
     )(q, k, v, q_marks, k_marks)
 
@@ -380,61 +393,75 @@
     pipeline(items, slopes, products, finish)
 
 
-def attend_back(q, k, v, mixed, inv, exps, grad, cosine, sine, first, jump):
+def attend_back(q, k, v, mixed, inv, exps, grad, cosine, sine, call):
     length = q.shape[0]
-    column = pl.BlockSpec((length, 128), lambda i: (0, first + jump * i))
+    pairs = 2 * SPLIT[call]
+    column = pl.BlockSpec((length, 128), pair_of(call))
     part = pl.BlockSpec((length, 128), lambda i: (0, i))
     fixed = pl.BlockSpec((length, 128), lambda i: (0, 0))
-    shape = jax.ShapeDtypeStruct((length, 256), bf16)
+    shape = jax.ShapeDtypeStruct((length, 128 * pairs), bf16)
     return pl.pallas_call(
         attend_back_kernel,
-        grid=(2,),
-        in_specs=[column] * 3
-        + [part, part, pl.BlockSpec((2,) + exps.shape[1:], lambda i: (i, 0, 0, 0)), column, fixed, fixed],
+        grid=(pairs,),
+        in_specs=[column] * 5
+        + [
+            pl.BlockSpec((2,) + exps.shape[1:], lambda i: (pair_of(call)(i)[1], 0, 0, 0)),
+            column,
+            fixed,
+            fixed,
+        ],
         out_specs=[part] * 3,
         out_shape=[shape] * 3,
         scratch_shapes=[pltpu.VMEM((2,) + exps.shape[1:], bf16)],
         compiler_params=params(),
-        cost_estimate=cost(20 * length * length * 256, 36 * length * 256),
+        cost_estimate=cost(2560 * pairs * length * length, 4608 * pairs * length),
         name="attend_back",
     )(q, k, v, mixed, inv, exps, grad, cosine, sine)
 
 
 def ffn_kernel(tab_ref, *refs, n_pieces, halves):
-    pieces, x_ref, mixed_refs = refs[:n_pieces], refs[n_pieces], refs[n_pieces + 1 : n_pieces + 4]
-    middle_ref, normed_ref, hidden_ref, slope_g_ref, slope_u_ref, w_out, w_in, sem = refs[n_pieces + 4 :]
+    pieces, (x_ref, mixed_ref), refs = refs[:n_pieces], refs[n_pieces : n_pieces + 2], refs[n_pieces + 2 :]
+    middle_ref, normed_ref, hidden_ref, slope_g_ref, slope_u_ref, w_out, w_in, sem = refs
     width = x_ref.shape[1] // halves
     inner = hidden_ref.shape[1] // halves
-    early = weight_copies(pieces, tab_ref, w_out, sem.at[0], 0, width)
-    late = weight_copies(pieces, tab_ref, w_in, sem.at[1], width, 2 * inner)
+    early = WeightCopies(pieces, tab_ref, w_out, sem.at[0], 0, width)
+    late = WeightCopies(pieces, tab_ref, w_in, sem.at[1], width, 2 * inner)
 
     @pl.when(pl.program_id(0) == 0)
     def _():
-        start_all(early)
-        start_all(late)
-        wait_all(early)
-
-    middle = x_ref[...].astype(f32) + dot(in_order(mixed_refs), w_out[...])
+        early.start()
+        late.start()
+        early.wait()
+
+    middle = x_ref[...].astype(f32) + dot(mixed_ref[...], w_out[...])
     middle_ref[...] = middle
     normed = (middle * lax.rsqrt(jnp.mean(middle * middle, -1, keepdims=True) + epsilon)).astype(bf16)
     normed_ref[...] = normed
 
     @pl.when(pl.program_id(0) == 0)
     def _():
-        wait_all(late)
-
-    step = min(512, inner)
-    for h in range(halves):
-        for c in range(0, inner, step):
-            first = 2 * h * inner + c
-            gate = dot(normed, w_in[:, first : first + step])
-            up = dot(normed, w_in[:, first + inner : first + inner + step])
-            sigmoid = jax.nn.sigmoid(gate)
-            silu = gate * sigmoid
-            cols = slice(h * inner + c, h * inner + c + step)
-            hidden_ref[:, cols] = (silu * up).astype(bf16)
-            slope_u_ref[:, cols] = silu.astype(bf16)
-            slope_g_ref[:, cols] = (up * sigmoid * (1.0 + gate * (1.0 - sigmoid))).astype(bf16)
+        late.wait()
+
+    step = min(256, inner)
+
+    def dots(first):
+        return (
+            dot(normed, w_in[:, first : first + step]),
+            dot(normed, w_in[:, first + inner : first + inner + step]),
+        )
+
+    def activate(first, values):
+        gate, up = values
+        half_tanh = 0.5 * jnp.tanh(0.5 * gate)
+        sigmoid = half_tanh + 0.5
+        silu = gate * sigmoid
+        cols = slice(first - first // (2 * inner) * inner, first - first // (2 * inner) * inner + step)
+        hidden_ref[:, cols] = (silu * up).astype(bf16)
+        slope_u_ref[:, cols] = silu.astype(bf16)
+        slope_g_ref[:, cols] = (up * (sigmoid + silu * (0.5 - half_tanh))).astype(bf16)
+
+    items = [2 * h * inner + c for h in range(halves) for c in range(0, inner, step)]
+    pipeline(items, dots, activate, lambda *_: None)
 
 
 def ffn(tab, pieces, x, mixed, inner, halves):
@@ -443,7 +470,6 @@
     n = len(pieces)
     blocks = sum(p.shape[0] for p in pieces)
     narrow = pl.BlockSpec((rows, width), lambda i, t: (i, 0))
-    third = pl.BlockSpec((rows, width // 3), lambda i, t: (i, 0))
     wide = pl.BlockSpec((rows, inner), lambda i, t: (i, 0))
     wide_shape = jax.ShapeDtypeStruct((length, inner), bf16)
     return pl.pallas_call(
@@ -451,7 +477,7 @@
         grid_spec=pltpu.PrefetchScalarGridSpec(
             num_scalar_prefetch=1,
             grid=(length // rows,),
-            in_specs=[ANY] * n + [narrow] + [third] * 3,
+            in_specs=[ANY] * n + [narrow, narrow],
             out_specs=[narrow, narrow, wide, wide, wide],
             scratch_shapes=[
                 pltpu.VMEM((width, width), bf16),
@@ -469,7 +495,7 @@
         compiler_params=params(),
         cost_estimate=cost(2 * length * width * (width + 2 * inner), 8 * width * inner + 8 * length * inner),
         name="ffn",
-    )(tab, *pieces, x, *mixed)
+    )(tab, *pieces, x, mixed)
 
 
 def hidden_back_kernel(tab_ref, *refs, n_pieces, halves):
@@ -525,36 +551,50 @@
     grad_middle_ref, attn_grad_ref, grad_mixed_ref, w_out, w_in, sem = refs[n_pieces + 4 :]
     width = cot_ref.shape[1] // halves
     inner = gg_ref.shape[1] // halves
-    early = weight_copies(pieces, tab_ref, w_in, sem.at[0], width, 2 * inner)
-    late = weight_copies(pieces, tab_ref, w_out, sem.at[1], 0, width)
+    early = WeightCopies(pieces, tab_ref, w_in, sem.at[0], width, 2 * inner)
+    late = WeightCopies(pieces, tab_ref, w_out, sem.at[1], 0, width)
 
     @pl.when(pl.program_id(0) == 0)
     def _():
-        start_all(early)
-        start_all(late)
-        wait_all(early)
-        wait_all(late)
-
-    middle = middle_ref[...]
-    both = [
-        ref[:, h * inner : (h + 1) * inner] for h in range(halves) for ref in (gg_ref, gu_ref)
-    ]
-    grad = dot(jnp.concatenate(both, 1), w_in[...], NT)
-    inverse = lax.rsqrt(jnp.mean(middle * middle, -1, keepdims=True) + epsilon)
-    normed = middle * inverse
-    grad_middle = cot_ref[...].astype(f32) + inverse * (
-        grad - normed * jnp.mean(grad * normed, -1, keepdims=True)
-    )
-    grad_middle_ref[...] = grad_middle
-    low = grad_middle.astype(bf16)
-    attn_grad_ref[...] = low
-    grad_mixed_ref[...] = dot(low, w_out[...], NT).astype(bf16)
+        early.start()
+        late.start()
+        early.wait()
+        late.wait()
+
+    def gradient(rows):
+        both = [
+            ref[rows, h * inner : (h + 1) * inner] for h in range(halves) for ref in (gg_ref, gu_ref)
+        ]
+        return dot(jnp.concatenate(both, 1), w_in[...], NT)
+
+    def norm_back(rows, grad):
+        middle = middle_ref[rows, :]
+        inverse = lax.rsqrt(jnp.mean(middle * middle, -1, keepdims=True) + epsilon)
+        normed = middle * inverse
+        grad_middle = cot_ref[rows, :].astype(f32) + inverse * (
+            grad - normed * jnp.mean(grad * normed, -1, keepdims=True)
+        )
+        grad_middle_ref[rows, :] = grad_middle
+        low = grad_middle.astype(bf16)
+        attn_grad_ref[rows, :] = low
+        return low
+
+    def mixed_grad(rows, low):
+        grad_mixed_ref[rows, :] = dot(low, w_out[...], NT).astype(bf16)
+
+    total = middle_ref.shape[0]
+    items = [slice(r, r + SUB) for r in range(0, total, SUB)]
+    pipeline(items, gradient, norm_back, mixed_grad, 1)
+
+
+SUB = 256
+MB_ROWS = 256
 
 
 def middle_back(tab, pieces, middle, gg, gu, cot, halves):
     length, width = middle.shape
     inner = gg.shape[1]
-    rows = BLOCK
+    rows = MB_ROWS
     n = len(pieces)
     narrow = pl.BlockSpec((rows, width), lambda i, t: (i, 0))
     wide = pl.BlockSpec((rows, inner), lambda i, t: (i, 0))
@@ -584,15 +624,16 @@
 def input_kernel(tab_ref, *refs, n_pieces, halves):
     pieces = refs[:n_pieces]
     x_ref, grad_middle_ref = refs[n_pieces : n_pieces + 2]
-    parts = refs[n_pieces + 2 : n_pieces + 2 + 3 * GROUPS]
-    out_ref, weight, sem = refs[n_pieces + 2 + 3 * GROUPS :]
+    calls = len(SPLIT)
+    parts = refs[n_pieces + 2 : n_pieces + 2 + 3 * calls]
+    out_ref, weight, sem = refs[n_pieces + 2 + 3 * calls :]
 
     @pl.when(pl.program_id(0) == 0)
     def _():
         load_weight(pieces, tab_ref, weight, sem)
 
     left = [
-        in_order(parts[part * GROUPS : (part + 1) * GROUPS], h, halves)
+        in_order(parts[part * calls : (part + 1) * calls], h, halves)
         for h in range(halves)
         for part in range(3)
     ]
@@ -611,13 +652,13 @@
     n = len(pieces)
     blocks = sum(p.shape[0] for p in pieces)
     block = pl.BlockSpec((rows, width), lambda i, t: (i, 0))
-    third = pl.BlockSpec((rows, width // GROUPS), lambda i, t: (i, 0))
+    shares = [pl.BlockSpec((rows, p.shape[1]), lambda i, t: (i, 0)) for p in parts]
     return pl.pallas_call(
         functools.partial(input_kernel, n_pieces=n, halves=halves),
         grid_spec=pltpu.PrefetchScalarGridSpec(
             num_scalar_prefetch=1,
             grid=(length // rows,),
-            in_specs=[ANY] * n + [block] * 2 + [third] * (3 * GROUPS),
+            in_specs=[ANY] * n + [block] * 2 + shares,
             out_specs=block,
             scratch_shapes=[
                 pltpu.VMEM((width, 3 * width), bf16),
@@ -631,32 +672,33 @@
     )(tab, *pieces, x, grad_middle, *parts)
 
 
-def weight_kernel(tab_ref, *refs, counts, block_rows, chunks):
+def weight_kernel(tab_ref, *refs, counts, block_rows, chunks, halves):
     n_left, n_right = sum(n for n, _ in counts), sum(n for _, n in counts)
     lefts, rights = list(refs[:n_left]), list(refs[n_left : n_left + n_right])
     keep_ref, send_ref, held, sem = refs[n_left + n_right :]
     step, steps = pl.program_id(0), pl.num_programs(0)
     slot = lax.rem(step, 2)
-    half, chunk = step // chunks, lax.rem(step, chunks)
-    halves = tab_ref.shape[0] * block_rows // held.shape[1]
+    here = halves if chunks == 0 else 1
+    parts = max(1, chunks)
+    rows = held.shape[2]
     kept = keep_ref.shape[0]
-    widths = [r.shape[1] for r in rights]
-    if chunks == 1:
-        widths = [sum(widths)]
+    widths = [r.shape[1] // here for r in rights]
+    sizes = [sum(widths)] if parts == 1 else widths
 
     def pieces():
-        for b in range(held.shape[1] // block_rows):
-            offset = 0
-            for i, width in enumerate(widths):
-                yield b, i, offset, width
-                offset += width
+        for b in range(rows // block_rows):
+            for h in range(here):
+                offset = 0
+                for i, width in enumerate(sizes):
+                    yield b, h, (b * here + h) * len(sizes) + i, offset, width
+                    offset += width
 
     def wait(which):
-        for b, i, offset, width in pieces():
+        for _, h, number, offset, width in pieces():
             pltpu.make_async_copy(
-                held.at[which, pl.ds(0, block_rows), pl.ds(offset, width)],
+                held.at[which, h, pl.ds(0, block_rows), pl.ds(offset, width)],
                 keep_ref.at[0, :, pl.ds(offset, width)],
-                sem.at[which, b * len(widths) + i],
+                sem.at[which, number],
             ).wait()
 
     @pl.when(step >= 2)
@@ -664,25 +706,36 @@
         wait(slot)
 
     offset = 0
-    queue = list(rights)
-    for n_left, n_right in counts:
-        left = lefts.pop(0)[...] if n_left == 1 else in_order([lefts.pop(0) for _ in range(n_left)])
-        right = jnp.concatenate([queue.pop(0)[...] for _ in range(n_right)], 1)
-        held[slot, :, offset : offset + right.shape[1]] = dot(left, right, TN).astype(bf16)
-        offset += right.shape[1]
-    for b, i, offset, width in pieces():
-        place = tab_ref[b * halves + half]
-        source = held.at[slot, pl.ds(b * block_rows, block_rows), pl.ds(offset, width)]
-        cols = pl.ds(pl.multiple_of(offset * chunks + chunk * width, 128), width)
-        signal = sem.at[slot, b * len(widths) + i]
-
-        @pl.when(place < kept)
-        def _():
-            pltpu.make_async_copy(source, keep_ref.at[place, :, cols], signal).start()
-
-        @pl.when(place >= kept)
-        def _():
-            pltpu.make_async_copy(source, send_ref.at[place - kept, :, cols], signal).start()
+    for _, n_right in counts:
+        left = lefts.pop(0)[...]
+        group = [rights.pop(0)[...] for _ in range(n_right)]
+        result = dot(left, jnp.concatenate(group, 1), TN).astype(bf16)
+        column = 0
+        for right in group:
+            width = right.shape[1] // here
+            for h in range(here):
+                held[slot, h, :, offset : offset + width] = result[:, column : column + width]
+                column += width
+            offset += width
+    if chunks == 0:
+        first, half, chunk = step * (rows // block_rows), 0, 0
+    else:
+        first, half, chunk = 0, step // chunks, lax.rem(step, chunks)
+    def send_out(parity):
+        for b, h, number, offset, width in pieces():
+            place = tab_ref[(first + b) * halves + half + h]
+            if b % 2 == parity:
+                target = keep_ref.at[place]
+            else:
+                target = send_ref.at[place - kept]
+            pltpu.make_async_copy(
+                held.at[slot, h, pl.ds(b * block_rows, block_rows), pl.ds(offset, width)],
+                target.at[:, pl.ds(pl.multiple_of(offset * parts + chunk * width, 128), width)],
+                sem.at[slot, number],
+            ).start()
+
+    for parity in range(2):
+        pl.when((tab_ref[0] < kept) == (parity == 0))(functools.partial(send_out, parity))
 
     @pl.when(step == steps - 1)
     def _():
@@ -693,28 +746,42 @@
             wait(1 - slot)
 
 
-def weight_grad(moves, products, chunks, name):
+def weight_grad(moves, products, name, chunks=0, row_steps=1):
     lefts = [left for group, _ in products for left in group]
     rights = [right for _, group in products for right in group]
     counts = [(len(left), len(right)) for left, right in products]
-    length, rows = lefts[0].shape
+    length = lefts[0].shape[0]
+    rows = sum(left.shape[1] for left in products[0][0])
     halves, blocks = moves.halves, moves.place.shape[0]
     block_rows = rows * halves // blocks
     columns = sum(r.shape[1] for r in rights) // halves
     kept = moves.kept
     sent = max(1, blocks - kept)
-    steps = halves * chunks
-    n_pieces = rows // block_rows * (1 if chunks == 1 else len(rights))
+    if halves == 1 and chunks == 0:
+        row_steps = 1
+    steps = halves * chunks if chunks else row_steps
+    here = 1 if chunks else halves
+    step_rows = rows if chunks else rows // row_steps
+    n_pieces = step_rows // block_rows * here * (len(rights) if chunks > 1 else 1)
+    if chunks:
+        left_specs = [pl.BlockSpec(left.shape, lambda i, t: (0, 0)) for left in lefts]
+        right_specs = [pl.BlockSpec((length, r.shape[1] // steps), lambda i, t: (0, i)) for r in rights]
+    else:
+        left_specs = [
+            pl.BlockSpec((length, left.shape[1] // row_steps), lambda i, t: (0, i)) for left in lefts
+        ]
+        right_specs = [pl.BlockSpec(r.shape, lambda i, t: (0, 0)) for r in rights]
     return pl.pallas_call(
-        functools.partial(weight_kernel, counts=counts, block_rows=block_rows, chunks=chunks),
+        functools.partial(
+            weight_kernel, counts=counts, block_rows=block_rows, chunks=chunks, halves=halves
+        ),
         grid_spec=pltpu.PrefetchScalarGridSpec(
             num_scalar_prefetch=1,
             grid=(steps,),
-            in_specs=[pl.BlockSpec(left.shape, lambda i, t: (0, 0)) for left in lefts]
-            + [pl.BlockSpec((length, r.shape[1] // steps), lambda i, t: (0, i)) for r in rights],
+            in_specs=left_specs + right_specs,
             out_specs=[ANY, ANY],
             scratch_shapes=[
-                pltpu.VMEM((2, rows, columns // chunks), bf16),
+                pltpu.VMEM((2, here, step_rows, columns // max(1, chunks)), bf16),
                 pltpu.SemaphoreType.DMA((2, n_pieces)),
             ],
         ),
@@ -979,27 +1046,22 @@
     sends = moves.stage0()
     normed1, q, k, v = project(tab, w1, after(x, *sends), cosine, sine, halves)
     sends = moves.stage1(normed1)
-    seen = []
-    for g in range(GROUPS):
-        seen.append(attend(q, k, v, after(q_marks, *sends), k_marks, g, GROUPS))
-        sends = (seen[-1][0],)
-        if g == 1:
-            sends = moves.stage2(*sends)
-    mixed = [s[0] for s in seen]
-    sends = moves.stage3(mixed[2])
+    mixed, inv, exps = attend(q, k, v, after(q_marks, *sends), k_marks)
+    sends = moves.stage2(mixed)
+    sends = moves.stage3(mixed, *sends)
     w2 = moves.own2
     middle, normed2, hidden, slope_g, slope_u = ffn(
         tab, w2, after(x, *sends), mixed, inner, halves
     )
     w3 = moves.with_core(moves.own3, hidden)
-    g3 = weight_grad(moves, [([after(hidden, *moves.own3)], [cot])], 1, "grad_down")
+    g3 = weight_grad(moves, [([after(hidden, *moves.own3)], [cot])], "grad_down", row_steps=4)
     sum3 = moves.scatter(g3)
     sum3.step(*g3, *w3)
     output, gg, gu = hidden_back(
         tab, w3, middle, after(hidden, *g3), slope_g, slope_u, cot, halves
     )
     sends = sum3.step(gg, *sum3.got)
-    g2 = weight_grad(moves, [([after(normed2, *sends)], [gg, gu])], 2, "grad_gate_up")
+    g2 = weight_grad(moves, [([after(normed2, *sends)], [gg, gu])], "grad_gate_up", chunks=2)
     sum2 = moves.scatter(g2)
     due = (*g2, *sum3.got)
     sends = sum3.step(*due)
@@ -1011,37 +1073,35 @@
     sends = sum3.step(*due)
     sends = (*sends, *sum2.step(*due))
 
-    def back(g, sends):
-        return attend_back(q, k, v, *seen[g], after(grad_mixed, *sends), cosine, sine, g, GROUPS)
+    def back(call, sends):
+        return attend_back(q, k, v, mixed, inv, exps, after(grad_mixed, *sends), cosine, sine, call)
 
     turned0 = back(0, sends)
-    sends = sum3.step(*turned0[:1], *sum3.got)
-    turned1 = back(1, (*turned0[:1], *sends))
-    due = (*turned1[:1], *sum2.got, *sum3.got)
+    due = (*turned0[:1], *sum2.got, *sum3.got)
     sends = sum2.step(*due)
     sends = (*sends, *sum3.step(*due))
     g1 = weight_grad(
         moves,
-        [([after(normed1, *sends)], [*turned0, *turned1]), (mixed, [attn_grad])],
-        1,
+        [([after(normed1, *sends)], turned0), ([mixed], [attn_grad])],
         "grad_qk_out",
+        row_steps=2,
     )
     sum1 = moves.scatter(g1)
     due = (*g1, *sum2.got, *sum3.got)
     sum1.step(*due)
-    sends = sum2.step(*due)
+    sends = (*sum2.step(*due), *sum3.step(*due))
     sends = (*sends, *sum1.step(*sends, *sum1.got))
-    turned2 = back(2, (*g1, *sends))
-    due = (*turned2[:1], *sum1.got, *sum2.got)
+    turned1 = back(1, (*g1, *sends))
+    due = (*turned1[:1], *sum1.got, *sum2.got)
     sends = sum1.step(*due)
     sends = (*sends, *sum2.step(*due))
-    g0 = weight_grad(moves, [([after(normed1, *sends)], turned2)], 1, "grad_qkv_rest")
+    g0 = weight_grad(moves, [([after(normed1, *sends)], turned1)], "grad_qkv_rest", row_steps=2)
     sum0 = moves.scatter(g0, True)
     due = (*g0, *sum1.got, *sum2.got)
     sum0.step(*due)
     sends = (*sum1.step(*due), *sum2.step(*due))
     sends = (*sends, *sum0.step(*sends, *sum0.got))
-    parts = [t[part] for part in range(3) for t in (turned0, turned1, turned2)]
+    parts = [t[part] for part in range(3) for t in (turned0, turned1)]
     grad_input = input_grad(tab, w1, after(x, *g0, *sends), grad_middle, parts, halves)
     sums = (sum0, sum1, sum2, sum3)
     due = (grad_input, *sum2.got, *sum1.got, *sum0.got)
@@ -1090,12 +1150,14 @@
     scale = 1.0 / (batch_size * replicas * members)
     down = columns(s3, 0, width)
     gate, up = columns(s2, 0, inner), columns(s2, inner, inner)
-    third = width // GROUPS
-    out = columns(s1, 6 * third, width)
+    shares = [width * count // sum(SPLIT) for count in SPLIT]
+    out = columns(s1, 3 * shares[0], width)
 
     def head_columns(part):
-        sources = [columns(s, start * third, third) for s, start in ((s1, part), (s1, part + 3), (s0, part))]
-        return jnp.concatenate([c[:, j * 128 : (j + 1) * 128] for j in range(2) for c in sources], 1)
+        sources = [columns(s, part * share, share) for s, share in zip((s1, s0), shares)]
+        return jnp.concatenate(
+            [c[:, j * c.shape[1] // 2 : (j + 1) * c.shape[1] // 2] for j in range(2) for c in sources], 1
+        )
 
     query, key, value = (head_columns(part) for part in range(3))
 

time: 328 us -> 310 us (0.945); the launches traced: 323 us -> 309 us
  Pallas kernels: 174 us -> 160 us
  waiting for transfers between devices: 36.9 us -> 46 us
  local copies, waits for them, and re-layouts: 10.5 us -> 4.89 us
    pallas_call x6 -> x3, Pallas kernels: 56.2 us -> 44.7 us  [the longest x2 27 us: attend_back(): pl.pallas_call(attend_back_kernel, grid=(pairs,), in_specs=[column] * 5 +...]
    ppermute x65, waiting for transfers between devices: 36.9 us -> 46 us  [swapped(): return lambda array: lax.ppermute(array, axis, pairs)]
    unnamed x116 -> x83, local copies, waits for them, and re-layouts: 6.79 us -> 1.93 us
  transfers between devices with their start and end apart: 65 -> 65, of which waited for: 15 -> 22; matrix products, arithmetic and copies ran while one was open for 9% -> 9% of each run, Pallas kernels for 53% -> 51%
where the time goes in v3:
time: 310 us; the launch traced here: 309 us
  Pallas kernels  160 us (52%)
  starting transfers between devices  60.4 us (19%)
  waiting for transfers between devices  46 us (15%)
  other arithmetic  36.4 us (12%)
  local copies, waits for them, and re-layouts  4.89 us (2%)
    ppermute x65, starting transfers between devices, swapped(): return lambda array: lax.ppermute(array, axis, pairs)  60.4 us
    ppermute x65, waiting for transfers between devices, swapped(): return lambda array: lax.ppermute(array, axis, pairs)  46 us
    pallas_call x4, Pallas kernels, weight_grad(): pl.pallas_call(functools.partial(weight_kernel, counts=counts, block_rows...  35.6 us
    pallas_call x2, Pallas kernels, attend_back(): pl.pallas_call(attend_back_kernel, grid=(pairs,), in_specs=[column] * 5 +...  27 us
    convert_element_type x18, other arithmetic, add(): return total.astype(bf16)  24.3 us
    pallas_call x1, Pallas kernels, middle_back(): pl.pallas_call(functools.partial(middle_back_kernel, n_pieces=n, halves=h...  19.2 us
    pallas_call x1, Pallas kernels, attend(): pl.pallas_call(attend_kernel, grid=(pairs,), in_specs=[column, column, co...  17.6 us
    pallas_call x1, Pallas kernels, ffn(): pl.pallas_call(functools.partial(ffn_kernel, n_pieces=n, halves=halves),...  17.6 us
  transfers between devices with their start and end apart: 65, of which 22 were waited for; matrix products, arithmetic and copies ran while one was open for 9% of the time, Pallas kernels for 51%

profile of v3, /device:TPU:0, one launch (start us, length us, event | category | flops | bytes accessed | tf_op | source)
XLA Modules:
  0.0 309.0 jit_solution(6328341728148024934)
XLA Ops:
  3.5 5.0 %collective-permute-start.2 = (bf16[1,48,1152]{2,1,0:T(8,128)(2,1)}, bf16[1,48,1152]{2,1,0:T(8,128)(2,1)S(1)}, u32[]{:S(2)}, u32[]{:S(2)}) collective-permute-start(bf16[1,48,1152]{2,1,0:T(8,128)(2,1)} %bitcast.59), channel_id=1, source_target_pairs={{0,12},{1,13},{2,14},{3,15},{4,8},{5,9},{6,10},{7,11},{8,4},{9,5},... | collective-permute-start | bytes 331784 | tf_op jit(solution)/shard_map/ppermute | solution.py:814
  15.5 2.6 collective-permute-done.1
  21.7 3.0 collective-permute-done.8
  28.9 2.4 collective-permute-start.5
  31.4 7.2 %collective-permute-done.5 = bf16[1,48,2432]{2,1,0:T(8,128)(2,1)S(1)} collective-permute-done((bf16[1,48,2432]{2,1,0:T(8,128)(2,1)S(1)}, bf16[1,48,2432]{2,1,0:T(8,128)(2,1)S(1)}, u32[]{:S(2)}, u32[]{:S(2)}) %collective-permute-start.5) | collective-permute-done | bytes 233504 | tf_op jit(solution)/shard_map/ppermute | solution.py:814
  39.1 9.6 %collective-permute-done.4 = bf16[1,48,2432]{2,1,0:T(8,128)(2,1)S(1)} collective-permute-done((bf16[1,48,2432]{2,1,0:T(8,128)(2,1)S(1)}, bf16[1,48,2432]{2,1,0:T(8,128)(2,1)S(1)}, u32[]{:S(2)}, u32[]{:S(2)}) %collective-permute-start.4) | collective-permute-done | bytes 233504 | tf_op jit(solution)/shard_map/ppermute | solution.py:814
  53.4 10.8 %project.1 = (bf16[1024,768]{1,0:T(8,128)(2,1)}, bf16[1024,768]{1,0:T(8,128)(2,1)}, bf16[1024,768]{1,0:T(8,128)(2,1)}, bf16[1024,768]{1,0:T(8,128)(2,1)}) custom-call(s32[2,32]{1,0:T(2,128)} %pad_add_fusion.tab_ref, bf16[4,48,1152]{2,1,0:T(8,128)(2,1)} %copy-done.1, bf16[4,48,1152]{2,1,0:T(8,128)(2,1)} %copy-done.13, bf16[4,48,1152]{2,1,0:T(8,128)(2,1)} %copy-done.8, ...), custom_call_target="tpu_custom_call" | custom-call | flops 3623878656 | bytes 12582912 | tf_op jit(solution)/shard_map/project/pallas_call | solution.py:194
  67.2 2.6 collective-permute-start.17
  69.8 17.6 %attend.1 = (bf16[1024,768]{1,0:T(8,128)(2,1)}, f32[1024,768]{1,0:T(8,128)}, bf16[12,4,256,768]{3,2,1,0:T(8,128)(2,1)}) custom-call(bf16[1024,768]{1,0:T(8,128)(2,1)} %get-tuple-element.103.q_ref, bf16[1024,768]{1,0:T(8,128)(2,1)} %get-tuple-element.104.k_ref, bf16[1024,768]{1,0:T(8,128)(2,1)} %get-tuple-element.105.v_ref, ...), custom_call_target="tpu_custom_call" | custom-call | flops 8053063680 | bytes 23592960 | tf_op jit(solution)/shard_map/attend/pallas_call | solution.py:298
  89.3 5.1 %collective-permute-done.22 = bf16[2,128,384]{2,1,0:T(8,128)(2,1)S(1)} collective-permute-done((bf16[2,128,384]{2,1,0:T(8,128)(2,1)S(1)}, bf16[2,128,384]{2,1,0:T(8,128)(2,1)S(1)}, u32[]{:S(2)}, u32[]{:S(2)}) %collective-permute-start.22) | collective-permute-done | bytes 196640 | tf_op jit(solution)/shard_map/ppermute | solution.py:814
  98.9 17.6 %ffn.1 = (f32[1024,768]{1,0:T(8,128)}, bf16[1024,768]{1,0:T(8,128)(2,1)}, bf16[1024,2048]{1,0:T(8,128)(2,1)}, bf16[1024,2048]{1,0:T(8,128)(2,1)}, bf16[1024,2048]{1,0:T(8,128)(2,1)}) custom-call(s32[2,32]{1,0:T(2,128)} %pad_add_fusion.tab_ref, bf16[4,48,2432]{2,1,0:T(8,128)(2,1)} %copy-done.22, bf16[4,48,2432]{2,1,0:T(8,128)(2,1)} %copy-done.30, ...), custom_call_target="tpu_custom_call" | custom-call | flops 7650410496 | bytes 29360128 | tf_op jit(solution)/shard_map/ffn/pallas_call | solution.py:475
  118.3 8.2 %grad_down.1 = (bf16[16,128,384]{2,1,0:T(8,128)(2,1)}, bf16[16,128,384]{2,1,0:T(8,128)(2,1)}) custom-call(s32[32]{0:T(128)} %add.401.tab_ref, bf16[1024,2048]{1,0:T(8,128)(2,1)} %get-tuple-element.126.refs_0_.refs_9_, bf16[1024,768]{1,0:T(8,128)(2,1)} %bitcast.71), custom_call_target="tpu_custom_call" | custom-call | flops 3221225472 | bytes 8912896 | tf_op jit(solution)/shard_map/grad_down/pallas_call | solution.py:774
  127.6 15.3 %hidden_back.1 = (bf16[1024,768]{1,0:T(8,128)(2,1)}, bf16[1024,2048]{1,0:T(8,128)(2,1)}, bf16[1024,2048]{1,0:T(8,128)(2,1)}) custom-call(s32[2,32]{1,0:T(2,128)} %pad_add_fusion.tab_ref, bf16[4,128,384]{2,1,0:T(8,128)(2,1)} %copy-done.26, bf16[4,128,384]{2,1,0:T(8,128)(2,1)} %copy-done.34, bf16[4,128,384]{2,1,0:T(8,128)(2,1)} %copy-done.25, ...), custom_call_target="tpu_custom_call" | custom-call | flops 6442450944 | bytes 28311552 | tf_op jit(solution)/shard_map/hidden_back/pallas_call | solution.py:529
  145.3 12.6 %grad_gate_up.1 = (bf16[16,48,2048]{2,1,0:T(8,128)(2,1)}, bf16[16,48,2048]{2,1,0:T(8,128)(2,1)}) custom-call(s32[32]{0:T(128)} %add.401.tab_ref, bf16[1024,768]{1,0:T(8,128)(2,1)} %get-tuple-element.135.refs_0_, bf16[1024,2048]{1,0:T(8,128)(2,1)} %get-tuple-element.132.refs_1_.refs_9_, bf16[1024,2048]{1,0:T(8,128)(2,1)} %get-tuple-element.136.refs_2_.refs_10_), custom_call_target="tpu_custom_call" | custom-call | flops 6442450944 | bytes 16252928 | tf_op jit(solution)/shard_map/grad_gate_up/pallas_call | solution.py:774
  162.3 19.2 %middle_back.1 = (f32[1024,768]{1,0:T(8,128)}, bf16[1024,768]{1,0:T(8,128)(2,1)}, bf16[1024,768]{1,0:T(8,128)(2,1)}) custom-call(s32[2,32]{1,0:T(2,128)} %pad_add_fusion.tab_ref, bf16[4,48,2432]{2,1,0:T(8,128)(2,1)} %copy-done.22, bf16[4,48,2432]{2,1,0:T(8,128)(2,1)} %copy-done.30, bf16[4,48,2432]{2,1,0:T(8,128)(2,1)} %copy-done.21, ...), custom_call_target="tpu_custom_call" | custom-call | flops 7650410496 | bytes 14680064 | tf_op jit(solution)/shard_map/middle_back/pallas_call | solution.py:602
  183.7 3.2 %add_convert_fusion = (bf16[4,48,2048]{2,1,0:T(8,128)(2,1)}, bf16[4,48,2048]{2,1,0:T(8,128)(2,1)}) fusion(bf16[16,48,2048]{2,1,0:T(8,128)(2,1)S(1)} %collective-permute-done.37, bf16[16,48,2048]{2,1,0:T(8,128)(2,1)} %get-tuple-element.173), kind=kLoop, calls=%fused_computation | loop fusion | flops 3145728 | bytes 4718592 | tf_op jit(solution)/shard_map/convert_element_type | solution.py:936
  188.8 16.5 %attend_back.2 = (bf16[1024,512]{1,0:T(8,128)(2,1)}, bf16[1024,512]{1,0:T(8,128)(2,1)}, bf16[1024,512]{1,0:T(8,128)(2,1)}) custom-call(bf16[1024,768]{1,0:T(8,128)(2,1)} %get-tuple-element.103.q_ref, bf16[1024,768]{1,0:T(8,128)(2,1)} %get-tuple-element.104.k_ref, bf16[1024,768]{1,0:T(8,128)(2,1)} %get-tuple-element.105.v_ref, ...), custom_call_target="tpu_custom_call" | custom-call | flops 10737418240 | bytes 18874368 | tf_op jit(solution)/shard_map/attend_back/pallas_call | solution.py:403
  213.9 9.6 %grad_qk_out.1 = (bf16[16,48,1152]{2,1,0:T(8,128)(2,1)}, bf16[16,48,1152]{2,1,0:T(8,128)(2,1)}) custom-call(s32[32]{0:T(128)} %add.401.tab_ref, bf16[1024,768]{1,0:T(8,128)(2,1)} %get-tuple-element.167.refs_0_, bf16[1024,768]{1,0:T(8,128)(2,1)} %get-tuple-element.109.refs_9_.mixed_ref.refs_1_, bf16[1024,512]{1,0:T(8,128)(2,1)} %get-tuple-element.150.refs_2_.refs_10_, ...), custom_call_target="tpu_custom_call" | custom-call | flops 3623878656 | bytes 9830400 | tf_op jit(solution)/shard_map/grad_qk_out/pallas_call | solution.py:774
  225.8 2.2 add_convert_fusion.4
  230.3 2.3 add_convert_fusion.2
  234.9 10.5 %attend_back.3 = (bf16[1024,256]{1,0:T(8,128)(2,1)}, bf16[1024,256]{1,0:T(8,128)(2,1)}, bf16[1024,256]{1,0:T(8,128)(2,1)}) custom-call(bf16[1024,768]{1,0:T(8,128)(2,1)} %get-tuple-element.103.q_ref, bf16[1024,768]{1,0:T(8,128)(2,1)} %get-tuple-element.104.k_ref, bf16[1024,768]{1,0:T(8,128)(2,1)} %get-tuple-element.105.v_ref, ...), custom_call_target="tpu_custom_call" | custom-call | flops 5368709120 | bytes 9437184 | tf_op jit(solution)/shard_map/attend_back/pallas_call | solution.py:403
  245.5 3.3 %collective-permute-done.47 = bf16[2,48,2048]{2,1,0:T(8,128)(2,1)} collective-permute-done((bf16[2,48,2048]{2,1,0:T(8,128)(2,1)}, bf16[2,48,2048]{2,1,0:T(8,128)(2,1)}, u32[]{:S(2)}, u32[]{:S(2)}) %collective-permute-start.47) | collective-permute-done | bytes 393248 | tf_op jit(solution)/shard_map/ppermute | solution.py:814
  248.8 2.2 fusion.7
  251.0 2.2 add_convert_fusion.10
  255.9 5.2 %grad_qkv_rest.1 = (bf16[16,48,384]{2,1,0:T(8,128)(2,1)}, bf16[16,48,384]{2,1,0:T(8,128)(2,1)}) custom-call(s32[32]{0:T(128)} %add.401.tab_ref, bf16[1024,768]{1,0:T(8,128)(2,1)} %get-tuple-element.167.refs_0_, bf16[1024,256]{1,0:T(8,128)(2,1)} %get-tuple-element.164.refs_1_.refs_11_, bf16[1024,256]{1,0:T(8,128)(2,1)} %get-tuple-element.168.refs_2_.refs_13_, ...), custom_call_target="tpu_custom_call" | custom-call | flops 1207959552 | bytes 4325376 | tf_op jit(solution)/shard_map/grad_qkv_rest/pallas_call | solution.py:774
  265.4 2.5 collective-permute-start.53
  272.6 11.5 %input_grad.1 = f32[1024,768]{1,0:T(8,128)} custom-call(s32[2,32]{1,0:T(2,128)} %pad_add_fusion.tab_ref, bf16[4,48,1152]{2,1,0:T(8,128)(2,1)} %copy-done.1, bf16[4,48,1152]{2,1,0:T(8,128)(2,1)} %copy-done.13, bf16[4,48,1152]{2,1,0:T(8,128)(2,1)} %copy-done.8, bf16[4,48,1152]{2,1,0:T(8,128)(2,1)} %copy-done.12, ...), custom_call_target="tpu_custom_call" | custom-call | flops 3623878656 | bytes 15728640 | tf_op jit(solution)/shard_map/input_grad/pallas_call | solution.py:656
  286.7 1.9 collective-permute-done.58
  289.8 2.3 collective-permute-start.61
  292.1 1.9 collective-permute-start.62
  295.1 2.1 collective-permute-start.56
  302.5 3.3 %collective-permute-done.57 = bf16[48,1152]{1,0:T(8,128)(2,1)S(1)} collective-permute-done((bf16[48,1152]{1,0:T(8,128)(2,1)S(1)}, bf16[48,1152]{1,0:T(8,128)(2,1)S(1)}, u32[]{:S(2)}, u32[]{:S(2)}) %collective-permute-start.57) | collective-permute-done | bytes 110624 | tf_op jit(solution)/shard_map/ppermute | solution.py:814
  (276 shorter events, 85.8 us)
Async XLA Ops:
  24.7 13.9 %collective-permute-start.9 = (bf16[4,48,1152]{2,1,0:T(8,128)(2,1)S(1)}, bf16[4,48,1152]{2,1,0:T(8,128)(2,1)S(1)}, u32[]{:S(2)}, u32[]{:S(2)}) collective-permute-start(bf16[4,48,1152]{2,1,0:T(8,128)(2,1)S(1)} %constant_dynamic-update-slice_fusion.refs_2_), channel_id=1, source_target_pairs={{0,2},{1,3},{2,0},{3,1},{4,6},{5,7},{6,4},{7,5},{8,10},{9,11},{10,... | collective-permute-start | bytes 1327112 | tf_op jit(solution)/shard_map/ppermute | solution.py:814
  26.4 12.6 %collective-permute-start.7 = (bf16[4,48,1152]{2,1,0:T(8,128)(2,1)S(1)}, bf16[4,48,1152]{2,1,0:T(8,128)(2,1)S(1)}, u32[]{:S(2)}, u32[]{:S(2)}) collective-permute-start(bf16[4,48,1152]{2,1,0:T(8,128)(2,1)S(1)} %pad_maximum_fusion.2.refs_0_), channel_id=1, source_target_pairs={{0,16},{16,0},{1,17},{17,1},{2,18},{18,2},{3,19},{19,3},{4,20},{20... | collective-permute-start | bytes 1327112 | tf_op jit(solution)/shard_map/ppermute | solution.py:814
  31.3 17.4 %collective-permute-start.4 = (bf16[1,48,2432]{2,1,0:T(8,128)(2,1)S(1)}, bf16[1,48,2432]{2,1,0:T(8,128)(2,1)S(1)}, u32[]{:S(2)}, u32[]{:S(2)}) collective-permute-start(bf16[1,48,2432]{2,1,0:T(8,128)(2,1)S(1)} %bitcast.66), channel_id=1, source_target_pairs={{0,8},{1,9},{2,10},{3,11},{4,12},{5,13},{6,14},{7,15},{8,0},{9,1},... | collective-permute-start | bytes 700424 | tf_op jit(solution)/shard_map/ppermute | solution.py:814
  31.3 18.1 %collective-permute-start.12 = (bf16[4,48,1152]{2,1,0:T(8,128)(2,1)S(1)}, bf16[4,48,1152]{2,1,0:T(8,128)(2,1)}, u32[]{:S(2)}, u32[]{:S(2)}) collective-permute-start(bf16[4,48,1152]{2,1,0:T(8,128)(2,1)S(1)} %constant_dynamic-update-slice_fusion.refs_2_), channel_id=1, source_target_pairs={{0,1},{1,0},{2,3},{3,2},{4,5},{5,4},{6,7},{7,6},{8,9},{9,8},{10,11... | collective-permute-start | bytes 1327112 | tf_op jit(solution)/shard_map/ppermute | solution.py:814
  38.5 14.8 %collective-permute-start.10 = (bf16[4,48,1152]{2,1,0:T(8,128)(2,1)S(1)}, bf16[4,48,1152]{2,1,0:T(8,128)(2,1)}, u32[]{:S(2)}, u32[]{:S(2)}) collective-permute-start(bf16[4,48,1152]{2,1,0:T(8,128)(2,1)S(1)} %pad_maximum_fusion.2.refs_0_), channel_id=1, source_target_pairs={{0,1},{1,0},{2,3},{3,2},{4,5},{5,4},{6,7},{7,6},{8,9},{9,8},{10,11... | collective-permute-start | bytes 1327112 | tf_op jit(solution)/shard_map/ppermute | solution.py:814
  38.5 14.8 %collective-permute-start.13 = (bf16[4,48,1152]{2,1,0:T(8,128)(2,1)S(1)}, bf16[4,48,1152]{2,1,0:T(8,128)(2,1)}, u32[]{:S(2)}, u32[]{:S(2)}) collective-permute-start(bf16[4,48,1152]{2,1,0:T(8,128)(2,1)S(1)} %collective-permute-done.9.refs_3_), channel_id=1, source_target_pairs={{0,1},{1,0},{2,3},{3,2},{4,5},{5,4},{6,7},{7,6},{8,9},{9,8},{10,11... | collective-permute-start | bytes 1327112 | tf_op jit(solution)/shard_map/ppermute | solution.py:814
  39.1 14.3 %collective-permute-start.11 = (bf16[4,48,1152]{2,1,0:T(8,128)(2,1)S(1)}, bf16[4,48,1152]{2,1,0:T(8,128)(2,1)}, u32[]{:S(2)}, u32[]{:S(2)}) collective-permute-start(bf16[4,48,1152]{2,1,0:T(8,128)(2,1)S(1)} %collective-permute-done.7.refs_1_), channel_id=1, source_target_pairs={{0,1},{1,0},{2,3},{3,2},{4,5},{5,4},{6,7},{7,6},{8,9},{9,8},{10,11... | collective-permute-start | bytes 1327112 | tf_op jit(solution)/shard_map/ppermute | solution.py:814
  48.8 15.5 %collective-permute-start.16 = (bf16[2,48,2432]{2,1,0:T(8,128)(2,1)S(1)}, bf16[2,48,2432]{2,1,0:T(8,128)(2,1)S(1)}, u32[]{:S(2)}, u32[]{:S(2)}) collective-permute-start(bf16[2,48,2432]{2,1,0:T(8,128)(2,1)S(1)} %pad_maximum_fusion.1), channel_id=1, source_target_pairs={{0,16},{16,0},{1,17},{17,1},{2,18},{18,2},{3,19},{19,3},{4,20},{20... | collective-permute-start | bytes 1400840 | tf_op jit(solution)/shard_map/ppermute | solution.py:814
  49.4 14.8 %collective-permute-start.15 = (bf16[2,48,2432]{2,1,0:T(8,128)(2,1)S(1)}, bf16[2,48,2432]{2,1,0:T(8,128)(2,1)S(1)}, u32[]{:S(2)}, u32[]{:S(2)}) collective-permute-start(bf16[2,48,2432]{2,1,0:T(8,128)(2,1)S(1)} %pad_maximum_fusion), channel_id=1, source_target_pairs={{0,2},{1,3},{2,0},{3,1},{4,6},{5,7},{6,4},{7,5},{8,10},{9,11},{10,... | collective-permute-start | bytes 1400840 | tf_op jit(solution)/shard_map/ppermute | solution.py:814
  64.4 24.9 %collective-permute-start.21 = (bf16[4,48,2432]{2,1,0:T(8,128)(2,1)S(1)}, bf16[4,48,2432]{2,1,0:T(8,128)(2,1)}, u32[]{:S(2)}, u32[]{:S(2)}) collective-permute-start(bf16[4,48,2432]{2,1,0:T(8,128)(2,1)S(1)} %constant_dynamic-update-slice_fusion.7.refs_2_), channel_id=1, source_target_pairs={{0,2},{1,3},{2,0},{3,1},{4,6},{5,7},{6,4},{7,5},{8,10},{9,11},{10,... | collective-permute-start | bytes 2801672 | tf_op jit(solution)/shard_map/ppermute | solution.py:814
  65.3 22.1 %collective-permute-start.19 = (bf16[4,48,2432]{2,1,0:T(8,128)(2,1)S(1)}, bf16[4,48,2432]{2,1,0:T(8,128)(2,1)}, u32[]{:S(2)}, u32[]{:S(2)}) collective-permute-start(bf16[4,48,2432]{2,1,0:T(8,128)(2,1)S(1)} %constant_dynamic-update-slice_fusion.7.refs_2_), channel_id=1, source_target_pairs={{0,1},{1,0},{2,3},{3,2},{4,5},{5,4},{6,7},{7,6},{8,9},{9,8},{10,11... | collective-permute-start | bytes 2801672 | tf_op jit(solution)/shard_map/ppermute | solution.py:814
  65.4 23.8 %collective-permute-start.20 = (bf16[4,48,2432]{2,1,0:T(8,128)(2,1)S(1)}, bf16[4,48,2432]{2,1,0:T(8,128)(2,1)S(1)}, u32[]{:S(2)}, u32[]{:S(2)}) collective-permute-start(bf16[4,48,2432]{2,1,0:T(8,128)(2,1)S(1)} %constant_dynamic-update-slice_fusion.5.refs_0_), channel_id=1, source_target_pairs={{0,16},{16,0},{1,17},{17,1},{2,18},{18,2},{3,19},{19,3},{4,20},{20... | collective-permute-start | bytes 2801672 | tf_op jit(solution)/shard_map/ppermute | solution.py:814
  66.9 20.5 %collective-permute-start.18 = (bf16[4,48,2432]{2,1,0:T(8,128)(2,1)S(1)}, bf16[4,48,2432]{2,1,0:T(8,128)(2,1)}, u32[]{:S(2)}, u32[]{:S(2)}) collective-permute-start(bf16[4,48,2432]{2,1,0:T(8,128)(2,1)S(1)} %constant_dynamic-update-slice_fusion.5.refs_0_), channel_id=1, source_target_pairs={{0,1},{1,0},{2,3},{3,2},{4,5},{5,4},{6,7},{7,6},{8,9},{9,8},{10,11... | collective-permute-start | bytes 2801672 | tf_op jit(solution)/shard_map/ppermute | solution.py:814
  67.2 20.2 %collective-permute-start.17 = (bf16[2,128,384]{2,1,0:T(8,128)(2,1)S(1)}, bf16[2,128,384]{2,1,0:T(8,128)(2,1)S(1)}, u32[]{:S(2)}, u32[]{:S(2)}) collective-permute-start(bf16[2,128,384]{2,1,0:T(8,128)(2,1)S(1)} %constant_dynamic-update-slice_fusion.3), channel_id=1, source_target_pairs={{0,8},{1,9},{2,10},{3,11},{4,12},{5,13},{6,14},{7,15},{8,0},{9,1},... | collective-permute-start | bytes 589832 | tf_op jit(solution)/shard_map/ppermute | solution.py:814
  95.3 21.2 %collective-permute-start.27 = (bf16[4,128,384]{2,1,0:T(8,128)(2,1)S(1)}, bf16[4,128,384]{2,1,0:T(8,128)(2,1)S(1)}, u32[]{:S(2)}, u32[]{:S(2)}) collective-permute-start(bf16[4,128,384]{2,1,0:T(8,128)(2,1)S(1)} %constant_dynamic-update-slice_fusion.11.refs_2_), channel_id=1, source_target_pairs={{0,2},{1,3},{2,0},{3,1},{4,6},{5,7},{6,4},{7,5},{8,10},{9,11},{10,... | collective-permute-start | bytes 1179656 | tf_op jit(solution)/shard_map/ppermute | solution.py:814
  96.9 19.6 %collective-permute-start.26 = (bf16[4,128,384]{2,1,0:T(8,128)(2,1)S(1)}, bf16[4,128,384]{2,1,0:T(8,128)(2,1)S(1)}, u32[]{:S(2)}, u32[]{:S(2)}) collective-permute-start(bf16[4,128,384]{2,1,0:T(8,128)(2,1)S(1)} %constant_dynamic-update-slice_fusion.9.refs_0_), channel_id=1, source_target_pairs={{0,16},{16,0},{1,17},{17,1},{2,18},{18,2},{3,19},{19,3},{4,20},{20... | collective-permute-start | bytes 1179656 | tf_op jit(solution)/shard_map/ppermute | solution.py:814
  127.3 15.6 %collective-permute-start.32 = (bf16[16,128,384]{2,1,0:T(8,128)(2,1)}, bf16[16,128,384]{2,1,0:T(8,128)(2,1)S(1)}, u32[]{:S(2)}, u32[]{:S(2)}) collective-permute-start(bf16[16,128,384]{2,1,0:T(8,128)(2,1)} %get-tuple-element.133), channel_id=1, source_target_pairs={{0,1},{1,0},{2,3},{3,2},{4,5},{5,4},{6,7},{7,6},{8,9},{9,8},{10,11... | collective-permute-start | bytes 4718600 | tf_op jit(solution)/shard_map/ppermute | solution.py:814
  143.2 14.8 %collective-permute-start.34 = (bf16[4,128,384]{2,1,0:T(8,128)(2,1)S(1)}, bf16[4,128,384]{2,1,0:T(8,128)(2,1)S(1)}, u32[]{:S(2)}, u32[]{:S(2)}) collective-permute-start(bf16[4,128,384]{2,1,0:T(8,128)(2,1)S(1)} %get-tuple-element.191), channel_id=1, source_target_pairs={{0,2},{1,3},{2,0},{3,1},{4,6},{5,7},{6,4},{7,5},{8,10},{9,11},{10,... | collective-permute-start | bytes 1179656 | tf_op jit(solution)/shard_map/ppermute | solution.py:814
  144.8 13.2 %collective-permute-start.33 = (bf16[4,128,384]{2,1,0:T(8,128)(2,1)S(1)}, bf16[4,128,384]{2,1,0:T(8,128)(2,1)S(1)}, u32[]{:S(2)}, u32[]{:S(2)}) collective-permute-start(bf16[4,128,384]{2,1,0:T(8,128)(2,1)S(1)} %get-tuple-element.192), channel_id=1, source_target_pairs={{0,16},{16,0},{1,17},{17,1},{2,18},{18,2},{3,19},{19,3},{4,20},{20... | collective-permute-start | bytes 1179656 | tf_op jit(solution)/shard_map/ppermute | solution.py:814
  158.9 22.7 %collective-permute-start.37 = (bf16[16,48,2048]{2,1,0:T(8,128)(2,1)}, bf16[16,48,2048]{2,1,0:T(8,128)(2,1)S(1)}, u32[]{:S(2)}, u32[]{:S(2)}) collective-permute-start(bf16[16,48,2048]{2,1,0:T(8,128)(2,1)} %get-tuple-element.141), channel_id=1, source_target_pairs={{0,1},{1,0},{2,3},{3,2},{4,5},{5,4},{6,7},{7,6},{8,9},{9,8},{10,11... | collective-permute-start | bytes 9437192 | tf_op jit(solution)/shard_map/ppermute | solution.py:814
  160.4 21.2 %collective-permute-start.36 = (bf16[2,128,384]{2,1,0:T(8,128)(2,1)S(1)}, bf16[2,128,384]{2,1,0:T(8,128)(2,1)}, u32[]{:S(2)}, u32[]{:S(2)}) collective-permute-start(bf16[2,128,384]{2,1,0:T(8,128)(2,1)S(1)} %get-tuple-element.189), channel_id=1, source_target_pairs={{0,16},{16,0},{1,17},{17,1},{2,18},{18,2},{3,19},{19,3},{4,20},{20... | collective-permute-start | bytes 589832 | tf_op jit(solution)/shard_map/ppermute | solution.py:814
  161.8 19.7 %collective-permute-start.35 = (bf16[2,128,384]{2,1,0:T(8,128)(2,1)S(1)}, bf16[2,128,384]{2,1,0:T(8,128)(2,1)}, u32[]{:S(2)}, u32[]{:S(2)}) collective-permute-start(bf16[2,128,384]{2,1,0:T(8,128)(2,1)S(1)} %get-tuple-element.190), channel_id=1, source_target_pairs={{0,2},{1,3},{2,0},{3,1},{4,6},{5,7},{6,4},{7,5},{8,10},{9,11},{10,... | collective-permute-start | bytes 589832 | tf_op jit(solution)/shard_map/ppermute | solution.py:814
  182.8 22.6 %collective-permute-start.40 = (bf16[2,128,384]{2,1,0:T(8,128)(2,1)S(1)}, bf16[2,128,384]{2,1,0:T(8,128)(2,1)S(1)}, u32[]{:S(2)}, u32[]{:S(2)}) collective-permute-start(bf16[2,128,384]{2,1,0:T(8,128)(2,1)S(1)} %add_convert_fusion.13), channel_id=1, source_target_pairs={{0,8},{1,9},{2,10},{3,11},{4,12},{5,13},{6,14},{7,15},{8,0},{9,1},... | collective-permute-start | bytes 589832 | tf_op jit(solution)/shard_map/ppermute | solution.py:814
  186.9 19.4 %collective-permute-start.39 = (bf16[4,48,2048]{2,1,0:T(8,128)(2,1)}, bf16[4,48,2048]{2,1,0:T(8,128)(2,1)}, u32[]{:S(2)}, u32[]{:S(2)}) collective-permute-start(bf16[4,48,2048]{2,1,0:T(8,128)(2,1)} %get-tuple-element.183), channel_id=1, source_target_pairs={{0,2},{1,3},{2,0},{3,1},{4,6},{5,7},{6,4},{7,5},{8,10},{9,11},{10,... | collective-permute-start | bytes 2359304 | tf_op jit(solution)/shard_map/ppermute | solution.py:814
  188.0 19.1 %collective-permute-start.38 = (bf16[4,48,2048]{2,1,0:T(8,128)(2,1)}, bf16[4,48,2048]{2,1,0:T(8,128)(2,1)}, u32[]{:S(2)}, u32[]{:S(2)}) collective-permute-start(bf16[4,48,2048]{2,1,0:T(8,128)(2,1)} %get-tuple-element.184), channel_id=1, source_target_pairs={{0,16},{16,0},{1,17},{17,1},{2,18},{18,2},{3,19},{19,3},{4,20},{20... | collective-permute-start | bytes 2359304 | tf_op jit(solution)/shard_map/ppermute | solution.py:814
  209.0 14.6 %collective-permute-start.42 = (bf16[2,48,2048]{2,1,0:T(8,128)(2,1)S(1)}, bf16[2,48,2048]{2,1,0:T(8,128)(2,1)}, u32[]{:S(2)}, u32[]{:S(2)}) collective-permute-start(bf16[2,48,2048]{2,1,0:T(8,128)(2,1)S(1)} %get-tuple-element.181), channel_id=1, source_target_pairs={{0,16},{16,0},{1,17},{17,1},{2,18},{18,2},{3,19},{19,3},{4,20},{20... | collective-permute-start | bytes 1179656 | tf_op jit(solution)/shard_map/ppermute | solution.py:814
  209.9 13.7 %collective-permute-start.41 = (bf16[2,48,2048]{2,1,0:T(8,128)(2,1)S(1)}, bf16[2,48,2048]{2,1,0:T(8,128)(2,1)}, u32[]{:S(2)}, u32[]{:S(2)}) collective-permute-start(bf16[2,48,2048]{2,1,0:T(8,128)(2,1)S(1)} %get-tuple-element.182), channel_id=1, source_target_pairs={{0,2},{1,3},{2,0},{3,1},{4,6},{5,7},{6,4},{7,5},{8,10},{9,11},{10,... | collective-permute-start | bytes 1179656 | tf_op jit(solution)/shard_map/ppermute | solution.py:814
  228.1 20.8 %collective-permute-start.47 = (bf16[2,48,2048]{2,1,0:T(8,128)(2,1)}, bf16[2,48,2048]{2,1,0:T(8,128)(2,1)}, u32[]{:S(2)}, u32[]{:S(2)}) collective-permute-start(bf16[2,48,2048]{2,1,0:T(8,128)(2,1)} %add_convert_fusion.4), channel_id=1, source_target_pairs={{0,8},{1,9},{2,10},{3,11},{4,12},{5,13},{6,14},{7,15},{8,0},{9,1},... | collective-permute-start | bytes 1179656 | tf_op jit(solution)/shard_map/ppermute | solution.py:814
  232.5 16.3 %collective-permute-start.46 = (bf16[4,48,1152]{2,1,0:T(8,128)(2,1)}, bf16[4,48,1152]{2,1,0:T(8,128)(2,1)}, u32[]{:S(2)}, u32[]{:S(2)}) collective-permute-start(bf16[4,48,1152]{2,1,0:T(8,128)(2,1)} %get-tuple-element.187), channel_id=1, source_target_pairs={{0,2},{1,3},{2,0},{3,1},{4,6},{5,7},{6,4},{7,5},{8,10},{9,11},{10,... | collective-permute-start | bytes 1327112 | tf_op jit(solution)/shard_map/ppermute | solution.py:814
  233.5 15.4 %collective-permute-start.45 = (bf16[4,48,1152]{2,1,0:T(8,128)(2,1)}, bf16[4,48,1152]{2,1,0:T(8,128)(2,1)S(1)}, u32[]{:S(2)}, u32[]{:S(2)}) collective-permute-start(bf16[4,48,1152]{2,1,0:T(8,128)(2,1)} %get-tuple-element.188), channel_id=1, source_target_pairs={{0,16},{16,0},{1,17},{17,1},{2,18},{18,2},{3,19},{19,3},{4,20},{20... | collective-permute-start | bytes 1327112 | tf_op jit(solution)/shard_map/ppermute | solution.py:814
  265.4 18.8 %collective-permute-start.53 = (bf16[2,48,1152]{2,1,0:T(8,128)(2,1)S(1)}, bf16[2,48,1152]{2,1,0:T(8,128)(2,1)S(1)}, u32[]{:S(2)}, u32[]{:S(2)}) collective-permute-start(bf16[2,48,1152]{2,1,0:T(8,128)(2,1)S(1)} %add_convert_fusion.9), channel_id=1, source_target_pairs={{0,8},{1,9},{2,10},{3,11},{4,12},{5,13},{6,14},{7,15},{8,0},{9,1},... | collective-permute-start | bytes 663560 | tf_op jit(solution)/shard_map/ppermute | solution.py:814
  270.4 13.7 %collective-permute-start.55 = (bf16[4,48,384]{2,1,0:T(8,128)(2,1)S(1)}, bf16[4,48,384]{2,1,0:T(8,128)(2,1)S(1)}, u32[]{:S(2)}, u32[]{:S(2)}) collective-permute-start(bf16[4,48,384]{2,1,0:T(8,128)(2,1)S(1)} %get-tuple-element.198), channel_id=1, source_target_pairs={{0,2},{1,3},{2,0},{3,1},{4,6},{5,7},{6,4},{7,5},{8,10},{9,11},{10,... | collective-permute-start | bytes 442376 | tf_op jit(solution)/shard_map/ppermute | solution.py:814
  (71 other events, 695.5 us)

commit v4 on v3

--- a/solution.py
+++ b/solution.py
@@ -757,7 +757,7 @@
     columns = sum(r.shape[1] for r in rights) // halves
     kept = moves.kept
     sent = max(1, blocks - kept)
-    if halves == 1 and chunks == 0:
+    if blocks == 1 and chunks == 0:
         row_steps = 1
     steps = halves * chunks if chunks else row_steps
     here = 1 if chunks else halves
@@ -839,6 +839,16 @@
         rel_shard = jnp.array([o[0] for o in order], jnp.int32)
         rel_half = jnp.array([o[1] for o in order], jnp.int32)
         self.tab = jnp.stack([rel_shard ^ self.me, rel_half ^ self.x])
+        order = [(zr * 4 + yr * 2 + cr, xr) for cr in range(2) for xr in range(2) for yr in range(2) for zr in range(4)]
+        rel_shard = jnp.array([o[0] for o in order], jnp.int32)
+        rel_half = jnp.array([o[1] for o in order], jnp.int32)
+        self.tab3 = jnp.stack([rel_shard ^ self.me, rel_half ^ self.x])
+        rel = rel[:, 0]
+        self.wide = Wide(self, (rel & 1) * 8 + ((rel >> 1) & 1) * 4 + (rel >> 2))
+
+    def xy(self, array):
+        pairs = [(i, i ^ 18) for i in range(32)]
+        return lax.ppermute(array, ("rep", "shard"), pairs)
 
     def pack(self, arrays, gain):
         return pack(self.x, arrays, gain, 2)
@@ -887,22 +897,14 @@
         self.core2 = [self.core(a), None, self.core(b), None]
         return a, b, a3
 
-    def stage2(self, *deps):
-        deps = (*deps, self.b3, self.core2[0], self.core2[2])
-        self.a3, self.b3 = after(self.a3, *deps), after(self.b3, *deps)
-        self.pair3 = self.one_axis(self.a3, self.b3)
-        return self.a3, self.b3
-
     def stage3(self, *deps):
-        (a, ay), (b, bx) = self.pair3
-        deps = (*deps, *self.own2, ay, bx)
-        a = jnp.concatenate([after(a, *deps), ay], 0)
-        b = jnp.concatenate([after(b, *deps), bx], 0)
-        self.own3 = self.rest(a, b)
+        deps = (*deps, *self.own2, self.b3, self.core2[0], self.core2[2])
+        block = jnp.concatenate([after(self.a3, *deps), after(self.b3, *deps)], 0)
+        self.own3 = [block, self.y(block), self.x_move(block), self.xy(block)]
         for i in (1, 3):
-            self.core2[i] = self.core(after(self.own2[i], *deps, a, b))
+            self.core2[i] = self.core(after(self.own2[i], *deps, block))
         self.own2 += self.core2
-        return a, b
+        return (block,)
 
     def scatter(self, grads, direct=False):
         return Direct.Sum(self, grads, direct)
@@ -986,13 +988,61 @@
             return (own,)
 
 
+class Wide:
+    halves = 1
+    kept = 8
+
+    def __init__(self, moves, place):
+        self.moves, self.place = moves, place
+
+    def scatter(self, grads, direct=False):
+        return Wide.Sum(self.moves, grads, direct)
+
+    class Sum(Direct.Sum):
+        def __init__(self, moves, grads, direct):
+            super().__init__(moves, grads, direct)
+            self.steps = [s for s in self.steps if s != self.over_other]
+
+        def over_two(self):
+            send = self.add(self.keep[4:8], self.core[4:8])
+            self.by = self.moves.y(send)
+            self.got = (self.by,)
+            return (send,)
+
+        def over_z(self):
+            sends = tuple(self.add(self.keep[i], self.core[i], self.by[i]) for i in (1, 2, 3))
+            self.got = self.zs = tuple(move(send) for move, send in zip(self.moves.z, sends))
+            return sends
+
+        def over_z2(self):
+            send = self.add(self.keep[2:4], self.core[2:4], self.by[2:4])
+            self.z2 = self.moves.z[1](send)
+            self.got = (self.z2,)
+            return (send,)
+
+        def over_z1(self):
+            send = self.add(self.keep[1], self.core[1], self.by[1], self.z2[1])
+            z1 = self.moves.z[0](send)
+            self.zs = (self.z2[0], z1)
+            self.got = (z1,)
+            return (send,)
+
+        def over_x(self):
+            own = self.add(self.keep[0], self.core[0], self.by[0], *self.zs)
+            other = self.moves.x_move(own)
+            self.result = [own.astype(f32) + other.astype(f32)]
+            self.got = (other,)
+            return (own,)
+
+
 class Plain:
     halves = 1
     kept = 1
 
     def __init__(self):
         self.place = jnp.zeros((1,), jnp.int32)
-        self.tab = jnp.zeros((2, 1), jnp.int32)
+        self.tab = self.tab3 = jnp.zeros((2, 1), jnp.int32)
+        self.wide = self
 
     def pack(self, arrays, gain):
         return pack(jnp.int32(0), arrays, gain, 1)
@@ -1013,7 +1063,7 @@
     def stage1(self, *deps):
         return ()
 
-    stage2 = stage3 = stage1
+    stage3 = stage1
 
     def scatter(self, grads, direct=False):
         return Plain.Sum(grads)
@@ -1047,27 +1097,24 @@
     normed1, q, k, v = project(tab, w1, after(x, *sends), cosine, sine, halves)
     sends = moves.stage1(normed1)
     mixed, inv, exps = attend(q, k, v, after(q_marks, *sends), k_marks)
-    sends = moves.stage2(mixed)
-    sends = moves.stage3(mixed, *sends)
+    sends = moves.stage3(mixed)
     w2 = moves.own2
     middle, normed2, hidden, slope_g, slope_u = ffn(
         tab, w2, after(x, *sends), mixed, inner, halves
     )
     w3 = moves.with_core(moves.own3, hidden)
-    g3 = weight_grad(moves, [([after(hidden, *moves.own3)], [cot])], "grad_down", row_steps=4)
-    sum3 = moves.scatter(g3)
+    g3 = weight_grad(moves.wide, [([after(hidden, *moves.own3)], [cot])], "grad_down", row_steps=4)
+    sum3 = moves.wide.scatter(g3)
     sum3.step(*g3, *w3)
     output, gg, gu = hidden_back(
-        tab, w3, middle, after(hidden, *g3), slope_g, slope_u, cot, halves
+        moves.tab3, w3, middle, after(hidden, *g3), slope_g, slope_u, cot, halves
     )
     sends = sum3.step(gg, *sum3.got)
     g2 = weight_grad(moves, [([after(normed2, *sends)], [gg, gu])], "grad_gate_up", chunks=2)
     sum2 = moves.scatter(g2)
-    due = (*g2, *sum3.got)
-    sends = sum3.step(*due)
-    sends = (*sends, *sum2.step(*due))
+    sum2.step(*g2)
     grad_middle, attn_grad, grad_mixed = middle_back(
-        tab, w2, after(middle, *g2, *sends), gg, gu, cot, halves
+        tab, w2, after(middle, *g2), gg, gu, cot, halves
     )
     due = (attn_grad, *sum3.got, *sum2.got)
     sends = sum3.step(*due)
@@ -1095,8 +1142,8 @@
     due = (*turned1[:1], *sum1.got, *sum2.got)
     sends = sum1.step(*due)
     sends = (*sends, *sum2.step(*due))
-    g0 = weight_grad(moves, [([after(normed1, *sends)], turned1)], "grad_qkv_rest", row_steps=2)
-    sum0 = moves.scatter(g0, True)
+    g0 = weight_grad(moves.wide, [([after(normed1, *sends)], turned1)], "grad_qkv_rest", row_steps=2)
+    sum0 = moves.wide.scatter(g0, True)
     due = (*g0, *sum1.got, *sum2.got)
     sum0.step(*due)
     sends = (*sum1.step(*due), *sum2.step(*due))

time: 310 us -> 299 us (0.965)
  waiting for transfers between devices: 46 us -> 36.2 us
  starting transfers between devices: 60.4 us -> 56.6 us
    ppermute x65 -> x57, waiting for transfers between devices: 46 us -> 36.2 us  [swapped(): return lambda array: lax.ppermute(array, axis, pairs)]
    ppermute x65 -> x57, starting transfers between devices: 60.4 us -> 55.2 us  [swapped(): return lambda array: lax.ppermute(array, axis, pairs)]
    convert_element_type x18 -> x16, other arithmetic: 24.3 us -> 23.1 us  [add(): return total.astype(bf16)]
  transfers between devices with their start and end apart: 65 -> 58, of which waited for: 22 -> 16; matrix products, arithmetic and copies ran while one was open for 9% -> 11% of each run, Pallas kernels for 51% -> 49%
where the time goes in v4:
time: 299 us; the launch traced here: 297 us
  Pallas kernels  159 us (53%)
  starting transfers between devices  56.6 us (19%)
  other arithmetic  39 us (13%)
  waiting for transfers between devices  36.2 us (12%)
  local copies, waits for them, and re-layouts  4.93 us (2%)
    ppermute x57, starting transfers between devices, swapped(): return lambda array: lax.ppermute(array, axis, pairs)  55.2 us
    ppermute x57, waiting for transfers between devices, swapped(): return lambda array: lax.ppermute(array, axis, pairs)  36.2 us
    pallas_call x4, Pallas kernels, weight_grad(): pl.pallas_call(functools.partial(weight_kernel, counts=counts, block_rows...  35.2 us
    pallas_call x2, Pallas kernels, attend_back(): pl.pallas_call(attend_back_kernel, grid=(pairs,), in_specs=[column] * 5 +...  27.1 us
    convert_element_type x16, other arithmetic, add(): return total.astype(bf16)  23.1 us
    pallas_call x1, Pallas kernels, middle_back(): pl.pallas_call(functools.partial(middle_back_kernel, n_pieces=n, halves=h...  19.2 us
    pallas_call x1, Pallas kernels, attend(): pl.pallas_call(attend_kernel, grid=(pairs,), in_specs=[column, column, co...  17.6 us
    pallas_call x1, Pallas kernels, ffn(): pl.pallas_call(functools.partial(ffn_kernel, n_pieces=n, halves=halves),...  17.5 us
  transfers between devices with their start and end apart: 58, of which 16 were waited for; matrix products, arithmetic and copies ran while one was open for 11% of the time, Pallas kernels for 49%

profile of v4, /device:TPU:0, one launch (start us, length us, event | category | flops | bytes accessed | tf_op | source)
XLA Modules:
  0.0 297.3 jit_solution(17491657592223985870)
XLA Ops:
  3.5 5.0 %collective-permute-start.2 = (bf16[1,48,1152]{2,1,0:T(8,128)(2,1)}, bf16[1,48,1152]{2,1,0:T(8,128)(2,1)S(1)}, u32[]{:S(2)}, u32[]{:S(2)}) collective-permute-start(bf16[1,48,1152]{2,1,0:T(8,128)(2,1)} %bitcast.63), channel_id=1, source_target_pairs={{0,12},{1,13},{2,14},{3,15},{4,8},{5,9},{6,10},{7,11},{8,4},{9,5},... | collective-permute-start | bytes 331784 | tf_op jit(solution)/shard_map/ppermute | solution.py:814
  15.5 2.6 collective-permute-done.1
  21.7 3.0 %collective-permute-done.8 = bf16[2,48,1152]{2,1,0:T(8,128)(2,1)S(1)} collective-permute-done((bf16[2,48,1152]{2,1,0:T(8,128)(2,1)S(1)}, bf16[2,48,1152]{2,1,0:T(8,128)(2,1)S(1)}, u32[]{:S(2)}, u32[]{:S(2)}) %collective-permute-start.8) | collective-permute-done | bytes 221216 | tf_op jit(solution)/shard_map/ppermute | solution.py:814
  28.9 2.4 collective-permute-start.5
  31.4 7.2 %collective-permute-done.5 = bf16[1,48,2432]{2,1,0:T(8,128)(2,1)S(1)} collective-permute-done((bf16[1,48,2432]{2,1,0:T(8,128)(2,1)S(1)}, bf16[1,48,2432]{2,1,0:T(8,128)(2,1)S(1)}, u32[]{:S(2)}, u32[]{:S(2)}) %collective-permute-start.5) | collective-permute-done | bytes 233504 | tf_op jit(solution)/shard_map/ppermute | solution.py:814
  39.1 9.6 %collective-permute-done.4 = bf16[1,48,2432]{2,1,0:T(8,128)(2,1)S(1)} collective-permute-done((bf16[1,48,2432]{2,1,0:T(8,128)(2,1)S(1)}, bf16[1,48,2432]{2,1,0:T(8,128)(2,1)S(1)}, u32[]{:S(2)}, u32[]{:S(2)}) %collective-permute-start.4) | collective-permute-done | bytes 233504 | tf_op jit(solution)/shard_map/ppermute | solution.py:814
  53.4 10.8 %project.1 = (bf16[1024,768]{1,0:T(8,128)(2,1)}, bf16[1024,768]{1,0:T(8,128)(2,1)}, bf16[1024,768]{1,0:T(8,128)(2,1)}, bf16[1024,768]{1,0:T(8,128)(2,1)}) custom-call(s32[2,32]{1,0:T(2,128)} %pad_add_fusion.1.tab_ref, bf16[4,48,1152]{2,1,0:T(8,128)(2,1)} %copy-done.1, bf16[4,48,1152]{2,1,0:T(8,128)(2,1)} %copy-done.11, bf16[4,48,1152]{2,1,0:T(8,128)(2,1)} %copy-done.8, ...), custom_call_target="tpu_custom_call" | custom-call | flops 3623878656 | bytes 12582912 | tf_op jit(solution)/shard_map/project/pallas_call | solution.py:194
  67.1 2.6 collective-permute-start.19
  69.7 17.6 %attend.1 = (bf16[1024,768]{1,0:T(8,128)(2,1)}, f32[1024,768]{1,0:T(8,128)}, bf16[12,4,256,768]{3,2,1,0:T(8,128)(2,1)}) custom-call(bf16[1024,768]{1,0:T(8,128)(2,1)} %get-tuple-element.100.q_ref, bf16[1024,768]{1,0:T(8,128)(2,1)} %get-tuple-element.101.k_ref, bf16[1024,768]{1,0:T(8,128)(2,1)} %get-tuple-element.102.v_ref, ...), custom_call_target="tpu_custom_call" | custom-call | flops 8053063680 | bytes 23592960 | tf_op jit(solution)/shard_map/attend/pallas_call | solution.py:298
  93.8 17.5 %ffn.1 = (f32[1024,768]{1,0:T(8,128)}, bf16[1024,768]{1,0:T(8,128)(2,1)}, bf16[1024,2048]{1,0:T(8,128)(2,1)}, bf16[1024,2048]{1,0:T(8,128)(2,1)}, bf16[1024,2048]{1,0:T(8,128)(2,1)}) custom-call(s32[2,32]{1,0:T(2,128)} %pad_add_fusion.1.tab_ref, bf16[4,48,2432]{2,1,0:T(8,128)(2,1)} %copy-done.19, bf16[4,48,2432]{2,1,0:T(8,128)(2,1)} %collective-permute-done.17.refs_1_, ...), custom_call_target="tpu_custom_call" | custom-call | flops 7650410496 | bytes 29360128 | tf_op jit(solution)/shard_map/ffn/pallas_call | solution.py:475
  113.0 8.2 %grad_down.1 = (bf16[8,128,768]{2,1,0:T(8,128)(2,1)}, bf16[8,128,768]{2,1,0:T(8,128)(2,1)}) custom-call(s32[16]{0:T(128)} %get-tuple-element.236.tab_ref, bf16[1024,2048]{1,0:T(8,128)(2,1)} %get-tuple-element.121.refs_0_.refs_9_, bf16[1024,768]{1,0:T(8,128)(2,1)} %bitcast.75), custom_call_target="tpu_custom_call" | custom-call | flops 3221225472 | bytes 8912896 | tf_op jit(solution)/shard_map/grad_down/pallas_call | solution.py:774
  123.8 15.3 %hidden_back.1 = (bf16[1024,768]{1,0:T(8,128)(2,1)}, bf16[1024,2048]{1,0:T(8,128)(2,1)}, bf16[1024,2048]{1,0:T(8,128)(2,1)}) custom-call(s32[2,32]{1,0:T(2,128)} %pad_add_fusion.tab_ref, bf16[4,128,384]{2,1,0:T(8,128)(2,1)} %copy-done.20, bf16[4,128,384]{2,1,0:T(8,128)(2,1)} %copy-done.31, bf16[4,128,384]{2,1,0:T(8,128)(2,1)} %copy-done.30, ...), custom_call_target="tpu_custom_call" | custom-call | flops 6442450944 | bytes 28311552 | tf_op jit(solution)/shard_map/hidden_back/pallas_call | solution.py:529
  140.3 12.6 %grad_gate_up.1 = (bf16[16,48,2048]{2,1,0:T(8,128)(2,1)}, bf16[16,48,2048]{2,1,0:T(8,128)(2,1)}) custom-call(s32[32]{0:T(128)} %add.354.tab_ref, bf16[1024,768]{1,0:T(8,128)(2,1)} %get-tuple-element.130.refs_0_, bf16[1024,2048]{1,0:T(8,128)(2,1)} %get-tuple-element.127.refs_1_.refs_9_, bf16[1024,2048]{1,0:T(8,128)(2,1)} %get-tuple-element.131.refs_2_.refs_10_), custom_call_target="tpu_custom_call" | custom-call | flops 6442450944 | bytes 16252928 | tf_op jit(solution)/shard_map/grad_gate_up/pallas_call | solution.py:774
  154.7 19.2 %middle_back.1 = (f32[1024,768]{1,0:T(8,128)}, bf16[1024,768]{1,0:T(8,128)(2,1)}, bf16[1024,768]{1,0:T(8,128)(2,1)}) custom-call(s32[2,32]{1,0:T(2,128)} %pad_add_fusion.1.tab_ref, bf16[4,48,2432]{2,1,0:T(8,128)(2,1)} %copy-done.19, bf16[4,48,2432]{2,1,0:T(8,128)(2,1)} %collective-permute-done.17.refs_1_, bf16[4,48,2432]{2,1,0:T(8,128)(2,1)} %copy-done.18, ...), custom_call_target="tpu_custom_call" | custom-call | flops 7650410496 | bytes 14680064 | tf_op jit(solution)/shard_map/middle_back/pallas_call | solution.py:602
  175.3 2.6 collective-permute-start.36
  177.9 3.2 %add_convert_fusion = (bf16[4,48,2048]{2,1,0:T(8,128)(2,1)}, bf16[4,48,2048]{2,1,0:T(8,128)(2,1)}) fusion(bf16[16,48,2048]{2,1,0:T(8,128)(2,1)S(1)} %collective-permute-done.33, bf16[16,48,2048]{2,1,0:T(8,128)(2,1)} %get-tuple-element.167), kind=kLoop, calls=%fused_computation | loop fusion | flops 3145728 | bytes 4718592 | tf_op jit(solution)/shard_map/convert_element_type | solution.py:938
  183.3 16.5 %attend_back.2 = (bf16[1024,512]{1,0:T(8,128)(2,1)}, bf16[1024,512]{1,0:T(8,128)(2,1)}, bf16[1024,512]{1,0:T(8,128)(2,1)}) custom-call(bf16[1024,768]{1,0:T(8,128)(2,1)} %get-tuple-element.100.q_ref, bf16[1024,768]{1,0:T(8,128)(2,1)} %get-tuple-element.101.k_ref, bf16[1024,768]{1,0:T(8,128)(2,1)} %get-tuple-element.102.v_ref, ...), custom_call_target="tpu_custom_call" | custom-call | flops 10737418240 | bytes 18874368 | tf_op jit(solution)/shard_map/attend_back/pallas_call | solution.py:403
  204.7 1.9 fusion.8
  206.6 9.4 %grad_qk_out.1 = (bf16[16,48,1152]{2,1,0:T(8,128)(2,1)}, bf16[16,48,1152]{2,1,0:T(8,128)(2,1)}) custom-call(s32[32]{0:T(128)} %add.354.tab_ref, bf16[1024,768]{1,0:T(8,128)(2,1)} %get-tuple-element.161.refs_0_, bf16[1024,768]{1,0:T(8,128)(2,1)} %get-tuple-element.106.refs_9_.mixed_ref.refs_1_, bf16[1024,512]{1,0:T(8,128)(2,1)} %get-tuple-element.144.refs_2_.refs_10_, ...), custom_call_target="tpu_custom_call" | custom-call | flops 3623878656 | bytes 9830400 | tf_op jit(solution)/shard_map/grad_qk_out/pallas_call | solution.py:774
  219.0 2.2 add_convert_fusion.5
  221.2 2.3 collective-permute-start.43
  223.5 2.3 add_convert_fusion.3
  228.1 10.6 %attend_back.3 = (bf16[1024,256]{1,0:T(8,128)(2,1)}, bf16[1024,256]{1,0:T(8,128)(2,1)}, bf16[1024,256]{1,0:T(8,128)(2,1)}) custom-call(bf16[1024,768]{1,0:T(8,128)(2,1)} %get-tuple-element.100.q_ref, bf16[1024,768]{1,0:T(8,128)(2,1)} %get-tuple-element.101.k_ref, bf16[1024,768]{1,0:T(8,128)(2,1)} %get-tuple-element.102.v_ref, ...), custom_call_target="tpu_custom_call" | custom-call | flops 5368709120 | bytes 9437184 | tf_op jit(solution)/shard_map/attend_back/pallas_call | solution.py:403
  238.7 3.3 %collective-permute-done.43 = bf16[2,48,2048]{2,1,0:T(8,128)(2,1)S(1)} collective-permute-done((bf16[2,48,2048]{2,1,0:T(8,128)(2,1)}, bf16[2,48,2048]{2,1,0:T(8,128)(2,1)S(1)}, u32[]{:S(2)}, u32[]{:S(2)}) %collective-permute-start.43) | collective-permute-done | bytes 393248 | tf_op jit(solution)/shard_map/ppermute | solution.py:814
  242.0 1.9 fusion.9
  243.9 2.2 add_convert_fusion.11
  250.2 5.0 %grad_qkv_rest.1 = (bf16[8,48,768]{2,1,0:T(8,128)(2,1)}, bf16[8,48,768]{2,1,0:T(8,128)(2,1)}) custom-call(s32[16]{0:T(128)} %get-tuple-element.236.tab_ref, bf16[1024,768]{1,0:T(8,128)(2,1)} %get-tuple-element.161.refs_0_, bf16[1024,256]{1,0:T(8,128)(2,1)} %get-tuple-element.158.refs_1_.refs_11_, bf16[1024,256]{1,0:T(8,128)(2,1)} %get-tuple-element.162.refs_2_.refs_13_, ...), custom_call_target="tpu_custom_call" | custom-call | flops 1207959552 | bytes 4325376 | tf_op jit(solution)/shard_map/grad_qkv_rest/pallas_call | solution.py:774
  258.7 2.4 collective-permute-start.49
  264.8 11.4 %input_grad.1 = f32[1024,768]{1,0:T(8,128)} custom-call(s32[2,32]{1,0:T(2,128)} %pad_add_fusion.1.tab_ref, bf16[4,48,1152]{2,1,0:T(8,128)(2,1)} %copy-done.1, bf16[4,48,1152]{2,1,0:T(8,128)(2,1)} %copy-done.11, bf16[4,48,1152]{2,1,0:T(8,128)(2,1)} %copy-done.8, bf16[4,48,1152]{2,1,0:T(8,128)(2,1)} %copy-done.10, ...), custom_call_target="tpu_custom_call" | custom-call | flops 3623878656 | bytes 15728640 | tf_op jit(solution)/shard_map/input_grad/pallas_call | solution.py:656
  276.3 2.1 collective-permute-start.53
  281.3 2.7 collective-permute-start.51
  290.7 3.3 %collective-permute-done.52 = bf16[48,1152]{1,0:T(8,128)(2,1)S(1)} collective-permute-done((bf16[48,1152]{1,0:T(8,128)(2,1)S(1)}, bf16[48,1152]{1,0:T(8,128)(2,1)S(1)}, u32[]{:S(2)}, u32[]{:S(2)}) %collective-permute-start.52) | collective-permute-done | bytes 110624 | tf_op jit(solution)/shard_map/ppermute | solution.py:814
  (248 shorter events, 76.9 us)
Async XLA Ops:
  3.5 12.0 %collective-permute-start.2 = (bf16[1,48,1152]{2,1,0:T(8,128)(2,1)}, bf16[1,48,1152]{2,1,0:T(8,128)(2,1)S(1)}, u32[]{:S(2)}, u32[]{:S(2)}) collective-permute-start(bf16[1,48,1152]{2,1,0:T(8,128)(2,1)} %bitcast.63), channel_id=1, source_target_pairs={{0,12},{1,13},{2,14},{3,15},{4,8},{5,9},{6,10},{7,11},{8,4},{9,5},... | collective-permute-start | bytes 331784 | tf_op jit(solution)/shard_map/ppermute | solution.py:814
  24.7 13.9 %collective-permute-start.9 = (bf16[4,48,1152]{2,1,0:T(8,128)(2,1)S(1)}, bf16[4,48,1152]{2,1,0:T(8,128)(2,1)S(1)}, u32[]{:S(2)}, u32[]{:S(2)}) collective-permute-start(bf16[4,48,1152]{2,1,0:T(8,128)(2,1)S(1)} %constant_dynamic-update-slice_fusion.refs_2_), channel_id=1, source_target_pairs={{0,2},{1,3},{2,0},{3,1},{4,6},{5,7},{6,4},{7,5},{8,10},{9,11},{10,... | collective-permute-start | bytes 1327112 | tf_op jit(solution)/shard_map/ppermute | solution.py:814
  26.4 12.6 %collective-permute-start.7 = (bf16[4,48,1152]{2,1,0:T(8,128)(2,1)S(1)}, bf16[4,48,1152]{2,1,0:T(8,128)(2,1)S(1)}, u32[]{:S(2)}, u32[]{:S(2)}) collective-permute-start(bf16[4,48,1152]{2,1,0:T(8,128)(2,1)S(1)} %pad_maximum_fusion.2.refs_0_), channel_id=1, source_target_pairs={{0,16},{16,0},{1,17},{17,1},{2,18},{18,2},{3,19},{19,3},{4,20},{20... | collective-permute-start | bytes 1327112 | tf_op jit(solution)/shard_map/ppermute | solution.py:814
  31.3 17.4 %collective-permute-start.4 = (bf16[1,48,2432]{2,1,0:T(8,128)(2,1)S(1)}, bf16[1,48,2432]{2,1,0:T(8,128)(2,1)S(1)}, u32[]{:S(2)}, u32[]{:S(2)}) collective-permute-start(bf16[1,48,2432]{2,1,0:T(8,128)(2,1)S(1)} %bitcast.70), channel_id=1, source_target_pairs={{0,8},{1,9},{2,10},{3,11},{4,12},{5,13},{6,14},{7,15},{8,0},{9,1},... | collective-permute-start | bytes 700424 | tf_op jit(solution)/shard_map/ppermute | solution.py:814
  31.3 18.1 %collective-permute-start.12 = (bf16[4,48,1152]{2,1,0:T(8,128)(2,1)S(1)}, bf16[4,48,1152]{2,1,0:T(8,128)(2,1)}, u32[]{:S(2)}, u32[]{:S(2)}) collective-permute-start(bf16[4,48,1152]{2,1,0:T(8,128)(2,1)S(1)} %constant_dynamic-update-slice_fusion.refs_2_), channel_id=1, source_target_pairs={{0,1},{1,0},{2,3},{3,2},{4,5},{5,4},{6,7},{7,6},{8,9},{9,8},{10,11... | collective-permute-start | bytes 1327112 | tf_op jit(solution)/shard_map/ppermute | solution.py:814
  38.5 14.8 %collective-permute-start.10 = (bf16[4,48,1152]{2,1,0:T(8,128)(2,1)S(1)}, bf16[4,48,1152]{2,1,0:T(8,128)(2,1)}, u32[]{:S(2)}, u32[]{:S(2)}) collective-permute-start(bf16[4,48,1152]{2,1,0:T(8,128)(2,1)S(1)} %pad_maximum_fusion.2.refs_0_), channel_id=1, source_target_pairs={{0,1},{1,0},{2,3},{3,2},{4,5},{5,4},{6,7},{7,6},{8,9},{9,8},{10,11... | collective-permute-start | bytes 1327112 | tf_op jit(solution)/shard_map/ppermute | solution.py:814
  38.5 14.8 %collective-permute-start.13 = (bf16[4,48,1152]{2,1,0:T(8,128)(2,1)S(1)}, bf16[4,48,1152]{2,1,0:T(8,128)(2,1)}, u32[]{:S(2)}, u32[]{:S(2)}) collective-permute-start(bf16[4,48,1152]{2,1,0:T(8,128)(2,1)S(1)} %collective-permute-done.9.refs_3_), channel_id=1, source_target_pairs={{0,1},{1,0},{2,3},{3,2},{4,5},{5,4},{6,7},{7,6},{8,9},{9,8},{10,11... | collective-permute-start | bytes 1327112 | tf_op jit(solution)/shard_map/ppermute | solution.py:814
  39.1 14.3 %collective-permute-start.11 = (bf16[4,48,1152]{2,1,0:T(8,128)(2,1)S(1)}, bf16[4,48,1152]{2,1,0:T(8,128)(2,1)}, u32[]{:S(2)}, u32[]{:S(2)}) collective-permute-start(bf16[4,48,1152]{2,1,0:T(8,128)(2,1)S(1)} %collective-permute-done.7.refs_1_), channel_id=1, source_target_pairs={{0,1},{1,0},{2,3},{3,2},{4,5},{5,4},{6,7},{7,6},{8,9},{9,8},{10,11... | collective-permute-start | bytes 1327112 | tf_op jit(solution)/shard_map/ppermute | solution.py:814
  48.8 15.4 %collective-permute-start.16 = (bf16[2,48,2432]{2,1,0:T(8,128)(2,1)S(1)}, bf16[2,48,2432]{2,1,0:T(8,128)(2,1)S(1)}, u32[]{:S(2)}, u32[]{:S(2)}) collective-permute-start(bf16[2,48,2432]{2,1,0:T(8,128)(2,1)S(1)} %pad_maximum_fusion.1), channel_id=1, source_target_pairs={{0,16},{16,0},{1,17},{17,1},{2,18},{18,2},{3,19},{19,3},{4,20},{20... | collective-permute-start | bytes 1400840 | tf_op jit(solution)/shard_map/ppermute | solution.py:814
  49.4 14.8 %collective-permute-start.15 = (bf16[2,48,2432]{2,1,0:T(8,128)(2,1)S(1)}, bf16[2,48,2432]{2,1,0:T(8,128)(2,1)S(1)}, u32[]{:S(2)}, u32[]{:S(2)}) collective-permute-start(bf16[2,48,2432]{2,1,0:T(8,128)(2,1)S(1)} %pad_maximum_fusion), channel_id=1, source_target_pairs={{0,2},{1,3},{2,0},{3,1},{4,6},{5,7},{6,4},{7,5},{8,10},{9,11},{10,... | collective-permute-start | bytes 1400840 | tf_op jit(solution)/shard_map/ppermute | solution.py:814
  64.3 23.1 %collective-permute-start.21 = (bf16[4,48,2432]{2,1,0:T(8,128)(2,1)S(1)}, bf16[4,48,2432]{2,1,0:T(8,128)(2,1)}, u32[]{:S(2)}, u32[]{:S(2)}) collective-permute-start(bf16[4,48,2432]{2,1,0:T(8,128)(2,1)S(1)} %constant_dynamic-update-slice_fusion.7.refs_2_), channel_id=1, source_target_pairs={{0,1},{1,0},{2,3},{3,2},{4,5},{5,4},{6,7},{7,6},{8,9},{9,8},{10,11... | collective-permute-start | bytes 2801672 | tf_op jit(solution)/shard_map/ppermute | solution.py:814
  64.4 23.2 %collective-permute-start.18 = (bf16[4,48,2432]{2,1,0:T(8,128)(2,1)S(1)}, bf16[4,48,2432]{2,1,0:T(8,128)(2,1)}, u32[]{:S(2)}, u32[]{:S(2)}) collective-permute-start(bf16[4,48,2432]{2,1,0:T(8,128)(2,1)S(1)} %constant_dynamic-update-slice_fusion.7.refs_2_), channel_id=1, source_target_pairs={{0,2},{1,3},{2,0},{3,1},{4,6},{5,7},{6,4},{7,5},{8,10},{9,11},{10,... | collective-permute-start | bytes 2801672 | tf_op jit(solution)/shard_map/ppermute | solution.py:814
  65.4 22.2 %collective-permute-start.20 = (bf16[4,48,2432]{2,1,0:T(8,128)(2,1)S(1)}, bf16[4,48,2432]{2,1,0:T(8,128)(2,1)S(1)}, u32[]{:S(2)}, u32[]{:S(2)}) collective-permute-start(bf16[4,48,2432]{2,1,0:T(8,128)(2,1)S(1)} %constant_dynamic-update-slice_fusion.5.refs_0_), channel_id=1, source_target_pairs={{0,1},{1,0},{2,3},{3,2},{4,5},{5,4},{6,7},{7,6},{8,9},{9,8},{10,11... | collective-permute-start | bytes 2801672 | tf_op jit(solution)/shard_map/ppermute | solution.py:814
  65.7 23.1 %collective-permute-start.17 = (bf16[4,48,2432]{2,1,0:T(8,128)(2,1)S(1)}, bf16[4,48,2432]{2,1,0:T(8,128)(2,1)}, u32[]{:S(2)}, u32[]{:S(2)}) collective-permute-start(bf16[4,48,2432]{2,1,0:T(8,128)(2,1)S(1)} %constant_dynamic-update-slice_fusion.5.refs_0_), channel_id=1, source_target_pairs={{0,16},{16,0},{1,17},{17,1},{2,18},{18,2},{3,19},{19,3},{4,20},{20... | collective-permute-start | bytes 2801672 | tf_op jit(solution)/shard_map/ppermute | solution.py:814
  67.1 20.2 %collective-permute-start.19 = (bf16[2,128,384]{2,1,0:T(8,128)(2,1)S(1)}, bf16[2,128,384]{2,1,0:T(8,128)(2,1)S(1)}, u32[]{:S(2)}, u32[]{:S(2)}) collective-permute-start(bf16[2,128,384]{2,1,0:T(8,128)(2,1)S(1)} %constant_dynamic-update-slice_fusion.3), channel_id=1, source_target_pairs={{0,8},{1,9},{2,10},{3,11},{4,12},{5,13},{6,14},{7,15},{8,0},{9,1},... | collective-permute-start | bytes 589832 | tf_op jit(solution)/shard_map/ppermute | solution.py:814
  89.4 21.9 %collective-permute-start.26 = (bf16[4,128,384]{2,1,0:T(8,128)(2,1)S(1)}, bf16[4,128,384]{2,1,0:T(8,128)(2,1)S(1)}, u32[]{:S(2)}, u32[]{:S(2)}) collective-permute-start(bf16[4,128,384]{2,1,0:T(8,128)(2,1)S(1)} %constant_dynamic-update-slice_fusion.9.refs_0_), channel_id=1, source_target_pairs={{0,18},{1,19},{2,16},{3,17},{4,22},{5,23},{6,20},{7,21},{8,26},{9,... | collective-permute-start | bytes 1179656 | tf_op jit(solution)/shard_map/ppermute | solution.py:851
  90.8 20.6 %collective-permute-start.25 = (bf16[4,128,384]{2,1,0:T(8,128)(2,1)S(1)}, bf16[4,128,384]{2,1,0:T(8,128)(2,1)S(1)}, u32[]{:S(2)}, u32[]{:S(2)}) collective-permute-start(bf16[4,128,384]{2,1,0:T(8,128)(2,1)S(1)} %constant_dynamic-update-slice_fusion.9.refs_0_), channel_id=1, source_target_pairs={{0,16},{16,0},{1,17},{17,1},{2,18},{18,2},{3,19},{19,3},{4,20},{20... | collective-permute-start | bytes 1179656 | tf_op jit(solution)/shard_map/ppermute | solution.py:814
  92.0 19.4 %collective-permute-start.24 = (bf16[4,128,384]{2,1,0:T(8,128)(2,1)S(1)}, bf16[4,128,384]{2,1,0:T(8,128)(2,1)S(1)}, u32[]{:S(2)}, u32[]{:S(2)}) collective-permute-start(bf16[4,128,384]{2,1,0:T(8,128)(2,1)S(1)} %constant_dynamic-update-slice_fusion.9.refs_0_), channel_id=1, source_target_pairs={{0,2},{1,3},{2,0},{3,1},{4,6},{5,7},{6,4},{7,5},{8,10},{9,11},{10,... | collective-permute-start | bytes 1179656 | tf_op jit(solution)/shard_map/ppermute | solution.py:814
  122.4 16.7 %collective-permute-start.31 = (bf16[8,128,768]{2,1,0:T(8,128)(2,1)}, bf16[8,128,768]{2,1,0:T(8,128)(2,1)S(1)}, u32[]{:S(2)}, u32[]{:S(2)}) collective-permute-start(bf16[8,128,768]{2,1,0:T(8,128)(2,1)} %get-tuple-element.128), channel_id=1, source_target_pairs={{0,1},{1,0},{2,3},{3,2},{4,5},{5,4},{6,7},{7,6},{8,9},{9,8},{10,11... | collective-permute-start | bytes 4718600 | tf_op jit(solution)/shard_map/ppermute | solution.py:814
  153.0 20.9 %collective-permute-start.33 = (bf16[16,48,2048]{2,1,0:T(8,128)(2,1)}, bf16[16,48,2048]{2,1,0:T(8,128)(2,1)S(1)}, u32[]{:S(2)}, u32[]{:S(2)}) collective-permute-start(bf16[16,48,2048]{2,1,0:T(8,128)(2,1)} %get-tuple-element.137), channel_id=1, source_target_pairs={{0,1},{1,0},{2,3},{3,2},{4,5},{5,4},{6,7},{7,6},{8,9},{9,8},{10,11... | collective-permute-start | bytes 9437192 | tf_op jit(solution)/shard_map/ppermute | solution.py:814
  153.5 20.4 %collective-permute-start.32 = (bf16[4,128,768]{2,1,0:T(8,128)(2,1)}, bf16[4,128,768]{2,1,0:T(8,128)(2,1)}, u32[]{:S(2)}, u32[]{:S(2)}) collective-permute-start(bf16[4,128,768]{2,1,0:T(8,128)(2,1)} %add_convert_fusion.2), channel_id=1, source_target_pairs={{0,2},{1,3},{2,0},{3,1},{4,6},{5,7},{6,4},{7,5},{8,10},{9,11},{10,... | collective-permute-start | bytes 2359304 | tf_op jit(solution)/shard_map/ppermute | solution.py:814
  175.3 24.5 %collective-permute-start.36 = (bf16[2,128,768]{2,1,0:T(8,128)(2,1)S(1)}, bf16[2,128,768]{2,1,0:T(8,128)(2,1)S(1)}, u32[]{:S(2)}, u32[]{:S(2)}) collective-permute-start(bf16[2,128,768]{2,1,0:T(8,128)(2,1)S(1)} %add_convert_fusion.8), channel_id=1, source_target_pairs={{0,8},{1,9},{2,10},{3,11},{4,12},{5,13},{6,14},{7,15},{8,0},{9,1},... | collective-permute-start | bytes 1179656 | tf_op jit(solution)/shard_map/ppermute | solution.py:814
  181.1 19.3 %collective-permute-start.35 = (bf16[4,48,2048]{2,1,0:T(8,128)(2,1)}, bf16[4,48,2048]{2,1,0:T(8,128)(2,1)}, u32[]{:S(2)}, u32[]{:S(2)}) collective-permute-start(bf16[4,48,2048]{2,1,0:T(8,128)(2,1)} %get-tuple-element.177), channel_id=1, source_target_pairs={{0,2},{1,3},{2,0},{3,1},{4,6},{5,7},{6,4},{7,5},{8,10},{9,11},{10,... | collective-permute-start | bytes 2359304 | tf_op jit(solution)/shard_map/ppermute | solution.py:814
  182.0 19.0 %collective-permute-start.34 = (bf16[4,48,2048]{2,1,0:T(8,128)(2,1)}, bf16[4,48,2048]{2,1,0:T(8,128)(2,1)}, u32[]{:S(2)}, u32[]{:S(2)}) collective-permute-start(bf16[4,48,2048]{2,1,0:T(8,128)(2,1)} %get-tuple-element.178), channel_id=1, source_target_pairs={{0,16},{16,0},{1,17},{17,1},{2,18},{18,2},{3,19},{19,3},{4,20},{20... | collective-permute-start | bytes 2359304 | tf_op jit(solution)/shard_map/ppermute | solution.py:814
  202.8 13.2 %collective-permute-start.38 = (bf16[2,48,2048]{2,1,0:T(8,128)(2,1)S(1)}, bf16[2,48,2048]{2,1,0:T(8,128)(2,1)}, u32[]{:S(2)}, u32[]{:S(2)}) collective-permute-start(bf16[2,48,2048]{2,1,0:T(8,128)(2,1)S(1)} %get-tuple-element.175), channel_id=1, source_target_pairs={{0,16},{16,0},{1,17},{17,1},{2,18},{18,2},{3,19},{19,3},{4,20},{20... | collective-permute-start | bytes 1179656 | tf_op jit(solution)/shard_map/ppermute | solution.py:814
  204.2 11.8 %collective-permute-start.37 = (bf16[2,48,2048]{2,1,0:T(8,128)(2,1)S(1)}, bf16[2,48,2048]{2,1,0:T(8,128)(2,1)}, u32[]{:S(2)}, u32[]{:S(2)}) collective-permute-start(bf16[2,48,2048]{2,1,0:T(8,128)(2,1)S(1)} %get-tuple-element.176), channel_id=1, source_target_pairs={{0,2},{1,3},{2,0},{3,1},{4,6},{5,7},{6,4},{7,5},{8,10},{9,11},{10,... | collective-permute-start | bytes 1179656 | tf_op jit(solution)/shard_map/ppermute | solution.py:814
  217.6 30.8 %collective-permute-start.57 = (bf16[128,768]{1,0:T(8,128)(2,1)S(1)}, bf16[128,768]{1,0:T(8,128)(2,1)}, u32[]{:S(2)}, u32[]{:S(2)}) collective-permute-start(bf16[128,768]{1,0:T(8,128)(2,1)S(1)} %fusion.6), channel_id=1, source_target_pairs={{0,16},{16,0},{1,17},{17,1},{2,18},{18,2},{3,19},{19,3},{4,20},{20... | collective-permute-start | bytes 589832 | tf_op jit(solution)/shard_map/ppermute | solution.py:814
  221.2 20.8 %collective-permute-start.43 = (bf16[2,48,2048]{2,1,0:T(8,128)(2,1)}, bf16[2,48,2048]{2,1,0:T(8,128)(2,1)S(1)}, u32[]{:S(2)}, u32[]{:S(2)}) collective-permute-start(bf16[2,48,2048]{2,1,0:T(8,128)(2,1)} %add_convert_fusion.5), channel_id=1, source_target_pairs={{0,8},{1,9},{2,10},{3,11},{4,12},{5,13},{6,14},{7,15},{8,0},{9,1},... | collective-permute-start | bytes 1179656 | tf_op jit(solution)/shard_map/ppermute | solution.py:814
  225.8 16.2 %collective-permute-start.42 = (bf16[4,48,1152]{2,1,0:T(8,128)(2,1)}, bf16[4,48,1152]{2,1,0:T(8,128)(2,1)}, u32[]{:S(2)}, u32[]{:S(2)}) collective-permute-start(bf16[4,48,1152]{2,1,0:T(8,128)(2,1)} %get-tuple-element.181), channel_id=1, source_target_pairs={{0,2},{1,3},{2,0},{3,1},{4,6},{5,7},{6,4},{7,5},{8,10},{9,11},{10,... | collective-permute-start | bytes 1327112 | tf_op jit(solution)/shard_map/ppermute | solution.py:814
  226.7 15.3 %collective-permute-start.41 = (bf16[4,48,1152]{2,1,0:T(8,128)(2,1)}, bf16[4,48,1152]{2,1,0:T(8,128)(2,1)}, u32[]{:S(2)}, u32[]{:S(2)}) collective-permute-start(bf16[4,48,1152]{2,1,0:T(8,128)(2,1)} %get-tuple-element.182), channel_id=1, source_target_pairs={{0,16},{16,0},{1,17},{17,1},{2,18},{18,2},{3,19},{19,3},{4,20},{20... | collective-permute-start | bytes 1327112 | tf_op jit(solution)/shard_map/ppermute | solution.py:814
  258.7 17.4 %collective-permute-start.49 = (bf16[2,48,1152]{2,1,0:T(8,128)(2,1)S(1)}, bf16[2,48,1152]{2,1,0:T(8,128)(2,1)S(1)}, u32[]{:S(2)}, u32[]{:S(2)}) collective-permute-start(bf16[2,48,1152]{2,1,0:T(8,128)(2,1)S(1)} %add_convert_fusion.10), channel_id=1, source_target_pairs={{0,8},{1,9},{2,10},{3,11},{4,12},{5,13},{6,14},{7,15},{8,0},{9,1},... | collective-permute-start | bytes 663560 | tf_op jit(solution)/shard_map/ppermute | solution.py:814
  264.2 12.0 %collective-permute-start.50 = (bf16[4,48,768]{2,1,0:T(8,128)(2,1)S(1)}, bf16[4,48,768]{2,1,0:T(8,128)(2,1)S(1)}, u32[]{:S(2)}, u32[]{:S(2)}) collective-permute-start(bf16[4,48,768]{2,1,0:T(8,128)(2,1)S(1)} %add_convert_fusion.9), channel_id=1, source_target_pairs={{0,2},{1,3},{2,0},{3,1},{4,6},{5,7},{6,4},{7,5},{8,10},{9,11},{10,... | collective-permute-start | bytes 884744 | tf_op jit(solution)/shard_map/ppermute | solution.py:814
  (62 other events, 612.0 us)

commit v5 on v4

--- a/solution.py
+++ b/solution.py
@@ -29,8 +29,8 @@
     return lax.dot_general(left, right, dims, preferred_element_type=f32)
 
 
-def params():
-    return pltpu.CompilerParams(vmem_limit_bytes=60 * MIB)
+def params(mib=60):
+    return pltpu.CompilerParams(vmem_limit_bytes=mib * MIB)
 
 
 HINT = 1.0
@@ -413,7 +413,7 @@
         out_specs=[part] * 3,
         out_shape=[shape] * 3,
         scratch_shapes=[pltpu.VMEM((2,) + exps.shape[1:], bf16)],
-        compiler_params=params(),
+        compiler_params=params(54),
         cost_estimate=cost(2560 * pairs * length * length, 4608 * pairs * length),
         name="attend_back",
     )(q, k, v, mixed, inv, exps, grad, cosine, sine)
@@ -789,7 +789,7 @@
             jax.ShapeDtypeStruct((kept, block_rows, columns), bf16),
             jax.ShapeDtypeStruct((sent, block_rows, columns), bf16),
         ],
-        compiler_params=params(),
+        compiler_params=params(54),
         cost_estimate=cost(
             2 * length * rows * columns * halves,
             2 * (length * rows + length * columns * halves + rows * columns * halves),

time: 299 us -> 294 us (0.983)
  other arithmetic: 39 us -> 32.1 us
    convert_element_type x16, other arithmetic: 23.1 us -> 17.7 us  [add(): return total.astype(bf16)]
  transfers between devices with their start and end apart: 58 -> 58, of which waited for: 16 -> 15; matrix products, arithmetic and copies ran while one was open for 11% -> 8% of each run, Pallas kernels for 49% -> 49%
where the time goes in v5:
time: 294 us; the launch traced here: 293 us
  Pallas kernels  159 us (54%)
  starting transfers between devices  56.9 us (19%)
  waiting for transfers between devices  36.6 us (12%)
  other arithmetic  32.1 us (11%)
  local copies, waits for them, and re-layouts  6.68 us (2%)
    ppermute x57, starting transfers between devices, swapped(): return lambda array: lax.ppermute(array, axis, pairs)  55.5 us
    ppermute x57, waiting for transfers between devices, swapped(): return lambda array: lax.ppermute(array, axis, pairs)  36.6 us
    pallas_call x4, Pallas kernels, weight_grad(): pl.pallas_call(functools.partial(weight_kernel, counts=counts, block_rows...  35.1 us
    pallas_call x2, Pallas kernels, attend_back(): pl.pallas_call(attend_back_kernel, grid=(pairs,), in_specs=[column] * 5 +...  27.1 us
    pallas_call x1, Pallas kernels, middle_back(): pl.pallas_call(functools.partial(middle_back_kernel, n_pieces=n, halves=h...  19.2 us
    convert_element_type x16, other arithmetic, add(): return total.astype(bf16)  17.7 us
    pallas_call x1, Pallas kernels, attend(): pl.pallas_call(attend_kernel, grid=(pairs,), in_specs=[column, column, co...  17.6 us
    pallas_call x1, Pallas kernels, ffn(): pl.pallas_call(functools.partial(ffn_kernel, n_pieces=n, halves=halves),...  17.6 us
  transfers between devices with their start and end apart: 58, of which 15 were waited for; matrix products, arithmetic and copies ran while one was open for 8% of the time, Pallas kernels for 49%

profile of v5, /device:TPU:0, one launch (start us, length us, event | category | flops | bytes accessed | tf_op | source)
XLA Modules:
  0.0 293.0 jit_solution(3563688906081445773)
XLA Ops:
  3.5 5.0 %collective-permute-start.2 = (bf16[1,48,1152]{2,1,0:T(8,128)(2,1)}, bf16[1,48,1152]{2,1,0:T(8,128)(2,1)S(1)}, u32[]{:S(2)}, u32[]{:S(2)}) collective-permute-start(bf16[1,48,1152]{2,1,0:T(8,128)(2,1)} %bitcast.63), channel_id=1, source_target_pairs={{0,12},{1,13},{2,14},{3,15},{4,8},{5,9},{6,10},{7,11},{8,4},{9,5},... | collective-permute-start | bytes 331784 | tf_op jit(solution)/shard_map/ppermute | solution.py:814
  10.5 1.7 multiply_add_fusion
  13.7 1.8 pack.4
  15.5 2.6 collective-permute-done.1
  19.7 1.6 collective-permute-start.6
  21.7 3.0 %collective-permute-done.8 = bf16[2,48,1152]{2,1,0:T(8,128)(2,1)S(1)} collective-permute-done((bf16[2,48,1152]{2,1,0:T(8,128)(2,1)S(1)}, bf16[2,48,1152]{2,1,0:T(8,128)(2,1)S(1)}, u32[]{:S(2)}, u32[]{:S(2)}) %collective-permute-start.8) | collective-permute-done | bytes 221216 | tf_op jit(solution)/shard_map/ppermute | solution.py:814
  28.9 2.4 collective-permute-start.5
  31.4 7.2 %collective-permute-done.5 = bf16[1,48,2432]{2,1,0:T(8,128)(2,1)S(1)} collective-permute-done((bf16[1,48,2432]{2,1,0:T(8,128)(2,1)S(1)}, bf16[1,48,2432]{2,1,0:T(8,128)(2,1)S(1)}, u32[]{:S(2)}, u32[]{:S(2)}) %collective-permute-start.5) | collective-permute-done | bytes 233504 | tf_op jit(solution)/shard_map/ppermute | solution.py:814
  39.1 9.6 %collective-permute-done.4 = bf16[1,48,2432]{2,1,0:T(8,128)(2,1)S(1)} collective-permute-done((bf16[1,48,2432]{2,1,0:T(8,128)(2,1)S(1)}, bf16[1,48,2432]{2,1,0:T(8,128)(2,1)S(1)}, u32[]{:S(2)}, u32[]{:S(2)}) %collective-permute-start.4) | collective-permute-done | bytes 233504 | tf_op jit(solution)/shard_map/ppermute | solution.py:814
  53.4 10.8 %project.1 = (bf16[1024,768]{1,0:T(8,128)(2,1)}, bf16[1024,768]{1,0:T(8,128)(2,1)}, bf16[1024,768]{1,0:T(8,128)(2,1)}, bf16[1024,768]{1,0:T(8,128)(2,1)}) custom-call(s32[2,32]{1,0:T(2,128)} %pad_add_fusion.1.tab_ref, bf16[4,48,1152]{2,1,0:T(8,128)(2,1)} %copy-done.1, bf16[4,48,1152]{2,1,0:T(8,128)(2,1)} %copy-done.16, bf16[4,48,1152]{2,1,0:T(8,128)(2,1)} %copy-done.11, ...), custom_call_target="tpu_custom_call" | custom-call | flops 3623878656 | bytes 12582912 | tf_op jit(solution)/shard_map/project/pallas_call | solution.py:194
  67.2 2.6 collective-permute-start.19
  69.8 17.6 %attend.1 = (bf16[1024,768]{1,0:T(8,128)(2,1)}, f32[1024,768]{1,0:T(8,128)}, bf16[12,4,256,768]{3,2,1,0:T(8,128)(2,1)}) custom-call(bf16[1024,768]{1,0:T(8,128)(2,1)} %get-tuple-element.100.q_ref, bf16[1024,768]{1,0:T(8,128)(2,1)} %get-tuple-element.101.k_ref, bf16[1024,768]{1,0:T(8,128)(2,1)} %get-tuple-element.102.v_ref, ...), custom_call_target="tpu_custom_call" | custom-call | flops 8053063680 | bytes 23592960 | tf_op jit(solution)/shard_map/attend/pallas_call | solution.py:298
  94.8 17.6 %ffn.1 = (f32[1024,768]{1,0:T(8,128)}, bf16[1024,768]{1,0:T(8,128)(2,1)}, bf16[1024,2048]{1,0:T(8,128)(2,1)}, bf16[1024,2048]{1,0:T(8,128)(2,1)}, bf16[1024,2048]{1,0:T(8,128)(2,1)}) custom-call(s32[2,32]{1,0:T(2,128)} %pad_add_fusion.1.tab_ref, bf16[4,48,2432]{2,1,0:T(8,128)(2,1)} %copy-done.24, bf16[4,48,2432]{2,1,0:T(8,128)(2,1)} %collective-permute-done.17.refs_1_, ...), custom_call_target="tpu_custom_call" | custom-call | flops 7650410496 | bytes 29360128 | tf_op jit(solution)/shard_map/ffn/pallas_call | solution.py:475
  114.0 8.3 %grad_down.1 = (bf16[8,128,768]{2,1,0:T(8,128)(2,1)}, bf16[8,128,768]{2,1,0:T(8,128)(2,1)}) custom-call(s32[16]{0:T(128)} %get-tuple-element.236.tab_ref, bf16[1024,2048]{1,0:T(8,128)(2,1)} %get-tuple-element.121.refs_0_.refs_9_, bf16[1024,768]{1,0:T(8,128)(2,1)} %bitcast.75), custom_call_target="tpu_custom_call" | custom-call | flops 3221225472 | bytes 8912896 | tf_op jit(solution)/shard_map/grad_down/pallas_call | solution.py:774
  124.6 15.3 %hidden_back.1 = (bf16[1024,768]{1,0:T(8,128)(2,1)}, bf16[1024,2048]{1,0:T(8,128)(2,1)}, bf16[1024,2048]{1,0:T(8,128)(2,1)}) custom-call(s32[2,32]{1,0:T(2,128)} %pad_add_fusion.tab_ref, bf16[4,128,384]{2,1,0:T(8,128)(2,1)} %copy-done.28, bf16[4,128,384]{2,1,0:T(8,128)(2,1)} %collective-permute-done.24.refs_1_, ...), custom_call_target="tpu_custom_call" | custom-call | flops 6442450944 | bytes 28311552 | tf_op jit(solution)/shard_map/hidden_back/pallas_call | solution.py:529
  141.2 12.6 %grad_gate_up.1 = (bf16[16,48,2048]{2,1,0:T(8,128)(2,1)}, bf16[16,48,2048]{2,1,0:T(8,128)(2,1)}) custom-call(s32[32]{0:T(128)} %add.354.tab_ref, bf16[1024,768]{1,0:T(8,128)(2,1)} %get-tuple-element.130.refs_0_, bf16[1024,2048]{1,0:T(8,128)(2,1)} %get-tuple-element.127.refs_1_.refs_9_, bf16[1024,2048]{1,0:T(8,128)(2,1)} %get-tuple-element.131.refs_2_.refs_10_), custom_call_target="tpu_custom_call" | custom-call | flops 6442450944 | bytes 16252928 | tf_op jit(solution)/shard_map/grad_gate_up/pallas_call | solution.py:774
  155.5 19.2 %middle_back.1 = (f32[1024,768]{1,0:T(8,128)}, bf16[1024,768]{1,0:T(8,128)(2,1)}, bf16[1024,768]{1,0:T(8,128)(2,1)}) custom-call(s32[2,32]{1,0:T(2,128)} %pad_add_fusion.1.tab_ref, bf16[4,48,2432]{2,1,0:T(8,128)(2,1)} %copy-done.24, bf16[4,48,2432]{2,1,0:T(8,128)(2,1)} %collective-permute-done.17.refs_1_, bf16[4,48,2432]{2,1,0:T(8,128)(2,1)} %copy-done.23, ...), custom_call_target="tpu_custom_call" | custom-call | flops 7650410496 | bytes 14680064 | tf_op jit(solution)/shard_map/middle_back/pallas_call | solution.py:602
  176.1 2.6 collective-permute-start.36
  178.6 2.0 add_convert_fusion
  183.0 16.5 %attend_back.2 = (bf16[1024,512]{1,0:T(8,128)(2,1)}, bf16[1024,512]{1,0:T(8,128)(2,1)}, bf16[1024,512]{1,0:T(8,128)(2,1)}) custom-call(bf16[1024,768]{1,0:T(8,128)(2,1)} %get-tuple-element.100.q_ref, bf16[1024,768]{1,0:T(8,128)(2,1)} %get-tuple-element.101.k_ref, bf16[1024,768]{1,0:T(8,128)(2,1)} %get-tuple-element.102.v_ref, ...), custom_call_target="tpu_custom_call" | custom-call | flops 10737418240 | bytes 18874368 | tf_op jit(solution)/shard_map/attend_back/pallas_call | solution.py:403
  200.3 1.8 add_convert_fusion.6
  205.5 9.3 %grad_qk_out.1 = (bf16[16,48,1152]{2,1,0:T(8,128)(2,1)}, bf16[16,48,1152]{2,1,0:T(8,128)(2,1)}) custom-call(s32[32]{0:T(128)} %add.354.tab_ref, bf16[1024,768]{1,0:T(8,128)(2,1)} %get-tuple-element.161.refs_0_, bf16[1024,768]{1,0:T(8,128)(2,1)} %get-tuple-element.106.refs_9_.mixed_ref.refs_1_, bf16[1024,512]{1,0:T(8,128)(2,1)} %get-tuple-element.144.refs_2_.refs_10_, ...), custom_call_target="tpu_custom_call" | custom-call | flops 3623878656 | bytes 9830400 | tf_op jit(solution)/shard_map/grad_qk_out/pallas_call | solution.py:774
  219.9 2.4 collective-permute-start.43
  226.0 10.6 %attend_back.3 = (bf16[1024,256]{1,0:T(8,128)(2,1)}, bf16[1024,256]{1,0:T(8,128)(2,1)}, bf16[1024,256]{1,0:T(8,128)(2,1)}) custom-call(bf16[1024,768]{1,0:T(8,128)(2,1)} %get-tuple-element.100.q_ref, bf16[1024,768]{1,0:T(8,128)(2,1)} %get-tuple-element.101.k_ref, bf16[1024,768]{1,0:T(8,128)(2,1)} %get-tuple-element.102.v_ref, ...), custom_call_target="tpu_custom_call" | custom-call | flops 5368709120 | bytes 9437184 | tf_op jit(solution)/shard_map/attend_back/pallas_call | solution.py:403
  236.6 3.9 %collective-permute-done.43 = bf16[2,48,2048]{2,1,0:T(8,128)(2,1)S(1)} collective-permute-done((bf16[2,48,2048]{2,1,0:T(8,128)(2,1)S(1)}, bf16[2,48,2048]{2,1,0:T(8,128)(2,1)S(1)}, u32[]{:S(2)}, u32[]{:S(2)}) %collective-permute-start.43) | collective-permute-done | bytes 393248 | tf_op jit(solution)/shard_map/ppermute | solution.py:814
  246.3 4.9 %grad_qkv_rest.1 = (bf16[8,48,768]{2,1,0:T(8,128)(2,1)}, bf16[8,48,768]{2,1,0:T(8,128)(2,1)}) custom-call(s32[16]{0:T(128)} %get-tuple-element.236.tab_ref, bf16[1024,768]{1,0:T(8,128)(2,1)} %get-tuple-element.161.refs_0_, bf16[1024,256]{1,0:T(8,128)(2,1)} %get-tuple-element.158.refs_1_.refs_11_, bf16[1024,256]{1,0:T(8,128)(2,1)} %get-tuple-element.162.refs_2_.refs_13_, ...), custom_call_target="tpu_custom_call" | custom-call | flops 1207959552 | bytes 4325376 | tf_op jit(solution)/shard_map/grad_qkv_rest/pallas_call | solution.py:774
  254.2 2.4 collective-permute-start.49
  260.8 11.5 %input_grad.1 = f32[1024,768]{1,0:T(8,128)} custom-call(s32[2,32]{1,0:T(2,128)} %pad_add_fusion.1.tab_ref, bf16[4,48,1152]{2,1,0:T(8,128)(2,1)} %copy-done.1, bf16[4,48,1152]{2,1,0:T(8,128)(2,1)} %copy-done.16, bf16[4,48,1152]{2,1,0:T(8,128)(2,1)} %copy-done.11, bf16[4,48,1152]{2,1,0:T(8,128)(2,1)} %copy-done.15, ...), custom_call_target="tpu_custom_call" | custom-call | flops 3623878656 | bytes 15728640 | tf_op jit(solution)/shard_map/input_grad/pallas_call | solution.py:656
  272.5 2.0 collective-permute-start.53
  274.5 1.8 collective-permute-start.55
  277.3 2.6 collective-permute-start.51
  287.3 2.5 collective-permute-done.52
  (262 shorter events, 75.7 us)
Async XLA Ops:
  3.5 12.0 %collective-permute-start.2 = (bf16[1,48,1152]{2,1,0:T(8,128)(2,1)}, bf16[1,48,1152]{2,1,0:T(8,128)(2,1)S(1)}, u32[]{:S(2)}, u32[]{:S(2)}) collective-permute-start(bf16[1,48,1152]{2,1,0:T(8,128)(2,1)} %bitcast.63), channel_id=1, source_target_pairs={{0,12},{1,13},{2,14},{3,15},{4,8},{5,9},{6,10},{7,11},{8,4},{9,5},... | collective-permute-start | bytes 331784 | tf_op jit(solution)/shard_map/ppermute | solution.py:814
  24.7 13.9 %collective-permute-start.9 = (bf16[4,48,1152]{2,1,0:T(8,128)(2,1)S(1)}, bf16[4,48,1152]{2,1,0:T(8,128)(2,1)S(1)}, u32[]{:S(2)}, u32[]{:S(2)}) collective-permute-start(bf16[4,48,1152]{2,1,0:T(8,128)(2,1)S(1)} %constant_dynamic-update-slice_fusion.refs_2_), channel_id=1, source_target_pairs={{0,2},{1,3},{2,0},{3,1},{4,6},{5,7},{6,4},{7,5},{8,10},{9,11},{10,... | collective-permute-start | bytes 1327112 | tf_op jit(solution)/shard_map/ppermute | solution.py:814
  26.4 12.6 %collective-permute-start.7 = (bf16[4,48,1152]{2,1,0:T(8,128)(2,1)S(1)}, bf16[4,48,1152]{2,1,0:T(8,128)(2,1)S(1)}, u32[]{:S(2)}, u32[]{:S(2)}) collective-permute-start(bf16[4,48,1152]{2,1,0:T(8,128)(2,1)S(1)} %pad_maximum_fusion.2.refs_0_), channel_id=1, source_target_pairs={{0,16},{16,0},{1,17},{17,1},{2,18},{18,2},{3,19},{19,3},{4,20},{20... | collective-permute-start | bytes 1327112 | tf_op jit(solution)/shard_map/ppermute | solution.py:814
  31.3 17.4 %collective-permute-start.4 = (bf16[1,48,2432]{2,1,0:T(8,128)(2,1)S(1)}, bf16[1,48,2432]{2,1,0:T(8,128)(2,1)S(1)}, u32[]{:S(2)}, u32[]{:S(2)}) collective-permute-start(bf16[1,48,2432]{2,1,0:T(8,128)(2,1)S(1)} %bitcast.70), channel_id=1, source_target_pairs={{0,8},{1,9},{2,10},{3,11},{4,12},{5,13},{6,14},{7,15},{8,0},{9,1},... | collective-permute-start | bytes 700424 | tf_op jit(solution)/shard_map/ppermute | solution.py:814
  31.3 18.1 %collective-permute-start.12 = (bf16[4,48,1152]{2,1,0:T(8,128)(2,1)S(1)}, bf16[4,48,1152]{2,1,0:T(8,128)(2,1)}, u32[]{:S(2)}, u32[]{:S(2)}) collective-permute-start(bf16[4,48,1152]{2,1,0:T(8,128)(2,1)S(1)} %constant_dynamic-update-slice_fusion.refs_2_), channel_id=1, source_target_pairs={{0,1},{1,0},{2,3},{3,2},{4,5},{5,4},{6,7},{7,6},{8,9},{9,8},{10,11... | collective-permute-start | bytes 1327112 | tf_op jit(solution)/shard_map/ppermute | solution.py:814
  38.5 14.8 %collective-permute-start.10 = (bf16[4,48,1152]{2,1,0:T(8,128)(2,1)S(1)}, bf16[4,48,1152]{2,1,0:T(8,128)(2,1)}, u32[]{:S(2)}, u32[]{:S(2)}) collective-permute-start(bf16[4,48,1152]{2,1,0:T(8,128)(2,1)S(1)} %pad_maximum_fusion.2.refs_0_), channel_id=1, source_target_pairs={{0,1},{1,0},{2,3},{3,2},{4,5},{5,4},{6,7},{7,6},{8,9},{9,8},{10,11... | collective-permute-start | bytes 1327112 | tf_op jit(solution)/shard_map/ppermute | solution.py:814
  38.5 14.8 %collective-permute-start.13 = (bf16[4,48,1152]{2,1,0:T(8,128)(2,1)S(1)}, bf16[4,48,1152]{2,1,0:T(8,128)(2,1)}, u32[]{:S(2)}, u32[]{:S(2)}) collective-permute-start(bf16[4,48,1152]{2,1,0:T(8,128)(2,1)S(1)} %collective-permute-done.9.refs_3_), channel_id=1, source_target_pairs={{0,1},{1,0},{2,3},{3,2},{4,5},{5,4},{6,7},{7,6},{8,9},{9,8},{10,11... | collective-permute-start | bytes 1327112 | tf_op jit(solution)/shard_map/ppermute | solution.py:814
  39.1 14.3 %collective-permute-start.11 = (bf16[4,48,1152]{2,1,0:T(8,128)(2,1)S(1)}, bf16[4,48,1152]{2,1,0:T(8,128)(2,1)}, u32[]{:S(2)}, u32[]{:S(2)}) collective-permute-start(bf16[4,48,1152]{2,1,0:T(8,128)(2,1)S(1)} %collective-permute-done.7.refs_1_), channel_id=1, source_target_pairs={{0,1},{1,0},{2,3},{3,2},{4,5},{5,4},{6,7},{7,6},{8,9},{9,8},{10,11... | collective-permute-start | bytes 1327112 | tf_op jit(solution)/shard_map/ppermute | solution.py:814
  48.8 15.5 %collective-permute-start.16 = (bf16[2,48,2432]{2,1,0:T(8,128)(2,1)S(1)}, bf16[2,48,2432]{2,1,0:T(8,128)(2,1)S(1)}, u32[]{:S(2)}, u32[]{:S(2)}) collective-permute-start(bf16[2,48,2432]{2,1,0:T(8,128)(2,1)S(1)} %pad_maximum_fusion.1), channel_id=1, source_target_pairs={{0,16},{16,0},{1,17},{17,1},{2,18},{18,2},{3,19},{19,3},{4,20},{20... | collective-permute-start | bytes 1400840 | tf_op jit(solution)/shard_map/ppermute | solution.py:814
  49.4 14.8 %collective-permute-start.15 = (bf16[2,48,2432]{2,1,0:T(8,128)(2,1)S(1)}, bf16[2,48,2432]{2,1,0:T(8,128)(2,1)S(1)}, u32[]{:S(2)}, u32[]{:S(2)}) collective-permute-start(bf16[2,48,2432]{2,1,0:T(8,128)(2,1)S(1)} %pad_maximum_fusion), channel_id=1, source_target_pairs={{0,2},{1,3},{2,0},{3,1},{4,6},{5,7},{6,4},{7,5},{8,10},{9,11},{10,... | collective-permute-start | bytes 1400840 | tf_op jit(solution)/shard_map/ppermute | solution.py:814
  64.3 23.1 %collective-permute-start.21 = (bf16[4,48,2432]{2,1,0:T(8,128)(2,1)S(1)}, bf16[4,48,2432]{2,1,0:T(8,128)(2,1)}, u32[]{:S(2)}, u32[]{:S(2)}) collective-permute-start(bf16[4,48,2432]{2,1,0:T(8,128)(2,1)S(1)} %constant_dynamic-update-slice_fusion.7.refs_2_), channel_id=1, source_target_pairs={{0,1},{1,0},{2,3},{3,2},{4,5},{5,4},{6,7},{7,6},{8,9},{9,8},{10,11... | collective-permute-start | bytes 2801672 | tf_op jit(solution)/shard_map/ppermute | solution.py:814
  64.4 23.2 %collective-permute-start.18 = (bf16[4,48,2432]{2,1,0:T(8,128)(2,1)S(1)}, bf16[4,48,2432]{2,1,0:T(8,128)(2,1)}, u32[]{:S(2)}, u32[]{:S(2)}) collective-permute-start(bf16[4,48,2432]{2,1,0:T(8,128)(2,1)S(1)} %constant_dynamic-update-slice_fusion.7.refs_2_), channel_id=1, source_target_pairs={{0,2},{1,3},{2,0},{3,1},{4,6},{5,7},{6,4},{7,5},{8,10},{9,11},{10,... | collective-permute-start | bytes 2801672 | tf_op jit(solution)/shard_map/ppermute | solution.py:814
  65.5 22.2 %collective-permute-start.20 = (bf16[4,48,2432]{2,1,0:T(8,128)(2,1)S(1)}, bf16[4,48,2432]{2,1,0:T(8,128)(2,1)S(1)}, u32[]{:S(2)}, u32[]{:S(2)}) collective-permute-start(bf16[4,48,2432]{2,1,0:T(8,128)(2,1)S(1)} %constant_dynamic-update-slice_fusion.5.refs_0_), channel_id=1, source_target_pairs={{0,1},{1,0},{2,3},{3,2},{4,5},{5,4},{6,7},{7,6},{8,9},{9,8},{10,11... | collective-permute-start | bytes 2801672 | tf_op jit(solution)/shard_map/ppermute | solution.py:814
  65.7 23.1 %collective-permute-start.17 = (bf16[4,48,2432]{2,1,0:T(8,128)(2,1)S(1)}, bf16[4,48,2432]{2,1,0:T(8,128)(2,1)}, u32[]{:S(2)}, u32[]{:S(2)}) collective-permute-start(bf16[4,48,2432]{2,1,0:T(8,128)(2,1)S(1)} %constant_dynamic-update-slice_fusion.5.refs_0_), channel_id=1, source_target_pairs={{0,16},{16,0},{1,17},{17,1},{2,18},{18,2},{3,19},{19,3},{4,20},{20... | collective-permute-start | bytes 2801672 | tf_op jit(solution)/shard_map/ppermute | solution.py:814
  67.2 20.2 %collective-permute-start.19 = (bf16[2,128,384]{2,1,0:T(8,128)(2,1)S(1)}, bf16[2,128,384]{2,1,0:T(8,128)(2,1)S(1)}, u32[]{:S(2)}, u32[]{:S(2)}) collective-permute-start(bf16[2,128,384]{2,1,0:T(8,128)(2,1)S(1)} %constant_dynamic-update-slice_fusion.3), channel_id=1, source_target_pairs={{0,8},{1,9},{2,10},{3,11},{4,12},{5,13},{6,14},{7,15},{8,0},{9,1},... | collective-permute-start | bytes 589832 | tf_op jit(solution)/shard_map/ppermute | solution.py:814
  89.4 23.0 %collective-permute-start.26 = (bf16[4,128,384]{2,1,0:T(8,128)(2,1)S(1)}, bf16[4,128,384]{2,1,0:T(8,128)(2,1)S(1)}, u32[]{:S(2)}, u32[]{:S(2)}) collective-permute-start(bf16[4,128,384]{2,1,0:T(8,128)(2,1)S(1)} %constant_dynamic-update-slice_fusion.9.refs_0_), channel_id=1, source_target_pairs={{0,18},{1,19},{2,16},{3,17},{4,22},{5,23},{6,20},{7,21},{8,26},{9,... | collective-permute-start | bytes 1179656 | tf_op jit(solution)/shard_map/ppermute | solution.py:851
  90.8 21.6 %collective-permute-start.25 = (bf16[4,128,384]{2,1,0:T(8,128)(2,1)S(1)}, bf16[4,128,384]{2,1,0:T(8,128)(2,1)}, u32[]{:S(2)}, u32[]{:S(2)}) collective-permute-start(bf16[4,128,384]{2,1,0:T(8,128)(2,1)S(1)} %constant_dynamic-update-slice_fusion.9.refs_0_), channel_id=1, source_target_pairs={{0,16},{16,0},{1,17},{17,1},{2,18},{18,2},{3,19},{19,3},{4,20},{20... | collective-permute-start | bytes 1179656 | tf_op jit(solution)/shard_map/ppermute | solution.py:814
  92.0 20.4 %collective-permute-start.24 = (bf16[4,128,384]{2,1,0:T(8,128)(2,1)S(1)}, bf16[4,128,384]{2,1,0:T(8,128)(2,1)}, u32[]{:S(2)}, u32[]{:S(2)}) collective-permute-start(bf16[4,128,384]{2,1,0:T(8,128)(2,1)S(1)} %constant_dynamic-update-slice_fusion.9.refs_0_), channel_id=1, source_target_pairs={{0,2},{1,3},{2,0},{3,1},{4,6},{5,7},{6,4},{7,5},{8,10},{9,11},{10,... | collective-permute-start | bytes 1179656 | tf_op jit(solution)/shard_map/ppermute | solution.py:814
  123.2 16.7 %collective-permute-start.31 = (bf16[8,128,768]{2,1,0:T(8,128)(2,1)}, bf16[8,128,768]{2,1,0:T(8,128)(2,1)S(1)}, u32[]{:S(2)}, u32[]{:S(2)}) collective-permute-start(bf16[8,128,768]{2,1,0:T(8,128)(2,1)} %get-tuple-element.128), channel_id=1, source_target_pairs={{0,1},{1,0},{2,3},{3,2},{4,5},{5,4},{6,7},{7,6},{8,9},{9,8},{10,11... | collective-permute-start | bytes 4718600 | tf_op jit(solution)/shard_map/ppermute | solution.py:814
  153.8 20.9 %collective-permute-start.33 = (bf16[16,48,2048]{2,1,0:T(8,128)(2,1)}, bf16[16,48,2048]{2,1,0:T(8,128)(2,1)S(1)}, u32[]{:S(2)}, u32[]{:S(2)}) collective-permute-start(bf16[16,48,2048]{2,1,0:T(8,128)(2,1)} %get-tuple-element.137), channel_id=1, source_target_pairs={{0,1},{1,0},{2,3},{3,2},{4,5},{5,4},{6,7},{7,6},{8,9},{9,8},{10,11... | collective-permute-start | bytes 9437192 | tf_op jit(solution)/shard_map/ppermute | solution.py:814
  154.3 20.3 %collective-permute-start.32 = (bf16[4,128,768]{2,1,0:T(8,128)(2,1)}, bf16[4,128,768]{2,1,0:T(8,128)(2,1)}, u32[]{:S(2)}, u32[]{:S(2)}) collective-permute-start(bf16[4,128,768]{2,1,0:T(8,128)(2,1)} %add_convert_fusion.2), channel_id=1, source_target_pairs={{0,2},{1,3},{2,0},{3,1},{4,6},{5,7},{6,4},{7,5},{8,10},{9,11},{10,... | collective-permute-start | bytes 2359304 | tf_op jit(solution)/shard_map/ppermute | solution.py:814
  176.1 23.4 %collective-permute-start.36 = (bf16[2,128,768]{2,1,0:T(8,128)(2,1)S(1)}, bf16[2,128,768]{2,1,0:T(8,128)(2,1)S(1)}, u32[]{:S(2)}, u32[]{:S(2)}) collective-permute-start(bf16[2,128,768]{2,1,0:T(8,128)(2,1)S(1)} %add_convert_fusion.8), channel_id=1, source_target_pairs={{0,8},{1,9},{2,10},{3,11},{4,12},{5,13},{6,14},{7,15},{8,0},{9,1},... | collective-permute-start | bytes 1179656 | tf_op jit(solution)/shard_map/ppermute | solution.py:814
  180.6 19.0 %collective-permute-start.35 = (bf16[4,48,2048]{2,1,0:T(8,128)(2,1)S(1)}, bf16[4,48,2048]{2,1,0:T(8,128)(2,1)S(1)}, u32[]{:S(2)}, u32[]{:S(2)}) collective-permute-start(bf16[4,48,2048]{2,1,0:T(8,128)(2,1)S(1)} %get-tuple-element.177), channel_id=1, source_target_pairs={{0,2},{1,3},{2,0},{3,1},{4,6},{5,7},{6,4},{7,5},{8,10},{9,11},{10,... | collective-permute-start | bytes 2359304 | tf_op jit(solution)/shard_map/ppermute | solution.py:814
  181.6 18.7 %collective-permute-start.34 = (bf16[4,48,2048]{2,1,0:T(8,128)(2,1)S(1)}, bf16[4,48,2048]{2,1,0:T(8,128)(2,1)S(1)}, u32[]{:S(2)}, u32[]{:S(2)}) collective-permute-start(bf16[4,48,2048]{2,1,0:T(8,128)(2,1)S(1)} %get-tuple-element.178), channel_id=1, source_target_pairs={{0,16},{16,0},{1,17},{17,1},{2,18},{18,2},{3,19},{19,3},{4,20},{20... | collective-permute-start | bytes 2359304 | tf_op jit(solution)/shard_map/ppermute | solution.py:814
  202.1 12.8 %collective-permute-start.38 = (bf16[2,48,2048]{2,1,0:T(8,128)(2,1)S(1)}, bf16[2,48,2048]{2,1,0:T(8,128)(2,1)S(1)}, u32[]{:S(2)}, u32[]{:S(2)}) collective-permute-start(bf16[2,48,2048]{2,1,0:T(8,128)(2,1)S(1)} %get-tuple-element.175), channel_id=1, source_target_pairs={{0,16},{16,0},{1,17},{17,1},{2,18},{18,2},{3,19},{19,3},{4,20},{20... | collective-permute-start | bytes 1179656 | tf_op jit(solution)/shard_map/ppermute | solution.py:814
  203.5 11.3 %collective-permute-start.37 = (bf16[2,48,2048]{2,1,0:T(8,128)(2,1)S(1)}, bf16[2,48,2048]{2,1,0:T(8,128)(2,1)S(1)}, u32[]{:S(2)}, u32[]{:S(2)}) collective-permute-start(bf16[2,48,2048]{2,1,0:T(8,128)(2,1)S(1)} %get-tuple-element.176), channel_id=1, source_target_pairs={{0,2},{1,3},{2,0},{3,1},{4,6},{5,7},{6,4},{7,5},{8,10},{9,11},{10,... | collective-permute-start | bytes 1179656 | tf_op jit(solution)/shard_map/ppermute | solution.py:814
  217.2 28.3 %collective-permute-start.57 = (bf16[128,768]{1,0:T(8,128)(2,1)S(1)}, bf16[128,768]{1,0:T(8,128)(2,1)S(1)}, u32[]{:S(2)}, u32[]{:S(2)}) collective-permute-start(bf16[128,768]{1,0:T(8,128)(2,1)S(1)} %fusion.6), channel_id=1, source_target_pairs={{0,16},{16,0},{1,17},{17,1},{2,18},{18,2},{3,19},{19,3},{4,20},{20... | collective-permute-start | bytes 589832 | tf_op jit(solution)/shard_map/ppermute | solution.py:814
  219.9 20.6 %collective-permute-start.43 = (bf16[2,48,2048]{2,1,0:T(8,128)(2,1)S(1)}, bf16[2,48,2048]{2,1,0:T(8,128)(2,1)S(1)}, u32[]{:S(2)}, u32[]{:S(2)}) collective-permute-start(bf16[2,48,2048]{2,1,0:T(8,128)(2,1)S(1)} %add_convert_fusion.5), channel_id=1, source_target_pairs={{0,8},{1,9},{2,10},{3,11},{4,12},{5,13},{6,14},{7,15},{8,0},{9,1},... | collective-permute-start | bytes 1179656 | tf_op jit(solution)/shard_map/ppermute | solution.py:814
  223.7 16.9 %collective-permute-start.42 = (bf16[4,48,1152]{2,1,0:T(8,128)(2,1)S(1)}, bf16[4,48,1152]{2,1,0:T(8,128)(2,1)S(1)}, u32[]{:S(2)}, u32[]{:S(2)}) collective-permute-start(bf16[4,48,1152]{2,1,0:T(8,128)(2,1)S(1)} %get-tuple-element.181), channel_id=1, source_target_pairs={{0,2},{1,3},{2,0},{3,1},{4,6},{5,7},{6,4},{7,5},{8,10},{9,11},{10,... | collective-permute-start | bytes 1327112 | tf_op jit(solution)/shard_map/ppermute | solution.py:814
  224.6 15.9 %collective-permute-start.41 = (bf16[4,48,1152]{2,1,0:T(8,128)(2,1)S(1)}, bf16[4,48,1152]{2,1,0:T(8,128)(2,1)S(1)}, u32[]{:S(2)}, u32[]{:S(2)}) collective-permute-start(bf16[4,48,1152]{2,1,0:T(8,128)(2,1)S(1)} %get-tuple-element.182), channel_id=1, source_target_pairs={{0,16},{16,0},{1,17},{17,1},{2,18},{18,2},{3,19},{19,3},{4,20},{20... | collective-permute-start | bytes 1327112 | tf_op jit(solution)/shard_map/ppermute | solution.py:814
  254.2 18.1 %collective-permute-start.49 = (bf16[2,48,1152]{2,1,0:T(8,128)(2,1)S(1)}, bf16[2,48,1152]{2,1,0:T(8,128)(2,1)S(1)}, u32[]{:S(2)}, u32[]{:S(2)}) collective-permute-start(bf16[2,48,1152]{2,1,0:T(8,128)(2,1)S(1)} %add_convert_fusion.10), channel_id=1, source_target_pairs={{0,8},{1,9},{2,10},{3,11},{4,12},{5,13},{6,14},{7,15},{8,0},{9,1},... | collective-permute-start | bytes 663560 | tf_op jit(solution)/shard_map/ppermute | solution.py:814
  260.1 12.3 %collective-permute-start.50 = (bf16[4,48,768]{2,1,0:T(8,128)(2,1)S(1)}, bf16[4,48,768]{2,1,0:T(8,128)(2,1)S(1)}, u32[]{:S(2)}, u32[]{:S(2)}) collective-permute-start(bf16[4,48,768]{2,1,0:T(8,128)(2,1)S(1)} %add_convert_fusion.9), channel_id=1, source_target_pairs={{0,2},{1,3},{2,0},{3,1},{4,6},{5,7},{6,4},{7,5},{8,10},{9,11},{10,... | collective-permute-start | bytes 884744 | tf_op jit(solution)/shard_map/ppermute | solution.py:814
  (69 other events, 660.8 us)

commit v6 on v5

--- a/solution.py
+++ b/solution.py
@@ -613,7 +613,7 @@
             ],
         ),
         out_shape=[jax.ShapeDtypeStruct((length, width), f32), low, low],
-        compiler_params=params(),
+        compiler_params=params(54),
         cost_estimate=cost(
             2 * length * width * (width + 2 * inner), 4 * width * inner + 4 * length * inner
         ),

time: 294 us -> 292 us (level)
  transfers between devices with their start and end apart: 58 -> 58, of which waited for: 15 -> 15; matrix products, arithmetic and copies ran while one was open for 8% -> 8% of each run, Pallas kernels for 49% -> 50%
where the time goes in v6:
time: 292 us; the launch traced here: 291 us
  Pallas kernels  159 us (54%)
  starting transfers between devices  56.8 us (19%)
  waiting for transfers between devices  36.7 us (13%)
  other arithmetic  29.6 us (10%)
  local copies, waits for them, and re-layouts  6.72 us (2%)
    ppermute x57, starting transfers between devices, swapped(): return lambda array: lax.ppermute(array, axis, pairs)  55.5 us
    ppermute x57, waiting for transfers between devices, swapped(): return lambda array: lax.ppermute(array, axis, pairs)  36.7 us
    pallas_call x4, Pallas kernels, weight_grad(): pl.pallas_call(functools.partial(weight_kernel, counts=counts, block_rows...  35.2 us
    pallas_call x2, Pallas kernels, attend_back(): pl.pallas_call(attend_back_kernel, grid=(pairs,), in_specs=[column] * 5 +...  27 us
    pallas_call x1, Pallas kernels, middle_back(): pl.pallas_call(functools.partial(middle_back_kernel, n_pieces=n, halves=h...  19.4 us
    pallas_call x1, Pallas kernels, attend(): pl.pallas_call(attend_kernel, grid=(pairs,), in_specs=[column, column, co...  17.6 us
    pallas_call x1, Pallas kernels, ffn(): pl.pallas_call(functools.partial(ffn_kernel, n_pieces=n, halves=halves),...  17.5 us
    convert_element_type x16, other arithmetic, add(): return total.astype(bf16)  15.3 us
  transfers between devices with their start and end apart: 58, of which 15 were waited for; matrix products, arithmetic and copies ran while one was open for 8% of the time, Pallas kernels for 50%

profile of v6, /device:TPU:0, one launch (start us, length us, event | category | flops | bytes accessed | tf_op | source)
XLA Modules:
  0.0 290.8 jit_solution(2324495548913243226)
XLA Ops:
  3.5 5.0 %collective-permute-start.2 = (bf16[1,48,1152]{2,1,0:T(8,128)(2,1)}, bf16[1,48,1152]{2,1,0:T(8,128)(2,1)S(1)}, u32[]{:S(2)}, u32[]{:S(2)}) collective-permute-start(bf16[1,48,1152]{2,1,0:T(8,128)(2,1)} %bitcast.63), channel_id=1, source_target_pairs={{0,12},{1,13},{2,14},{3,15},{4,8},{5,9},{6,10},{7,11},{8,4},{9,5},... | collective-permute-start | bytes 331784 | tf_op jit(solution)/shard_map/ppermute | solution.py:814
  10.5 1.7 multiply_add_fusion
  13.7 1.8 pack.4
  15.5 2.6 collective-permute-done.1
  19.7 1.6 collective-permute-start.6
  21.7 3.0 %collective-permute-done.8 = bf16[2,48,1152]{2,1,0:T(8,128)(2,1)S(1)} collective-permute-done((bf16[2,48,1152]{2,1,0:T(8,128)(2,1)S(1)}, bf16[2,48,1152]{2,1,0:T(8,128)(2,1)S(1)}, u32[]{:S(2)}, u32[]{:S(2)}) %collective-permute-start.8) | collective-permute-done | bytes 221216 | tf_op jit(solution)/shard_map/ppermute | solution.py:814
  24.7 1.6 collective-permute-start.9
  28.9 2.4 collective-permute-start.5
  31.4 7.2 %collective-permute-done.5 = bf16[1,48,2432]{2,1,0:T(8,128)(2,1)S(1)} collective-permute-done((bf16[1,48,2432]{2,1,0:T(8,128)(2,1)S(1)}, bf16[1,48,2432]{2,1,0:T(8,128)(2,1)S(1)}, u32[]{:S(2)}, u32[]{:S(2)}) %collective-permute-start.5) | collective-permute-done | bytes 233504 | tf_op jit(solution)/shard_map/ppermute | solution.py:814
  39.1 9.6 %collective-permute-done.4 = bf16[1,48,2432]{2,1,0:T(8,128)(2,1)S(1)} collective-permute-done((bf16[1,48,2432]{2,1,0:T(8,128)(2,1)S(1)}, bf16[1,48,2432]{2,1,0:T(8,128)(2,1)S(1)}, u32[]{:S(2)}, u32[]{:S(2)}) %collective-permute-start.4) | collective-permute-done | bytes 233504 | tf_op jit(solution)/shard_map/ppermute | solution.py:814
  53.4 10.8 %project.1 = (bf16[1024,768]{1,0:T(8,128)(2,1)}, bf16[1024,768]{1,0:T(8,128)(2,1)}, bf16[1024,768]{1,0:T(8,128)(2,1)}, bf16[1024,768]{1,0:T(8,128)(2,1)}) custom-call(s32[2,32]{1,0:T(2,128)} %pad_add_fusion.1.tab_ref, bf16[4,48,1152]{2,1,0:T(8,128)(2,1)} %copy-done.2, bf16[4,48,1152]{2,1,0:T(8,128)(2,1)} %copy-done.17, bf16[4,48,1152]{2,1,0:T(8,128)(2,1)} %copy-done.12, ...), custom_call_target="tpu_custom_call" | custom-call | flops 3623878656 | bytes 12582912 | tf_op jit(solution)/shard_map/project/pallas_call | solution.py:194
  67.2 2.6 collective-permute-start.19
  69.8 17.6 %attend.1 = (bf16[1024,768]{1,0:T(8,128)(2,1)}, f32[1024,768]{1,0:T(8,128)}, bf16[12,4,256,768]{3,2,1,0:T(8,128)(2,1)}) custom-call(bf16[1024,768]{1,0:T(8,128)(2,1)} %get-tuple-element.100.q_ref, bf16[1024,768]{1,0:T(8,128)(2,1)} %get-tuple-element.101.k_ref, bf16[1024,768]{1,0:T(8,128)(2,1)} %get-tuple-element.102.v_ref, ...), custom_call_target="tpu_custom_call" | custom-call | flops 8053063680 | bytes 23592960 | tf_op jit(solution)/shard_map/attend/pallas_call | solution.py:298
  94.8 17.5 %ffn.1 = (f32[1024,768]{1,0:T(8,128)}, bf16[1024,768]{1,0:T(8,128)(2,1)}, bf16[1024,2048]{1,0:T(8,128)(2,1)}, bf16[1024,2048]{1,0:T(8,128)(2,1)}, bf16[1024,2048]{1,0:T(8,128)(2,1)}) custom-call(s32[2,32]{1,0:T(2,128)} %pad_add_fusion.1.tab_ref, bf16[4,48,2432]{2,1,0:T(8,128)(2,1)} %copy-done.26, bf16[4,48,2432]{2,1,0:T(8,128)(2,1)} %collective-permute-done.17.refs_1_, ...), custom_call_target="tpu_custom_call" | custom-call | flops 7650410496 | bytes 29360128 | tf_op jit(solution)/shard_map/ffn/pallas_call | solution.py:475
  114.1 8.3 %grad_down.1 = (bf16[8,128,768]{2,1,0:T(8,128)(2,1)}, bf16[8,128,768]{2,1,0:T(8,128)(2,1)}) custom-call(s32[16]{0:T(128)} %get-tuple-element.236.tab_ref, bf16[1024,2048]{1,0:T(8,128)(2,1)} %get-tuple-element.121.refs_0_.refs_9_, bf16[1024,768]{1,0:T(8,128)(2,1)} %bitcast.75), custom_call_target="tpu_custom_call" | custom-call | flops 3221225472 | bytes 8912896 | tf_op jit(solution)/shard_map/grad_down/pallas_call | solution.py:774
  124.6 15.3 %hidden_back.1 = (bf16[1024,768]{1,0:T(8,128)(2,1)}, bf16[1024,2048]{1,0:T(8,128)(2,1)}, bf16[1024,2048]{1,0:T(8,128)(2,1)}) custom-call(s32[2,32]{1,0:T(2,128)} %pad_add_fusion.tab_ref, bf16[4,128,384]{2,1,0:T(8,128)(2,1)} %copy-done.30, bf16[4,128,384]{2,1,0:T(8,128)(2,1)} %collective-permute-done.24.refs_1_, ...), custom_call_target="tpu_custom_call" | custom-call | flops 6442450944 | bytes 28311552 | tf_op jit(solution)/shard_map/hidden_back/pallas_call | solution.py:529
  140.1 12.6 %grad_gate_up.1 = (bf16[16,48,2048]{2,1,0:T(8,128)(2,1)}, bf16[16,48,2048]{2,1,0:T(8,128)(2,1)}) custom-call(s32[32]{0:T(128)} %add.354.tab_ref, bf16[1024,768]{1,0:T(8,128)(2,1)} %get-tuple-element.130.refs_0_, bf16[1024,2048]{1,0:T(8,128)(2,1)} %get-tuple-element.127.refs_1_.refs_9_, bf16[1024,2048]{1,0:T(8,128)(2,1)} %get-tuple-element.131.refs_2_.refs_10_), custom_call_target="tpu_custom_call" | custom-call | flops 6442450944 | bytes 16252928 | tf_op jit(solution)/shard_map/grad_gate_up/pallas_call | solution.py:774
  154.5 19.4 %middle_back.1 = (f32[1024,768]{1,0:T(8,128)}, bf16[1024,768]{1,0:T(8,128)(2,1)}, bf16[1024,768]{1,0:T(8,128)(2,1)}) custom-call(s32[2,32]{1,0:T(2,128)} %pad_add_fusion.1.tab_ref, bf16[4,48,2432]{2,1,0:T(8,128)(2,1)} %copy-done.26, bf16[4,48,2432]{2,1,0:T(8,128)(2,1)} %collective-permute-done.17.refs_1_, bf16[4,48,2432]{2,1,0:T(8,128)(2,1)} %copy-done.25, ...), custom_call_target="tpu_custom_call" | custom-call | flops 7650410496 | bytes 14680064 | tf_op jit(solution)/shard_map/middle_back/pallas_call | solution.py:602
  175.5 2.6 collective-permute-start.36
  181.0 16.5 %attend_back.2 = (bf16[1024,512]{1,0:T(8,128)(2,1)}, bf16[1024,512]{1,0:T(8,128)(2,1)}, bf16[1024,512]{1,0:T(8,128)(2,1)}) custom-call(bf16[1024,768]{1,0:T(8,128)(2,1)} %get-tuple-element.100.q_ref, bf16[1024,768]{1,0:T(8,128)(2,1)} %get-tuple-element.101.k_ref, bf16[1024,768]{1,0:T(8,128)(2,1)} %get-tuple-element.102.v_ref, ...), custom_call_target="tpu_custom_call" | custom-call | flops 10737418240 | bytes 18874368 | tf_op jit(solution)/shard_map/attend_back/pallas_call | solution.py:403
  198.3 1.7 add_convert_fusion.6
  203.2 9.3 %grad_qk_out.1 = (bf16[16,48,1152]{2,1,0:T(8,128)(2,1)}, bf16[16,48,1152]{2,1,0:T(8,128)(2,1)}) custom-call(s32[32]{0:T(128)} %add.354.tab_ref, bf16[1024,768]{1,0:T(8,128)(2,1)} %get-tuple-element.161.refs_0_, bf16[1024,768]{1,0:T(8,128)(2,1)} %get-tuple-element.106.refs_9_.mixed_ref.refs_1_, bf16[1024,512]{1,0:T(8,128)(2,1)} %get-tuple-element.144.refs_2_.refs_10_, ...), custom_call_target="tpu_custom_call" | custom-call | flops 3623878656 | bytes 9830400 | tf_op jit(solution)/shard_map/grad_qk_out/pallas_call | solution.py:774
  217.8 2.4 collective-permute-start.43
  223.8 10.5 %attend_back.3 = (bf16[1024,256]{1,0:T(8,128)(2,1)}, bf16[1024,256]{1,0:T(8,128)(2,1)}, bf16[1024,256]{1,0:T(8,128)(2,1)}) custom-call(bf16[1024,768]{1,0:T(8,128)(2,1)} %get-tuple-element.100.q_ref, bf16[1024,768]{1,0:T(8,128)(2,1)} %get-tuple-element.101.k_ref, bf16[1024,768]{1,0:T(8,128)(2,1)} %get-tuple-element.102.v_ref, ...), custom_call_target="tpu_custom_call" | custom-call | flops 5368709120 | bytes 9437184 | tf_op jit(solution)/shard_map/attend_back/pallas_call | solution.py:403
  234.4 4.0 %collective-permute-done.43 = bf16[2,48,2048]{2,1,0:T(8,128)(2,1)S(1)} collective-permute-done((bf16[2,48,2048]{2,1,0:T(8,128)(2,1)S(1)}, bf16[2,48,2048]{2,1,0:T(8,128)(2,1)S(1)}, u32[]{:S(2)}, u32[]{:S(2)}) %collective-permute-start.43) | collective-permute-done | bytes 393248 | tf_op jit(solution)/shard_map/ppermute | solution.py:814
  244.0 4.9 %grad_qkv_rest.1 = (bf16[8,48,768]{2,1,0:T(8,128)(2,1)}, bf16[8,48,768]{2,1,0:T(8,128)(2,1)}) custom-call(s32[16]{0:T(128)} %get-tuple-element.236.tab_ref, bf16[1024,768]{1,0:T(8,128)(2,1)} %get-tuple-element.161.refs_0_, bf16[1024,256]{1,0:T(8,128)(2,1)} %get-tuple-element.158.refs_1_.refs_11_, bf16[1024,256]{1,0:T(8,128)(2,1)} %get-tuple-element.162.refs_2_.refs_13_, ...), custom_call_target="tpu_custom_call" | custom-call | flops 1207959552 | bytes 4325376 | tf_op jit(solution)/shard_map/grad_qkv_rest/pallas_call | solution.py:774
  252.0 2.5 collective-permute-start.49
  258.6 11.5 %input_grad.1 = f32[1024,768]{1,0:T(8,128)} custom-call(s32[2,32]{1,0:T(2,128)} %pad_add_fusion.1.tab_ref, bf16[4,48,1152]{2,1,0:T(8,128)(2,1)} %copy-done.2, bf16[4,48,1152]{2,1,0:T(8,128)(2,1)} %copy-done.17, bf16[4,48,1152]{2,1,0:T(8,128)(2,1)} %copy-done.12, bf16[4,48,1152]{2,1,0:T(8,128)(2,1)} %copy-done.16, ...), custom_call_target="tpu_custom_call" | custom-call | flops 3623878656 | bytes 15728640 | tf_op jit(solution)/shard_map/input_grad/pallas_call | solution.py:656
  270.3 2.0 collective-permute-start.53
  272.2 1.8 collective-permute-start.55
  275.1 2.6 collective-permute-start.51
  285.0 2.5 collective-permute-done.52
  (266 shorter events, 73.6 us)
Async XLA Ops:
  3.5 12.0 %collective-permute-start.2 = (bf16[1,48,1152]{2,1,0:T(8,128)(2,1)}, bf16[1,48,1152]{2,1,0:T(8,128)(2,1)S(1)}, u32[]{:S(2)}, u32[]{:S(2)}) collective-permute-start(bf16[1,48,1152]{2,1,0:T(8,128)(2,1)} %bitcast.63), channel_id=1, source_target_pairs={{0,12},{1,13},{2,14},{3,15},{4,8},{5,9},{6,10},{7,11},{8,4},{9,5},... | collective-permute-start | bytes 331784 | tf_op jit(solution)/shard_map/ppermute | solution.py:814
  24.7 13.9 %collective-permute-start.9 = (bf16[4,48,1152]{2,1,0:T(8,128)(2,1)S(1)}, bf16[4,48,1152]{2,1,0:T(8,128)(2,1)S(1)}, u32[]{:S(2)}, u32[]{:S(2)}) collective-permute-start(bf16[4,48,1152]{2,1,0:T(8,128)(2,1)S(1)} %constant_dynamic-update-slice_fusion.refs_2_), channel_id=1, source_target_pairs={{0,2},{1,3},{2,0},{3,1},{4,6},{5,7},{6,4},{7,5},{8,10},{9,11},{10,... | collective-permute-start | bytes 1327112 | tf_op jit(solution)/shard_map/ppermute | solution.py:814
  26.4 12.6 %collective-permute-start.7 = (bf16[4,48,1152]{2,1,0:T(8,128)(2,1)S(1)}, bf16[4,48,1152]{2,1,0:T(8,128)(2,1)S(1)}, u32[]{:S(2)}, u32[]{:S(2)}) collective-permute-start(bf16[4,48,1152]{2,1,0:T(8,128)(2,1)S(1)} %pad_maximum_fusion.2.refs_0_), channel_id=1, source_target_pairs={{0,16},{16,0},{1,17},{17,1},{2,18},{18,2},{3,19},{19,3},{4,20},{20... | collective-permute-start | bytes 1327112 | tf_op jit(solution)/shard_map/ppermute | solution.py:814
  31.3 17.4 %collective-permute-start.4 = (bf16[1,48,2432]{2,1,0:T(8,128)(2,1)S(1)}, bf16[1,48,2432]{2,1,0:T(8,128)(2,1)S(1)}, u32[]{:S(2)}, u32[]{:S(2)}) collective-permute-start(bf16[1,48,2432]{2,1,0:T(8,128)(2,1)S(1)} %bitcast.70), channel_id=1, source_target_pairs={{0,8},{1,9},{2,10},{3,11},{4,12},{5,13},{6,14},{7,15},{8,0},{9,1},... | collective-permute-start | bytes 700424 | tf_op jit(solution)/shard_map/ppermute | solution.py:814
  31.3 18.1 %collective-permute-start.12 = (bf16[4,48,1152]{2,1,0:T(8,128)(2,1)S(1)}, bf16[4,48,1152]{2,1,0:T(8,128)(2,1)}, u32[]{:S(2)}, u32[]{:S(2)}) collective-permute-start(bf16[4,48,1152]{2,1,0:T(8,128)(2,1)S(1)} %constant_dynamic-update-slice_fusion.refs_2_), channel_id=1, source_target_pairs={{0,1},{1,0},{2,3},{3,2},{4,5},{5,4},{6,7},{7,6},{8,9},{9,8},{10,11... | collective-permute-start | bytes 1327112 | tf_op jit(solution)/shard_map/ppermute | solution.py:814
  38.5 14.8 %collective-permute-start.10 = (bf16[4,48,1152]{2,1,0:T(8,128)(2,1)S(1)}, bf16[4,48,1152]{2,1,0:T(8,128)(2,1)}, u32[]{:S(2)}, u32[]{:S(2)}) collective-permute-start(bf16[4,48,1152]{2,1,0:T(8,128)(2,1)S(1)} %pad_maximum_fusion.2.refs_0_), channel_id=1, source_target_pairs={{0,1},{1,0},{2,3},{3,2},{4,5},{5,4},{6,7},{7,6},{8,9},{9,8},{10,11... | collective-permute-start | bytes 1327112 | tf_op jit(solution)/shard_map/ppermute | solution.py:814
  38.5 14.8 %collective-permute-start.13 = (bf16[4,48,1152]{2,1,0:T(8,128)(2,1)S(1)}, bf16[4,48,1152]{2,1,0:T(8,128)(2,1)}, u32[]{:S(2)}, u32[]{:S(2)}) collective-permute-start(bf16[4,48,1152]{2,1,0:T(8,128)(2,1)S(1)} %collective-permute-done.9.refs_3_), channel_id=1, source_target_pairs={{0,1},{1,0},{2,3},{3,2},{4,5},{5,4},{6,7},{7,6},{8,9},{9,8},{10,11... | collective-permute-start | bytes 1327112 | tf_op jit(solution)/shard_map/ppermute | solution.py:814
  39.1 14.3 %collective-permute-start.11 = (bf16[4,48,1152]{2,1,0:T(8,128)(2,1)S(1)}, bf16[4,48,1152]{2,1,0:T(8,128)(2,1)}, u32[]{:S(2)}, u32[]{:S(2)}) collective-permute-start(bf16[4,48,1152]{2,1,0:T(8,128)(2,1)S(1)} %collective-permute-done.7.refs_1_), channel_id=1, source_target_pairs={{0,1},{1,0},{2,3},{3,2},{4,5},{5,4},{6,7},{7,6},{8,9},{9,8},{10,11... | collective-permute-start | bytes 1327112 | tf_op jit(solution)/shard_map/ppermute | solution.py:814
  48.8 15.5 %collective-permute-start.16 = (bf16[2,48,2432]{2,1,0:T(8,128)(2,1)S(1)}, bf16[2,48,2432]{2,1,0:T(8,128)(2,1)S(1)}, u32[]{:S(2)}, u32[]{:S(2)}) collective-permute-start(bf16[2,48,2432]{2,1,0:T(8,128)(2,1)S(1)} %pad_maximum_fusion.1), channel_id=1, source_target_pairs={{0,16},{16,0},{1,17},{17,1},{2,18},{18,2},{3,19},{19,3},{4,20},{20... | collective-permute-start | bytes 1400840 | tf_op jit(solution)/shard_map/ppermute | solution.py:814
  49.4 14.8 %collective-permute-start.15 = (bf16[2,48,2432]{2,1,0:T(8,128)(2,1)S(1)}, bf16[2,48,2432]{2,1,0:T(8,128)(2,1)S(1)}, u32[]{:S(2)}, u32[]{:S(2)}) collective-permute-start(bf16[2,48,2432]{2,1,0:T(8,128)(2,1)S(1)} %pad_maximum_fusion), channel_id=1, source_target_pairs={{0,2},{1,3},{2,0},{3,1},{4,6},{5,7},{6,4},{7,5},{8,10},{9,11},{10,... | collective-permute-start | bytes 1400840 | tf_op jit(solution)/shard_map/ppermute | solution.py:814
  64.3 23.1 %collective-permute-start.21 = (bf16[4,48,2432]{2,1,0:T(8,128)(2,1)S(1)}, bf16[4,48,2432]{2,1,0:T(8,128)(2,1)}, u32[]{:S(2)}, u32[]{:S(2)}) collective-permute-start(bf16[4,48,2432]{2,1,0:T(8,128)(2,1)S(1)} %constant_dynamic-update-slice_fusion.7.refs_2_), channel_id=1, source_target_pairs={{0,1},{1,0},{2,3},{3,2},{4,5},{5,4},{6,7},{7,6},{8,9},{9,8},{10,11... | collective-permute-start | bytes 2801672 | tf_op jit(solution)/shard_map/ppermute | solution.py:814
  64.4 23.2 %collective-permute-start.18 = (bf16[4,48,2432]{2,1,0:T(8,128)(2,1)S(1)}, bf16[4,48,2432]{2,1,0:T(8,128)(2,1)}, u32[]{:S(2)}, u32[]{:S(2)}) collective-permute-start(bf16[4,48,2432]{2,1,0:T(8,128)(2,1)S(1)} %constant_dynamic-update-slice_fusion.7.refs_2_), channel_id=1, source_target_pairs={{0,2},{1,3},{2,0},{3,1},{4,6},{5,7},{6,4},{7,5},{8,10},{9,11},{10,... | collective-permute-start | bytes 2801672 | tf_op jit(solution)/shard_map/ppermute | solution.py:814
  65.5 22.2 %collective-permute-start.20 = (bf16[4,48,2432]{2,1,0:T(8,128)(2,1)S(1)}, bf16[4,48,2432]{2,1,0:T(8,128)(2,1)S(1)}, u32[]{:S(2)}, u32[]{:S(2)}) collective-permute-start(bf16[4,48,2432]{2,1,0:T(8,128)(2,1)S(1)} %constant_dynamic-update-slice_fusion.5.refs_0_), channel_id=1, source_target_pairs={{0,1},{1,0},{2,3},{3,2},{4,5},{5,4},{6,7},{7,6},{8,9},{9,8},{10,11... | collective-permute-start | bytes 2801672 | tf_op jit(solution)/shard_map/ppermute | solution.py:814
  65.7 23.1 %collective-permute-start.17 = (bf16[4,48,2432]{2,1,0:T(8,128)(2,1)S(1)}, bf16[4,48,2432]{2,1,0:T(8,128)(2,1)}, u32[]{:S(2)}, u32[]{:S(2)}) collective-permute-start(bf16[4,48,2432]{2,1,0:T(8,128)(2,1)S(1)} %constant_dynamic-update-slice_fusion.5.refs_0_), channel_id=1, source_target_pairs={{0,16},{16,0},{1,17},{17,1},{2,18},{18,2},{3,19},{19,3},{4,20},{20... | collective-permute-start | bytes 2801672 | tf_op jit(solution)/shard_map/ppermute | solution.py:814
  67.2 20.2 %collective-permute-start.19 = (bf16[2,128,384]{2,1,0:T(8,128)(2,1)S(1)}, bf16[2,128,384]{2,1,0:T(8,128)(2,1)S(1)}, u32[]{:S(2)}, u32[]{:S(2)}) collective-permute-start(bf16[2,128,384]{2,1,0:T(8,128)(2,1)S(1)} %constant_dynamic-update-slice_fusion.3), channel_id=1, source_target_pairs={{0,8},{1,9},{2,10},{3,11},{4,12},{5,13},{6,14},{7,15},{8,0},{9,1},... | collective-permute-start | bytes 589832 | tf_op jit(solution)/shard_map/ppermute | solution.py:814
  89.4 23.0 %collective-permute-start.26 = (bf16[4,128,384]{2,1,0:T(8,128)(2,1)S(1)}, bf16[4,128,384]{2,1,0:T(8,128)(2,1)S(1)}, u32[]{:S(2)}, u32[]{:S(2)}) collective-permute-start(bf16[4,128,384]{2,1,0:T(8,128)(2,1)S(1)} %constant_dynamic-update-slice_fusion.9.refs_0_), channel_id=1, source_target_pairs={{0,18},{1,19},{2,16},{3,17},{4,22},{5,23},{6,20},{7,21},{8,26},{9,... | collective-permute-start | bytes 1179656 | tf_op jit(solution)/shard_map/ppermute | solution.py:851
  90.8 21.6 %collective-permute-start.25 = (bf16[4,128,384]{2,1,0:T(8,128)(2,1)S(1)}, bf16[4,128,384]{2,1,0:T(8,128)(2,1)}, u32[]{:S(2)}, u32[]{:S(2)}) collective-permute-start(bf16[4,128,384]{2,1,0:T(8,128)(2,1)S(1)} %constant_dynamic-update-slice_fusion.9.refs_0_), channel_id=1, source_target_pairs={{0,16},{16,0},{1,17},{17,1},{2,18},{18,2},{3,19},{19,3},{4,20},{20... | collective-permute-start | bytes 1179656 | tf_op jit(solution)/shard_map/ppermute | solution.py:814
  92.0 20.4 %collective-permute-start.24 = (bf16[4,128,384]{2,1,0:T(8,128)(2,1)S(1)}, bf16[4,128,384]{2,1,0:T(8,128)(2,1)}, u32[]{:S(2)}, u32[]{:S(2)}) collective-permute-start(bf16[4,128,384]{2,1,0:T(8,128)(2,1)S(1)} %constant_dynamic-update-slice_fusion.9.refs_0_), channel_id=1, source_target_pairs={{0,2},{1,3},{2,0},{3,1},{4,6},{5,7},{6,4},{7,5},{8,10},{9,11},{10,... | collective-permute-start | bytes 1179656 | tf_op jit(solution)/shard_map/ppermute | solution.py:814
  123.2 16.7 %collective-permute-start.31 = (bf16[8,128,768]{2,1,0:T(8,128)(2,1)}, bf16[8,128,768]{2,1,0:T(8,128)(2,1)S(1)}, u32[]{:S(2)}, u32[]{:S(2)}) collective-permute-start(bf16[8,128,768]{2,1,0:T(8,128)(2,1)} %get-tuple-element.128), channel_id=1, source_target_pairs={{0,1},{1,0},{2,3},{3,2},{4,5},{5,4},{6,7},{7,6},{8,9},{9,8},{10,11... | collective-permute-start | bytes 4718600 | tf_op jit(solution)/shard_map/ppermute | solution.py:814
  152.8 21.1 %collective-permute-start.33 = (bf16[16,48,2048]{2,1,0:T(8,128)(2,1)}, bf16[16,48,2048]{2,1,0:T(8,128)(2,1)S(1)}, u32[]{:S(2)}, u32[]{:S(2)}) collective-permute-start(bf16[16,48,2048]{2,1,0:T(8,128)(2,1)} %get-tuple-element.137), channel_id=1, source_target_pairs={{0,1},{1,0},{2,3},{3,2},{4,5},{5,4},{6,7},{7,6},{8,9},{9,8},{10,11... | collective-permute-start | bytes 9437192 | tf_op jit(solution)/shard_map/ppermute | solution.py:814
  153.3 20.6 %collective-permute-start.32 = (bf16[4,128,768]{2,1,0:T(8,128)(2,1)S(1)}, bf16[4,128,768]{2,1,0:T(8,128)(2,1)S(1)}, u32[]{:S(2)}, u32[]{:S(2)}) collective-permute-start(bf16[4,128,768]{2,1,0:T(8,128)(2,1)S(1)} %add_convert_fusion.2), channel_id=1, source_target_pairs={{0,2},{1,3},{2,0},{3,1},{4,6},{5,7},{6,4},{7,5},{8,10},{9,11},{10,... | collective-permute-start | bytes 2359304 | tf_op jit(solution)/shard_map/ppermute | solution.py:814
  175.5 22.0 %collective-permute-start.36 = (bf16[2,128,768]{2,1,0:T(8,128)(2,1)S(1)}, bf16[2,128,768]{2,1,0:T(8,128)(2,1)S(1)}, u32[]{:S(2)}, u32[]{:S(2)}) collective-permute-start(bf16[2,128,768]{2,1,0:T(8,128)(2,1)S(1)} %add_convert_fusion.8), channel_id=1, source_target_pairs={{0,8},{1,9},{2,10},{3,11},{4,12},{5,13},{6,14},{7,15},{8,0},{9,1},... | collective-permute-start | bytes 1179656 | tf_op jit(solution)/shard_map/ppermute | solution.py:814
  178.7 19.1 %collective-permute-start.35 = (bf16[4,48,2048]{2,1,0:T(8,128)(2,1)S(1)}, bf16[4,48,2048]{2,1,0:T(8,128)(2,1)}, u32[]{:S(2)}, u32[]{:S(2)}) collective-permute-start(bf16[4,48,2048]{2,1,0:T(8,128)(2,1)S(1)} %get-tuple-element.177), channel_id=1, source_target_pairs={{0,2},{1,3},{2,0},{3,1},{4,6},{5,7},{6,4},{7,5},{8,10},{9,11},{10,... | collective-permute-start | bytes 2359304 | tf_op jit(solution)/shard_map/ppermute | solution.py:814
  179.6 18.7 %collective-permute-start.34 = (bf16[4,48,2048]{2,1,0:T(8,128)(2,1)S(1)}, bf16[4,48,2048]{2,1,0:T(8,128)(2,1)S(1)}, u32[]{:S(2)}, u32[]{:S(2)}) collective-permute-start(bf16[4,48,2048]{2,1,0:T(8,128)(2,1)S(1)} %get-tuple-element.178), channel_id=1, source_target_pairs={{0,16},{16,0},{1,17},{17,1},{2,18},{18,2},{3,19},{19,3},{4,20},{20... | collective-permute-start | bytes 2359304 | tf_op jit(solution)/shard_map/ppermute | solution.py:814
  200.0 12.6 %collective-permute-start.38 = (bf16[2,48,2048]{2,1,0:T(8,128)(2,1)S(1)}, bf16[2,48,2048]{2,1,0:T(8,128)(2,1)S(1)}, u32[]{:S(2)}, u32[]{:S(2)}) collective-permute-start(bf16[2,48,2048]{2,1,0:T(8,128)(2,1)S(1)} %get-tuple-element.175), channel_id=1, source_target_pairs={{0,16},{16,0},{1,17},{17,1},{2,18},{18,2},{3,19},{19,3},{4,20},{20... | collective-permute-start | bytes 1179656 | tf_op jit(solution)/shard_map/ppermute | solution.py:814
  201.4 11.2 %collective-permute-start.37 = (bf16[2,48,2048]{2,1,0:T(8,128)(2,1)S(1)}, bf16[2,48,2048]{2,1,0:T(8,128)(2,1)S(1)}, u32[]{:S(2)}, u32[]{:S(2)}) collective-permute-start(bf16[2,48,2048]{2,1,0:T(8,128)(2,1)S(1)} %get-tuple-element.176), channel_id=1, source_target_pairs={{0,2},{1,3},{2,0},{3,1},{4,6},{5,7},{6,4},{7,5},{8,10},{9,11},{10,... | collective-permute-start | bytes 1179656 | tf_op jit(solution)/shard_map/ppermute | solution.py:814
  214.9 28.3 %collective-permute-start.57 = (bf16[128,768]{1,0:T(8,128)(2,1)S(1)}, bf16[128,768]{1,0:T(8,128)(2,1)S(1)}, u32[]{:S(2)}, u32[]{:S(2)}) collective-permute-start(bf16[128,768]{1,0:T(8,128)(2,1)S(1)} %fusion.6), channel_id=1, source_target_pairs={{0,16},{16,0},{1,17},{17,1},{2,18},{18,2},{3,19},{19,3},{4,20},{20... | collective-permute-start | bytes 589832 | tf_op jit(solution)/shard_map/ppermute | solution.py:814
  217.8 20.6 %collective-permute-start.43 = (bf16[2,48,2048]{2,1,0:T(8,128)(2,1)S(1)}, bf16[2,48,2048]{2,1,0:T(8,128)(2,1)S(1)}, u32[]{:S(2)}, u32[]{:S(2)}) collective-permute-start(bf16[2,48,2048]{2,1,0:T(8,128)(2,1)S(1)} %add_convert_fusion.5), channel_id=1, source_target_pairs={{0,8},{1,9},{2,10},{3,11},{4,12},{5,13},{6,14},{7,15},{8,0},{9,1},... | collective-permute-start | bytes 1179656 | tf_op jit(solution)/shard_map/ppermute | solution.py:814
  221.5 16.9 %collective-permute-start.42 = (bf16[4,48,1152]{2,1,0:T(8,128)(2,1)S(1)}, bf16[4,48,1152]{2,1,0:T(8,128)(2,1)S(1)}, u32[]{:S(2)}, u32[]{:S(2)}) collective-permute-start(bf16[4,48,1152]{2,1,0:T(8,128)(2,1)S(1)} %get-tuple-element.181), channel_id=1, source_target_pairs={{0,2},{1,3},{2,0},{3,1},{4,6},{5,7},{6,4},{7,5},{8,10},{9,11},{10,... | collective-permute-start | bytes 1327112 | tf_op jit(solution)/shard_map/ppermute | solution.py:814
  222.5 15.9 %collective-permute-start.41 = (bf16[4,48,1152]{2,1,0:T(8,128)(2,1)S(1)}, bf16[4,48,1152]{2,1,0:T(8,128)(2,1)S(1)}, u32[]{:S(2)}, u32[]{:S(2)}) collective-permute-start(bf16[4,48,1152]{2,1,0:T(8,128)(2,1)S(1)} %get-tuple-element.182), channel_id=1, source_target_pairs={{0,16},{16,0},{1,17},{17,1},{2,18},{18,2},{3,19},{19,3},{4,20},{20... | collective-permute-start | bytes 1327112 | tf_op jit(solution)/shard_map/ppermute | solution.py:814
  252.0 18.1 %collective-permute-start.49 = (bf16[2,48,1152]{2,1,0:T(8,128)(2,1)S(1)}, bf16[2,48,1152]{2,1,0:T(8,128)(2,1)S(1)}, u32[]{:S(2)}, u32[]{:S(2)}) collective-permute-start(bf16[2,48,1152]{2,1,0:T(8,128)(2,1)S(1)} %add_convert_fusion.10), channel_id=1, source_target_pairs={{0,8},{1,9},{2,10},{3,11},{4,12},{5,13},{6,14},{7,15},{8,0},{9,1},... | collective-permute-start | bytes 663560 | tf_op jit(solution)/shard_map/ppermute | solution.py:814
  257.9 12.3 %collective-permute-start.50 = (bf16[4,48,768]{2,1,0:T(8,128)(2,1)S(1)}, bf16[4,48,768]{2,1,0:T(8,128)(2,1)S(1)}, u32[]{:S(2)}, u32[]{:S(2)}) collective-permute-start(bf16[4,48,768]{2,1,0:T(8,128)(2,1)S(1)} %add_convert_fusion.9), channel_id=1, source_target_pairs={{0,2},{1,3},{2,0},{3,1},{4,6},{5,7},{6,4},{7,5},{8,10},{9,11},{10,... | collective-permute-start | bytes 884744 | tf_op jit(solution)/shard_map/ppermute | solution.py:814
  (71 other events, 704.0 us)
